TPU v7x, 256 devices: a whole 4x4x8 slice. The times are simulated.
256 devices in a mesh: dp: 4 (over x), blk: 16 (over z_lo, y, core), mp: 4 (over z_hi).
Axes of the slice: x: 4, y: 4, z: 8 (z_hi: 4, z_lo: 2; z = z_hi * 2 + z_lo), core: 2. Of those that a mesh axis runs over, the one named last changes fastest.
Arguments:
- tokens: bfloat16 [16384, 7168], P('dp', ('blk', 'mp')), may hold values from -6 to 6
- trainer_q: float32 [3584, 7168], P(('mp', 'blk'), 'dp'), may hold values from -0.0625 to 0.0625
- kv_pool: bfloat16 [2, 8192, 3584], P(None, ('dp', 'blk'), 'mp')
- prompt_kv: bfloat16 [2, 16384, 3584], P(None, ('dp', 'blk'), 'mp'), may hold values from -15 to 15
- page_table: int32 [64, 64], P(('dp', 'blk')), may hold values from 0 to 127, as said below
- page_count: int32 [64], P(('dp', 'blk')), may hold values from 1 to 64
- prompt_len: int32 [64], P(('dp', 'blk')), may hold values from 64 to 256
Outputs:
- server_q: bfloat16 [3584, 7168], P('mp', 'blk')
- attn_out: bfloat16 [16384, 3584], P(('dp', 'blk'), 'mp')
Inputs may be any that keep to these rules, and one draw needn't show every extreme that they name: `page_table`: the entries of a row are distinct page numbers of the request's group.
All inputs are finite; a program needn't handle non-finite values.
Results may differ from a plain program's by a relative error of at most 0.012.
The roundings to bfloat16 on the way count: a program that leaves them out, or rounds other values in their place, can miss the bound.
Values may be sent and summed in bfloat16 or wider, within the bound.
A program may use at most 128 MiB of HBM per device.

v0:
```python
import jax
import jax.numpy as jnp
from jax import lax
from jax.sharding import PartitionSpec as P

HD = 224
PAGE = 16


def attend_block(softmax_state, query_heads, key_heads, value_heads, key_mask):
    running_max, row_total, weighted = softmax_state
    scores = jnp.einsum(
        "thd,khd->htk", query_heads, key_heads, preferred_element_type=jnp.float32
    ) * HD ** (-0.5)
    scores = jnp.where(key_mask[None], scores, -1e30)
    new_max = jnp.maximum(running_max, jnp.max(scores, axis=2))
    weights = jnp.where(key_mask[None], jnp.exp(scores - new_max[:, :, None]), 0.0)
    factor = jnp.exp(running_max - new_max)
    row_total = row_total * factor + jnp.sum(weights, axis=2)
    weighted = weighted * factor[:, :, None] + jnp.einsum(
        "htk,khd->htd",
        weights.astype(jnp.bfloat16),
        value_heads,
        preferred_element_type=jnp.float32,
    )
    return (new_max, row_total, weighted)


def body(tokens, trainer_q, kv_pool, prompt_kv, page_table, page_count, prompt_len):
    trainer_rows = lax.all_gather(trainer_q.astype(jnp.bfloat16), "dp", axis=1, tiled=True)
    server_q = lax.all_to_all(trainer_rows, "blk", split_axis=1, concat_axis=0, tiled=True)
    features = lax.all_gather(tokens, "mp", axis=1, tiled=True)
    own_rows = features.shape[0] // lax.axis_size("blk")
    head_width = server_q.shape[0]
    token_local = lax.all_to_all(features, "blk", split_axis=0, concat_axis=1, tiled=True)
    queries = jnp.einsum(
        "td,hd->th",
        token_local,
        lax.all_gather(server_q, "blk", axis=1, tiled=True),
        preferred_element_type=jnp.float32,
    )
    queries = queries.astype(jnp.bfloat16)
    head_count = head_width // HD
    query_heads = queries.reshape(own_rows, head_count, HD)
    length = prompt_len[0]
    row_pages = page_table[0]
    live_slots = jnp.arange(row_pages.shape[0], dtype=jnp.int32) < page_count[0]
    row_index = jnp.arange(own_rows, dtype=jnp.int32)
    own_mask = (row_index[None, :] <= row_index[:, None]) & (row_index[None, :] < length)
    softmax_state = (
        jnp.full((head_count, own_rows), -1e30, jnp.float32),
        jnp.zeros((head_count, own_rows), jnp.float32),
        jnp.zeros((head_count, own_rows, HD), jnp.float32),
    )
    softmax_state = attend_block(
        softmax_state,
        query_heads,
        prompt_kv[0].reshape(own_rows, head_count, HD),
        prompt_kv[1].reshape(own_rows, head_count, HD),
        own_mask,
    )
    shard_piece = lax.all_gather(kv_pool, "blk", axis=1, tiled=True)
    key_count = shard_piece.shape[1]
    page_ids = jnp.arange(key_count, dtype=jnp.int32) // PAGE
    page_used = jnp.any((row_pages[None, :] == page_ids[:, None]) & live_slots[None, :], axis=1)
    key_mask = jnp.broadcast_to(page_used[None, :], (own_rows, key_count))
    running_max, row_total, weighted = attend_block(
        softmax_state,
        query_heads,
        shard_piece[0].reshape(key_count, head_count, HD),
        shard_piece[1].reshape(key_count, head_count, HD),
        key_mask,
    )
    mixed = weighted / row_total[:, :, None]
    mixed = jnp.where((row_index < length)[None, :, None], mixed, 0.0)
    mixed = jnp.transpose(mixed, (1, 0, 2)).reshape(own_rows, head_width).astype(jnp.bfloat16)
    return (server_q, mixed)


def solution(mesh):
    in_specs = (
        P("dp", ("blk", "mp")),
        P(("mp", "blk"), "dp"),
        P(None, ("dp", "blk"), "mp"),
        P(None, ("dp", "blk"), "mp"),
        P(("dp", "blk"), None),
        P(("dp", "blk")),
        P(("dp", "blk")),
    )
    out_specs = (P("mp", "blk"), P(("dp", "blk"), "mp"))
    return jax.shard_map(body, mesh=mesh, in_specs=in_specs, out_specs=out_specs, check_vma=False)
```

profile of v0, /device:TPU:25, one launch (start us, length us, event | category | flops | bytes accessed | tf_op | source)
XLA Modules:
  0.0 292.4 jit_solution(181580022779690303)
XLA Ops:
  7.2 0.0 all-gather.4.cloned.1.call-start
  7.2 0.7 all-gather.4.cloned.1.call-update
  7.9 0.0 all-gather.8.cloned.1.call-start
  7.9 0.7 all-gather.8.cloned.1.call-update
  8.6 0.0 all-gather.6.cloned.1.call-start
  8.7 1.0 convert_element_type.18
  9.7 12.1 %all_gather.12 = bf16[56,7168]{1,0:T(8,128)(2,1)S(1)} all-gather(bf16[56,1792]{1,0:T(8,128)(2,1)S(1)} %convert_element_type.18), channel_id=1, replica_groups=mesh['dp'=4,'blk'=16,'mp'=4] {'dp'}, dimensions={1}, use_global_device_ids=true | all-gather | bytes 1003520 | tf_op jit(solution)/shard_map/all_gather | solution.py:30
  21.9 1.1 all_to_all.28
  23.0 0.5 copy.48
  23.5 49.5 %all_to_all.38 = bf16[56,16,448]{2,0,1:T(8,128)(2,1)S(1)} all-to-all(bf16[56,16,448]{2,0,1:T(8,128)(2,1)S(1)} %copy.48), channel_id=1, replica_groups=mesh['dp'=4,'blk'=16,'mp'=4] {'blk'}, dimensions={1} | all-to-all | bytes 1605632 | tf_op jit(solution)/shard_map/all_to_all | solution.py:31
  73.0 0.0 copy-start.1
  73.0 1.2 copy.57
  74.2 0.0 all-gather.6.cloned.1.call-update
  74.2 25.5 %all-gather.4.cloned.1.call-done = bf16[4096,448]{0,1:T(8,128)(2,1)} async-done(((bf16[4096,112]{0,1:T(8,128)(2,1)}), bf16[4096,448]{0,1:T(8,128)(2,1)}) %all-gather.4.cloned.1.call-update) | async-done | bytes 3670032 | tf_op jit(solution)/shard_map/all_gather | solution.py:32
  99.7 0.0 copy-start.2
  99.7 4.3 %copy.62 = bf16[56,16,8,256]{3,2,0,1:T(8,128)(2,1)} copy(bf16[56,16,8,256]{3,2,1,0:T(8,128)(2,1)} %bitcast.70) | data formatting | bytes 7340032 | tf_op jit(solution)/shard_map/all_to_all | solution.py:35
  104.1 5.1 %all-to-all-start.1 = ((bf16[16,256,448]{1,2,0:T(8,128)(2,1)}), bf16[16,256,448]{1,2,0:T(8,128)(2,1)}, u32[]{:S(2)}, u32[]{:S(2)}) async-start(bf16[16,256,448]{1,2,0:T(8,128)(2,1)} %bitcast.66), calls=%async_computation.1 | async-start | bytes 7340032 | tf_op jit(solution)/shard_map/all_to_all | solution.py:35
  109.8 0.0 copy-done.1
  109.8 0.1 fusion.37
  109.9 0.2 copy.52
  110.8 0.2 copy.53
  111.0 0.0 copy-done.2
  111.0 0.2 and_reduce_fusion
  111.2 0.1 fusion.22
  111.3 77.9 %all-gather.8.cloned.1.call-done = bf16[2,2048,896]{2,1,0:T(8,128)(2,1)} async-done(((bf16[2,128,896]{2,1,0:T(8,128)(2,1)}), bf16[2,2048,896]{2,1,0:T(8,128)(2,1)}) %all-gather.8.cloned.1.call-update) | async-done | bytes 7340048 | tf_op jit(solution)/shard_map/all_gather | solution.py:62
  189.2 6.8 %fusion.36 = (bf16[1,2048,896]{2,1,0:T(8,128)(2,1)}, bf16[1,2048,896]{2,1,0:T(8,128)(2,1)}) fusion(bf16[2,2048,896]{2,1,0:T(8,128)(2,1)} %all-gather.8.cloned.1.call-done), kind=kLoop, calls=%fused_computation.51 | loop fusion | bytes 14680064 | tf_op jit(solution)/shard_map/slice | solution.py:70
  196.0 6.2 %copy.55 = bf16[1,2048,896]{1,2,0:T(8,128)(2,1)} copy(bf16[1,2048,896]{2,1,0:T(8,128)(2,1)} %get-tuple-element.14) | data formatting | bytes 7340032 | tf_op jit(solution)/shard_map/slice | solution.py:70
  202.1 6.2 %copy.56 = bf16[1,2048,896]{1,2,0:T(8,128)(2,1)} copy(bf16[1,2048,896]{2,1,0:T(8,128)(2,1)} %get-tuple-element.15) | data formatting | bytes 7340032 | tf_op jit(solution)/shard_map/slice | solution.py:71
  208.4 0.0 all-to-all-done.1
  208.4 57.2 %all-gather.6.cloned.1.call-done = bf16[896,7168]{0,1:T(8,128)(2,1)} async-done(((bf16[896,448]{0,1:T(8,128)(2,1)}), bf16[896,7168]{0,1:T(8,128)(2,1)}) %all-gather.6.cloned.1.call-update) | async-done | bytes 12845072 | tf_op jit(solution)/shard_map/all_gather | solution.py:39
  265.6 9.8 %convolution_convert_fusion = bf16[256,896]{1,0:T(8,128)(2,1)S(1)} fusion(bf16[256,7168]{0,1:T(8,128)(2,1)} %bitcast.4, bf16[896,7168]{0,1:T(8,128)(2,1)} %all-gather.6.cloned.1.call-done), kind=kOutput, calls=%fused_computation.17 | convolution fusion | flops 3288563712 | bytes 16973824 | tf_op jit(solution)/shard_map/td,hd->th/dot_general | solution.py:36
  275.4 0.2 copy.51
  275.6 0.4 fusion.38
  276.0 0.0 copy-start
  276.0 4.0 %fusion = (f32[4,256]{1,0:T(4,128)S(1)}, f32[4,256,2048]{2,1,0:T(8,128)S(1)}) fusion(pred[2048]{0:T(1024)(128)(4,1)S(1)} %and_reduce_fusion, bf16[256,4,224]{0,2,1:T(8,128)(2,1)S(1)} %bitcast.69, bf16[2048,4,224]{0,2,1:T(8,128)(2,1)} %bitcast.67), kind=kOutput, calls=%fused_computation.2 | convolution fusion | flops 945814528 | bytes 12523520 | tf_op jit(solution)/shard_map/thd,khd->htk/dot_general | solution.py:12
  279.9 2.2 fusion.1
  282.1 0.0 copy-done
  282.2 2.1 fusion.7
  284.3 0.2 fusion.16
  284.5 0.4 fusion.15
  284.9 1.0 copy.58
  (5 shorter events, 0.0 us)
Async XLA Ops:
  7.2 92.6 %all-gather.4.cloned.1.call-start = ((), (), s32[]{:S(2)}) async-start(), calls=%async_computation.2 | async-start | bytes 4587520 | tf_op jit(solution)/shard_map/all_gather | solution.py:32
  7.9 181.3 %all-gather.8.cloned.1.call-start = ((), (), s32[]{:S(2)}) async-start(), calls=%async_computation.4 | async-start | bytes 7798784 | tf_op jit(solution)/shard_map/all_gather | solution.py:62
  8.6 256.9 %all-gather.6.cloned.1.call-start = ((), (), s32[]{:S(2)}) async-start(), calls=%async_computation.3 | async-start | bytes 13647872 | tf_op jit(solution)/shard_map/all_gather | solution.py:39
  73.0 36.9 %copy-start.1 = (bf16[2,256,896]{2,1,0:T(8,128)(2,1)S(1)}, bf16[2,256,896]{2,1,0:T(8,128)(2,1)}, u32[]{:S(2)}) copy-start(bf16[2,256,896]{2,1,0:T(8,128)(2,1)} %param.10) | copy-start | bytes 2752516
  99.7 11.3 %copy-start.2 = (s32[1,64]{1,0:T(1,128)S(1)}, s32[1,64]{1,0:T(1,128)}, u32[]{:S(2)}) copy-start(s32[1,64]{1,0:T(1,128)} %param.11) | copy-start | bytes 772
  104.1 104.3 %all-to-all-start.1 = ((bf16[16,256,448]{1,2,0:T(8,128)(2,1)}), bf16[16,256,448]{1,2,0:T(8,128)(2,1)}, u32[]{:S(2)}, u32[]{:S(2)}) async-start(bf16[16,256,448]{1,2,0:T(8,128)(2,1)} %bitcast.66), calls=%async_computation.1 | async-start | bytes 7340032 | tf_op jit(solution)/shard_map/all_to_all | solution.py:35
  276.0 6.2 %copy-start = (bf16[1,2048,896]{1,2,0:T(8,128)(2,1)S(1)}, bf16[1,2048,896]{1,2,0:T(8,128)(2,1)}, u32[]{:S(2)}) copy-start(bf16[1,2048,896]{1,2,0:T(8,128)(2,1)} %copy.56) | copy-start | bytes 11010052
Sparse Core Ops, SparseCore 0:
  9.8 89.8 all-gather.3
  101.5 87.6 all-gather.7
  191.6 73.9 all-gather.5
where the time goes:
time: 294 us; the launch traced here: 292 us
  waiting for transfers between devices  162 us (55%)
  blocking collectives  61.6 us (21%)
  local copies, waits for them, and re-layouts  28 us (10%)
  matrix products  16.6 us (6%)
  between operations  15.2 us (5%)
  starting transfers between devices  5.23 us (2%)
  other arithmetic  3.74 us (1%)
    all_gather x1, waiting for transfers between devices, body(): shard_piece = lax.all_gather(kv_pool, 'blk', axis=1, tiled=True)  77.9 us
    all_gather x1, waiting for transfers between devices, body(): lax.all_gather(server_q, 'blk', axis=1, tiled=True)  57.2 us
    all_to_all x1, blocking collectives, body(): lax.all_to_all(trainer_rows, 'blk', split_axis=1, concat_axis=0, tiled=True)  49.5 us
    all_gather x1, waiting for transfers between devices, body(): features = lax.all_gather(tokens, 'mp', axis=1, tiled=True)  25.5 us
    slice x2, local copies, waits for them, and re-layouts, body(): shard_piece[0].reshape(key_count, head_count, HD)  12.9 us
    all_gather x1, blocking collectives, body(): lax.all_gather(trainer_q.astype(jnp.bfloat16), 'dp', axis=1, tiled=True)  12.1 us
    dot_general x1, matrix products, body(): jnp.einsum('td,hd->th', token_local, lax.all_gather(server_q, 'blk', axis...  9.77 us
    slice x1, local copies, waits for them, and re-layouts, body(): shard_piece[1].reshape(key_count, head_count, HD)  6.2 us
  transfers between devices with their start and end apart: 4, of which 3 were waited for; matrix products, arithmetic and copies ran while one was open for 9% of the time, Pallas kernels for 0%

commit v1 on v0

--- a/solution.py
+++ b/solution.py
@@ -27,17 +27,24 @@
 
 
 def body(tokens, trainer_q, kv_pool, prompt_kv, page_table, page_count, prompt_len):
+    blk_size = lax.axis_size("blk")
+    mp_size = lax.axis_size("mp")
     trainer_rows = lax.all_gather(trainer_q.astype(jnp.bfloat16), "dp", axis=1, tiled=True)
-    server_q = lax.all_to_all(trainer_rows, "blk", split_axis=1, concat_axis=0, tiled=True)
-    features = lax.all_gather(tokens, "mp", axis=1, tiled=True)
-    own_rows = features.shape[0] // lax.axis_size("blk")
-    head_width = server_q.shape[0]
-    token_local = lax.all_to_all(features, "blk", split_axis=0, concat_axis=1, tiled=True)
+    head_weights = lax.all_gather(trainer_rows, "blk", axis=0, tiled=True)
+    head_width, model_width = head_weights.shape
+    block_cols = model_width // blk_size
+    server_q = lax.dynamic_slice_in_dim(
+        head_weights, lax.axis_index("blk") * block_cols, block_cols, axis=1
+    )
+    group_rows, piece_cols = tokens.shape
+    own_rows = group_rows // blk_size
+    pieces = tokens.reshape(blk_size, 1, own_rows, piece_cols)
+    pieces = jnp.broadcast_to(pieces, (blk_size, mp_size, own_rows, piece_cols))
+    pieces = pieces.reshape(blk_size * mp_size, own_rows, piece_cols)
+    pieces = lax.all_to_all(pieces, ("blk", "mp"), 0, 0, tiled=True)
+    token_local = jnp.transpose(pieces, (1, 0, 2)).reshape(own_rows, -1)
     queries = jnp.einsum(
-        "td,hd->th",
-        token_local,
-        lax.all_gather(server_q, "blk", axis=1, tiled=True),
-        preferred_element_type=jnp.float32,
+        "td,hd->th", token_local, head_weights, preferred_element_type=jnp.float32
     )
     queries = queries.astype(jnp.bfloat16)
     head_count = head_width // HD

time: 294 us -> 234 us (0.80)
  blocking collectives: 61.6 us -> 12.5 us
  waiting for transfers between devices: 162 us -> 142 us
  starting transfers between devices: 5.23 us -> 14.4 us
    all_to_all x1 -> x0, blocking collectives: 49.5 us -> none  [body(): lax.all_to_all(trainer_rows, 'blk', split_axis=1, concat_axis=0, tiled=True)]
    all_gather x2 -> x1, waiting for transfers between devices: 82.7 us -> 71.3 us  [body(): head_weights = lax.all_gather(trainer_rows, 'blk', axis=0, tiled=True)]
    all_to_all x1, starting transfers between devices: 5.11 us -> 14.3 us  [body(): pieces = lax.all_to_all(pieces, ('blk', 'mp'), 0, 0, tiled=True)]
    all_gather x1, waiting for transfers between devices: 77.9 us -> 69.7 us  [body(): shard_piece = lax.all_gather(kv_pool, 'blk', axis=1, tiled=True)]
    all_to_all x3 -> x0, local copies, waits for them, and re-layouts: 5.9 us -> none  [the longest x1 4.32 us: body(): lax.all_to_all(features, 'blk', split_axis=0, concat_axis=1, tiled=True)]
    broadcast_in_dim x0 -> x2, local copies, waits for them, and re-layouts: none -> 3.41 us  [body(): pieces = jnp.broadcast_to(pieces, (blk_size, mp_size, own_rows, piece_cols))]
  transfers between devices with their start and end apart: 4 -> 3, of which waited for: 3 -> 2; matrix products, arithmetic and copies ran while one was open for 9% -> 12% of each run, Pallas kernels for 0% -> 0%
where the time goes in v1:
time: 234 us; the launch traced here: 232 us
  waiting for transfers between devices  142 us (61%)
  local copies, waits for them, and re-layouts  27.1 us (12%)
  matrix products  16.7 us (7%)
  between operations  15.5 us (7%)
  starting transfers between devices  14.4 us (6%)
  blocking collectives  12.5 us (5%)
  other arithmetic  3.91 us (2%)
    all_gather x1, waiting for transfers between devices, body(): head_weights = lax.all_gather(trainer_rows, 'blk', axis=0, tiled=True)  71.3 us
    all_gather x1, waiting for transfers between devices, body(): shard_piece = lax.all_gather(kv_pool, 'blk', axis=1, tiled=True)  69.7 us
    all_to_all x1, starting transfers between devices, body(): pieces = lax.all_to_all(pieces, ('blk', 'mp'), 0, 0, tiled=True)  14.3 us
    slice x2, local copies, waits for them, and re-layouts, body(): shard_piece[0].reshape(key_count, head_count, HD)  12.9 us
    all_gather x1, blocking collectives, body(): lax.all_gather(trainer_q.astype(jnp.bfloat16), 'dp', axis=1, tiled=True)  12.5 us
    dot_general x1, matrix products, body(): jnp.einsum('td,hd->th', token_local, head_weights, preferred_element_type...  9.78 us
    slice x1, local copies, waits for them, and re-layouts, body(): shard_piece[1].reshape(key_count, head_count, HD)  6.21 us
  transfers between devices with their start and end apart: 3, of which 2 were waited for; matrix products, arithmetic and copies ran while one was open for 12% of the time, Pallas kernels for 0%

profile of v1, /device:TPU:25, one launch (start us, length us, event | category | flops | bytes accessed | tf_op | source)
XLA Modules:
  0.0 231.9 jit_solution(18041598933790976390)
XLA Ops:
  7.2 0.0 copy-start.1
  7.2 0.0 all-gather.5.cloned.1.call-start
  7.2 0.7 all-gather.5.cloned.1.call-update
  7.9 0.0 all-gather.3.cloned.1.call-start
  8.0 1.0 convert_element_type.18
  9.0 12.5 %all_gather.9 = bf16[56,7168]{1,0:T(8,128)(2,1)} all-gather(bf16[56,1792]{1,0:T(8,128)(2,1)S(1)} %convert_element_type.18), channel_id=1, replica_groups=mesh['dp'=4,'blk'=16,'mp'=4] {'dp'}, dimensions={1}, use_global_device_ids=true | all-gather | bytes 1003520 | tf_op jit(solution)/shard_map/all_gather | solution.py:32
  21.5 0.0 all-gather.3.cloned.1.call-update
  21.5 0.0 copy-start.2
  21.6 1.2 copy.49
  22.8 2.2 broadcast_in_dim.82
  25.0 14.3 %all-to-all-start = ((bf16[64,256,112]{1,2,0:T(8,128)(2,1)}), bf16[64,256,112]{1,2,0:T(8,128)(2,1)}, u32[]{:S(2)}, u32[]{:S(2)}) async-start(bf16[64,256,112]{1,2,0:T(8,128)(2,1)} %bitcast.64), calls=%async_computation | async-start | bytes 7340032 | tf_op jit(solution)/shard_map/all_to_all | solution.py:44
  39.9 0.0 copy-done.1
  39.9 0.1 fusion.37
  40.0 0.2 copy.39
  40.9 0.2 copy.40
  41.2 0.0 copy-done.2
  41.2 0.2 and_reduce_fusion
  41.3 0.1 fusion.22
  41.4 69.7 %all-gather.5.cloned.1.call-done = bf16[2,2048,896]{2,1,0:T(8,128)(2,1)} async-done(((bf16[2,128,896]{2,1,0:T(8,128)(2,1)}), bf16[2,2048,896]{2,1,0:T(8,128)(2,1)}) %all-gather.5.cloned.1.call-update) | async-done | bytes 7340048 | tf_op jit(solution)/shard_map/all_gather | solution.py:69
  111.2 6.7 %fusion.36 = (bf16[1,2048,896]{2,1,0:T(8,128)(2,1)}, bf16[1,2048,896]{2,1,0:T(8,128)(2,1)}) fusion(bf16[2,2048,896]{2,1,0:T(8,128)(2,1)} %all-gather.5.cloned.1.call-done), kind=kLoop, calls=%fused_computation.52 | loop fusion | bytes 14680064 | tf_op jit(solution)/shard_map/slice | solution.py:77
  117.9 6.2 %copy.43 = bf16[1,2048,896]{1,2,0:T(8,128)(2,1)} copy(bf16[1,2048,896]{2,1,0:T(8,128)(2,1)} %get-tuple-element.13) | data formatting | bytes 7340032 | tf_op jit(solution)/shard_map/slice | solution.py:78
  124.1 6.2 %copy.42 = bf16[1,2048,896]{1,2,0:T(8,128)(2,1)} copy(bf16[1,2048,896]{2,1,0:T(8,128)(2,1)} %get-tuple-element.12) | data formatting | bytes 7340032 | tf_op jit(solution)/shard_map/slice | solution.py:77
  130.3 71.3 %all-gather.3.cloned.1.call-done = bf16[896,7168]{1,0:T(8,128)(2,1)} async-done(((bf16[56,7168]{1,0:T(8,128)(2,1)}), bf16[896,7168]{1,0:T(8,128)(2,1)}) %all-gather.3.cloned.1.call-update) | async-done | bytes 12845072 | tf_op jit(solution)/shard_map/all_gather | solution.py:33
  201.6 1.6 constant_dynamic-slice_fusion
  203.2 1.2 copy.44
  204.5 0.0 all-to-all-done
  204.5 9.8 %convolution_convert_fusion = bf16[256,896]{1,0:T(8,128)(2,1)S(1)} fusion(bf16[256,7168]{0,1:T(8,128)(2,1)} %bitcast.3, bf16[896,7168]{1,0:T(8,128)(2,1)} %all-gather.3.cloned.1.call-done), kind=kOutput, calls=%fused_computation.16 | convolution fusion | flops 3288563712 | bytes 16973824 | tf_op jit(solution)/shard_map/td,hd->th/dot_general | solution.py:46
  214.3 0.2 copy.38
  214.5 0.0 copy-start
  214.5 4.0 %fusion = (f32[4,256]{1,0:T(4,128)S(1)}, f32[4,256,2048]{2,1,0:T(8,128)S(1)}) fusion(pred[2048]{0:T(1024)(128)(4,1)S(1)} %and_reduce_fusion, bf16[256,4,224]{0,2,1:T(8,128)(2,1)S(1)} %bitcast.66, bf16[2048,4,224]{0,2,1:T(8,128)(2,1)} %bitcast.65), kind=kOutput, calls=%fused_computation.2 | convolution fusion | flops 945814528 | bytes 12523520 | tf_op jit(solution)/shard_map/thd,khd->htk/dot_general | solution.py:12
  218.5 0.4 fusion.38
  218.9 2.4 %fusion.1 = f32[4,256]{1,0:T(4,128)S(1)} fusion(f32[4,256,2048]{2,1,0:T(8,128)S(1)} %get-tuple-element.22, f32[4,256]{1,0:T(4,128)S(1)} %get-tuple-element.18, pred[2048]{0:T(1024)(128)(4,1)S(1)} %and_reduce_fusion), kind=kLoop, calls=%fused_computation.3 | loop fusion | flops 10484736 | bytes 8398848 | tf_op jit(solution)/shard_map/reduce_sum | solution.py:19
  221.2 0.0 copy-done
  221.3 2.1 fusion.7
  223.4 0.2 fusion.16
  223.6 0.4 fusion.15
  224.0 1.0 copy.45
  (5 shorter events, 0.0 us)
Async XLA Ops:
  7.2 32.8 %copy-start.1 = (bf16[2,256,896]{2,1,0:T(8,128)(2,1)S(1)}, bf16[2,256,896]{2,1,0:T(8,128)(2,1)}, u32[]{:S(2)}) copy-start(bf16[2,256,896]{2,1,0:T(8,128)(2,1)} %param.10) | copy-start | bytes 2752516
  7.2 104.0 %all-gather.5.cloned.1.call-start = ((), (), s32[]{:S(2)}) async-start(), calls=%async_computation.2 | async-start | bytes 7798784 | tf_op jit(solution)/shard_map/all_gather | solution.py:69
  7.9 193.7 %all-gather.3.cloned.1.call-start = ((), (), s32[]{:S(2)}) async-start(), calls=%async_computation.1 | async-start | bytes 13647872 | tf_op jit(solution)/shard_map/all_gather | solution.py:33
  21.5 19.6 %copy-start.2 = (s32[1,64]{1,0:T(1,128)S(1)}, s32[1,64]{1,0:T(1,128)}, u32[]{:S(2)}) copy-start(s32[1,64]{1,0:T(1,128)} %param.11) | copy-start | bytes 772
  25.0 179.5 %all-to-all-start = ((bf16[64,256,112]{1,2,0:T(8,128)(2,1)}), bf16[64,256,112]{1,2,0:T(8,128)(2,1)}, u32[]{:S(2)}, u32[]{:S(2)}) async-start(bf16[64,256,112]{1,2,0:T(8,128)(2,1)} %bitcast.64), calls=%async_computation | async-start | bytes 7340032 | tf_op jit(solution)/shard_map/all_to_all | solution.py:44
  214.5 6.8 %copy-start = (bf16[1,2048,896]{1,2,0:T(8,128)(2,1)S(1)}, bf16[1,2048,896]{1,2,0:T(8,128)(2,1)}, u32[]{:S(2)}) copy-start(bf16[1,2048,896]{1,2,0:T(8,128)(2,1)} %copy.43) | copy-start | bytes 11010052
Sparse Core Ops, SparseCore 0:
  9.8 101.2 all-gather.4
  113.0 88.5 all-gather.2

commit v2 on v1

--- a/solution.py
+++ b/solution.py
@@ -26,22 +26,35 @@
     return (new_max, row_total, weighted)
 
 
+def blk_index():
+    return lax.axis_index("chips") * lax.axis_size("core") + lax.axis_index("core")
+
+
+def gather_blk(x, axis):
+    parts = lax.all_gather(x, "chips", axis=0)
+    parts = lax.all_gather(parts, "core", axis=1)
+    parts = jnp.moveaxis(parts.reshape((-1,) + x.shape), 0, axis)
+    shape = list(x.shape)
+    shape[axis] = -1
+    return parts.reshape(shape)
+
+
 def body(tokens, trainer_q, kv_pool, prompt_kv, page_table, page_count, prompt_len):
-    blk_size = lax.axis_size("blk")
+    blk_size = lax.axis_size("chips") * lax.axis_size("core")
     mp_size = lax.axis_size("mp")
     trainer_rows = lax.all_gather(trainer_q.astype(jnp.bfloat16), "dp", axis=1, tiled=True)
-    head_weights = lax.all_gather(trainer_rows, "blk", axis=0, tiled=True)
+    head_weights = gather_blk(trainer_rows, 0)
     head_width, model_width = head_weights.shape
     block_cols = model_width // blk_size
     server_q = lax.dynamic_slice_in_dim(
-        head_weights, lax.axis_index("blk") * block_cols, block_cols, axis=1
+        head_weights, blk_index() * block_cols, block_cols, axis=1
     )
     group_rows, piece_cols = tokens.shape
     own_rows = group_rows // blk_size
     pieces = tokens.reshape(blk_size, 1, own_rows, piece_cols)
     pieces = jnp.broadcast_to(pieces, (blk_size, mp_size, own_rows, piece_cols))
     pieces = pieces.reshape(blk_size * mp_size, own_rows, piece_cols)
-    pieces = lax.all_to_all(pieces, ("blk", "mp"), 0, 0, tiled=True)
+    pieces = lax.all_to_all(pieces, ("chips", "core", "mp"), 0, 0, tiled=True)
     token_local = jnp.transpose(pieces, (1, 0, 2)).reshape(own_rows, -1)
     queries = jnp.einsum(
         "td,hd->th", token_local, head_weights, preferred_element_type=jnp.float32
@@ -66,7 +79,7 @@
         prompt_kv[1].reshape(own_rows, head_count, HD),
         own_mask,
     )
-    shard_piece = lax.all_gather(kv_pool, "blk", axis=1, tiled=True)
+    shard_piece = gather_blk(kv_pool, 1)
     key_count = shard_piece.shape[1]
     page_ids = jnp.arange(key_count, dtype=jnp.int32) // PAGE
     page_used = jnp.any((row_pages[None, :] == page_ids[:, None]) & live_slots[None, :], axis=1)
@@ -85,14 +98,19 @@
 
 
 def solution(mesh):
+    dp_size, blk_size, mp_size = mesh.devices.shape
+    fine = jax.sharding.Mesh(
+        mesh.devices.reshape(dp_size, blk_size // 2, 2, mp_size), ("dp", "chips", "core", "mp")
+    )
+    blk = ("chips", "core")
     in_specs = (
-        P("dp", ("blk", "mp")),
-        P(("mp", "blk"), "dp"),
-        P(None, ("dp", "blk"), "mp"),
-        P(None, ("dp", "blk"), "mp"),
-        P(("dp", "blk"), None),
-        P(("dp", "blk")),
-        P(("dp", "blk")),
+        P("dp", blk + ("mp",)),
+        P(("mp",) + blk, "dp"),
+        P(None, ("dp",) + blk, "mp"),
+        P(None, ("dp",) + blk, "mp"),
+        P(("dp",) + blk, None),
+        P(("dp",) + blk),
+        P(("dp",) + blk),
     )
-    out_specs = (P("mp", "blk"), P(("dp", "blk"), "mp"))
-    return jax.shard_map(body, mesh=mesh, in_specs=in_specs, out_specs=out_specs, check_vma=False)
+    out_specs = (P("mp", blk), P(("dp",) + blk, "mp"))
+    return jax.shard_map(body, mesh=fine, in_specs=in_specs, out_specs=out_specs, check_vma=False)

time: 234 us -> 266 us (1.14)
  waiting for transfers between devices: 142 us -> 166 us
  local copies, waits for them, and re-layouts: 27.1 us -> 34.8 us
  starting transfers between devices: 14.4 us -> 10.9 us
    all_to_all x1, waiting for transfers between devices: 0.01 us -> 32.4 us  [body(): pieces = lax.all_to_all(pieces, ('chips', 'core', 'mp'), 0, 0, tiled=True)]
    another operation x0 -> x2, local copies, waits for them, and re-layouts: none -> 20.8 us  [the longest x1 10.6 us: body(): shard_piece[0].reshape(key_count, head_count, HD)]
    all_gather x2 -> x4, waiting for transfers between devices: 141 us -> 133 us  [the longest x2 116 us: gather_blk(): parts = lax.all_gather(x, 'chips', axis=0)]
    slice x1 -> x0, local copies, waits for them, and re-layouts: 6.21 us -> none  [body(): shard_piece[1].reshape(key_count, head_count, HD)]
    slice x2 -> x1, local copies, waits for them, and re-layouts: 12.9 us -> 7.23 us  [body(): shard_piece[0].reshape(key_count, head_count, HD)]
    all_to_all x1, starting transfers between devices: 14.3 us -> 10.7 us  [body(): pieces = lax.all_to_all(pieces, ('chips', 'core', 'mp'), 0, 0, tiled=True)]
  transfers between devices with their start and end apart: 3 -> 5, of which waited for: 2 -> 5; matrix products, arithmetic and copies ran while one was open for 12% -> 13% of each run, Pallas kernels for 0% -> 0%
where the time goes in v2:
time: 266 us; the launch traced here: 262 us
  waiting for transfers between devices  166 us (62%)
  local copies, waits for them, and re-layouts  34.8 us (13%)
  matrix products  18.1 us (7%)
  between operations  15.3 us (6%)
  blocking collectives  12.5 us (5%)
  starting transfers between devices  10.9 us (4%)
  other arithmetic  3.92 us (1%)
    all_gather x2, waiting for transfers between devices, gather_blk(): parts = lax.all_gather(x, 'chips', axis=0)  116 us
    all_to_all x1, waiting for transfers between devices, body(): pieces = lax.all_to_all(pieces, ('chips', 'core', 'mp'), 0, 0, tiled=True)  32.4 us
    all_gather x2, waiting for transfers between devices, gather_blk(): parts = lax.all_gather(parts, 'core', axis=1)  17 us
    all_gather x1, blocking collectives, body(): lax.all_gather(trainer_q.astype(jnp.bfloat16), 'dp', axis=1, tiled=True)  12.5 us
    all_to_all x1, starting transfers between devices, body(): pieces = lax.all_to_all(pieces, ('chips', 'core', 'mp'), 0, 0, tiled=True)  10.7 us
    another operation x1, local copies, waits for them, and re-layouts, body(): shard_piece[0].reshape(key_count, head_count, HD)  10.6 us
    another operation x1, local copies, waits for them, and re-layouts, body(): shard_piece[1].reshape(key_count, head_count, HD)  10.2 us
    dot_general x1, matrix products, body(): jnp.einsum('td,hd->th', token_local, head_weights, preferred_element_type...  9.78 us
  transfers between devices with their start and end apart: 5, of which 5 were waited for; matrix products, arithmetic and copies ran while one was open for 13% of the time, Pallas kernels for 0%

profile of v2, /device:TPU:25, one launch (start us, length us, event | category | flops | bytes accessed | tf_op | source)
XLA Modules:
  0.0 261.8 jit_solution(8854749194765089448)
XLA Ops:
  7.2 0.0 copy-start.1
  7.2 0.0 all-gather.13.cloned.1.call-start
  7.2 0.7 all-gather.13.cloned.1.call-update
  7.9 0.0 all-gather.9.cloned.1.call-start
  8.0 1.0 convert_element_type.18
  9.0 12.5 %all_gather.27 = bf16[56,7168]{1,0:T(8,128)(2,1)} all-gather(bf16[56,1792]{1,0:T(8,128)(2,1)S(1)} %convert_element_type.18), channel_id=1, replica_groups=mesh['dp'=4,'chips'=8,'core'=2,'mp'=4] {'dp'}, dimensions={1}, use_global_device_ids=true | all-gather | bytes 1003520 | tf_op jit(solution)/shard_map/all_gather | solution.py:45
  21.5 0.0 all-gather.9.cloned.1.call-update
  21.5 0.0 all-gather.15.cloned.1.call-start
  21.6 39.1 %all-gather.13.cloned.1.call-done = bf16[16,128,896]{2,1,0:T(8,128)(2,1)} async-done(((bf16[2,128,896]{2,1,0:T(8,128)(2,1)}), bf16[16,128,896]{2,1,0:T(8,128)(2,1)}) %all-gather.13.cloned.1.call-update) | async-done | bytes 3670032 | tf_op jit(solution)/shard_map/all_gather | solution.py:34
  60.7 0.0 all-gather.15.cloned.1.call-update
  60.7 0.0 all-gather.11.cloned.1.call-start
  60.7 77.0 %all-gather.9.cloned.1.call-done = bf16[448,7168]{1,0:T(8,128)(2,1)} async-done(((bf16[56,7168]{1,0:T(8,128)(2,1)}), bf16[448,7168]{1,0:T(8,128)(2,1)}) %all-gather.9.cloned.1.call-update) | async-done | bytes 6422544 | tf_op jit(solution)/shard_map/all_gather | solution.py:34
  137.7 0.0 all-gather.11.cloned.1.call-update
  137.8 0.0 copy-start.2
  137.8 0.0 copy-done.1
  137.8 0.0 copy-start.3
  137.8 0.1 copy.57
  137.9 2.2 broadcast_in_dim.82
  140.1 10.7 %all-to-all-start = ((bf16[64,256,112]{1,2,0:T(8,128)(2,1)}), bf16[64,256,112]{1,2,0:T(8,128)(2,1)}, u32[]{:S(2)}, u32[]{:S(2)}) async-start(bf16[64,256,112]{1,2,0:T(8,128)(2,1)} %bitcast.74), calls=%async_computation | async-start | bytes 7340032 | tf_op jit(solution)/shard_map/all_to_all | solution.py:57
  151.5 0.0 copy-done.2
  151.5 0.1 fusion.46
  151.6 0.2 copy.37
  152.4 0.2 copy.38
  152.7 0.0 copy-done.3
  152.7 0.2 and_reduce_fusion
  152.9 0.1 fusion.31
  153.0 11.7 %all-gather.15.cloned.1.call-done = bf16[8,4,128,896]{3,2,1,0:T(8,128)(2,1)} async-done(((bf16[8,2,128,896]{3,2,1,0:T(8,128)(2,1)}), bf16[8,4,128,896]{3,2,1,0:T(8,128)(2,1)}) %all-gather.15.cloned.1.call-update) | async-done | bytes 7340048 | tf_op jit(solution)/shard_map/all_gather | solution.py:35
  164.7 7.2 %fusion.45 = (bf16[1,16,128,896]{3,2,0,1:T(8,128)(2,1)}, bf16[1,16,128,896]{3,2,0,1:T(8,128)(2,1)}) fusion(bf16[2,16,128,896]{3,2,0,1:T(8,128)(2,1)} %bitcast.75), kind=kLoop, calls=%fused_computation.59 | loop fusion | bytes 14680064 | tf_op jit(solution)/shard_map/slice | solution.py:90
  171.9 10.2 %reshape.119 = bf16[2048,4,224]{2,1,0:T(4,128)(2,1)} reshape(bf16[1,16,128,896]{3,2,0,1:T(8,128)(2,1)} %get-tuple-element.13) | data formatting | bytes 7340032 | tf_op jit(solution)/shard_map/reshape;squeeze | solution.py:91
  182.2 10.6 %reshape.118 = bf16[2048,4,224]{2,1,0:T(4,128)(2,1)} reshape(bf16[1,16,128,896]{3,2,0,1:T(8,128)(2,1)} %get-tuple-element.12) | data formatting | bytes 7340032 | tf_op jit(solution)/shard_map/reshape;squeeze | solution.py:90
  192.7 5.2 %all-gather.11.cloned.1.call-done = bf16[8,112,7168]{2,1,0:T(8,128)(2,1)} async-done(((bf16[8,56,7168]{2,1,0:T(8,128)(2,1)}), bf16[8,112,7168]{2,1,0:T(8,128)(2,1)}) %all-gather.11.cloned.1.call-update) | async-done | bytes 12845072 | tf_op jit(solution)/shard_map/all_gather | solution.py:35
  198.0 1.6 constant_dynamic-slice_fusion
  199.6 1.2 copy.42
  200.8 32.4 %all-to-all-done = bf16[64,256,112]{1,2,0:T(8,128)(2,1)} async-done(((bf16[64,256,112]{1,2,0:T(8,128)(2,1)}), bf16[64,256,112]{1,2,0:T(8,128)(2,1)}, u32[]{:S(2)}, u32[]{:S(2)}) %all-to-all-start) | async-done | bytes 3670048 | tf_op jit(solution)/shard_map/all_to_all | solution.py:57
  233.3 9.8 %convolution_convert_fusion = bf16[256,896]{1,0:T(8,128)(2,1)S(1)} fusion(bf16[256,7168]{0,1:T(8,128)(2,1)} %bitcast.5, bf16[896,7168]{1,0:T(8,128)(2,1)} %bitcast.86), kind=kOutput, calls=%fused_computation.23 | convolution fusion | flops 3288563712 | bytes 16973824 | tf_op jit(solution)/shard_map/td,hd->th/dot_general | solution.py:59
  243.1 0.2 copy.36
  243.3 4.8 %fusion = (f32[4,256]{1,0:T(4,128)S(1)}, f32[4,256,2048]{2,1,0:T(8,128)S(1)}) fusion(pred[2048]{0:T(1024)(128)(4,1)S(1)} %and_reduce_fusion, bf16[256,4,224]{0,2,1:T(8,128)(2,1)S(1)} %bitcast.80, bf16[2048,4,224]{2,1,0:T(4,128)(2,1)} %reshape.118), kind=kOutput, calls=%fused_computation.2 | convolution fusion | flops 945814528 | bytes 12523520 | tf_op jit(solution)/shard_map/thd,khd->htk/dot_general | solution.py:12
  248.1 0.0 copy-start
  248.1 0.4 fusion.47
  248.5 2.4 fusion.1
  250.9 0.0 copy-done
  250.9 2.7 %fusion.14 = f32[256,4,224]{0,2,1:T(8,128)S(1)} fusion(bf16[2048,4,224]{2,1,0:T(4,128)(2,1)S(1)} %copy-done, f32[4,256,2048]{2,1,0:T(8,128)S(1)} %get-tuple-element.22, f32[4,256]{1,0:T(4,128)S(1)} %get-tuple-element.18, pred[2048]{0:T(1024)(128)(4,1)S(1)} %and_reduce_fusion), kind=kOutput, calls=%fused_computation.16 | convolution fusion | flops 950009856 | bytes 12982272 | tf_op jit(solution)/shard_map/htk,khd->htd/dot_general | solution.py:20
  253.6 0.2 fusion.25
  253.8 0.4 fusion.24
  254.2 1.0 copy.43
  (5 shorter events, 0.0 us)
Async XLA Ops:
  7.2 130.6 %copy-start.1 = (bf16[4096,112]{0,1:T(8,128)(2,1)S(1)}, bf16[4096,112]{0,1:T(8,128)(2,1)}, u32[]{:S(2)}) copy-start(bf16[4096,112]{0,1:T(8,128)(2,1)} %param.7) | copy-start | bytes 2752516
  7.2 53.5 %all-gather.13.cloned.1.call-start = ((), (), s32[]{:S(2)}) async-start(), calls=%async_computation.3 | async-start | bytes 4128768 | tf_op jit(solution)/shard_map/all_gather | solution.py:34
  7.9 129.8 %all-gather.9.cloned.1.call-start = ((), (), s32[]{:S(2)}) async-start(), calls=%async_computation.1 | async-start | bytes 7225344 | tf_op jit(solution)/shard_map/all_gather | solution.py:34
  21.5 143.1 %all-gather.15.cloned.1.call-start = ((), (), s32[]{:S(2)}) async-start(), calls=%async_computation.4 | async-start | bytes 11010048 | tf_op jit(solution)/shard_map/all_gather | solution.py:35
  60.7 137.3 %all-gather.11.cloned.1.call-start = ((), (), s32[]{:S(2)}) async-start(), calls=%async_computation.2 | async-start | bytes 19267584 | tf_op jit(solution)/shard_map/all_gather | solution.py:35
  137.8 13.7 %copy-start.2 = (bf16[2,256,896]{2,1,0:T(8,128)(2,1)S(1)}, bf16[2,256,896]{2,1,0:T(8,128)(2,1)}, u32[]{:S(2)}) copy-start(bf16[2,256,896]{2,1,0:T(8,128)(2,1)} %param.10) | copy-start | bytes 2752516
  137.8 14.9 %copy-start.3 = (s32[1,64]{1,0:T(1,128)S(1)}, s32[1,64]{1,0:T(1,128)}, u32[]{:S(2)}) copy-start(s32[1,64]{1,0:T(1,128)} %param.11) | copy-start | bytes 772
  140.1 93.2 %all-to-all-start = ((bf16[64,256,112]{1,2,0:T(8,128)(2,1)}), bf16[64,256,112]{1,2,0:T(8,128)(2,1)}, u32[]{:S(2)}, u32[]{:S(2)}) async-start(bf16[64,256,112]{1,2,0:T(8,128)(2,1)} %bitcast.74), calls=%async_computation | async-start | bytes 7340032 | tf_op jit(solution)/shard_map/all_to_all | solution.py:57
  248.1 2.8 %copy-start = (bf16[2048,4,224]{2,1,0:T(4,128)(2,1)S(1)}, bf16[2048,4,224]{2,1,0:T(4,128)(2,1)}, u32[]{:S(2)}) copy-start(bf16[2048,4,224]{2,1,0:T(4,128)(2,1)} %reshape.119) | copy-start | bytes 11010052
Sparse Core Ops, SparseCore 0:
  9.8 50.8 all-gather.12
  62.5 75.2 all-gather.8
  139.5 25.1 all-gather.14
  166.4 31.5 all-gather.10

commit v3 on v1

--- a/solution.py
+++ b/solution.py
@@ -29,13 +29,19 @@
 def body(tokens, trainer_q, kv_pool, prompt_kv, page_table, page_count, prompt_len):
     blk_size = lax.axis_size("blk")
     mp_size = lax.axis_size("mp")
-    trainer_rows = lax.all_gather(trainer_q.astype(jnp.bfloat16), "dp", axis=1, tiled=True)
-    head_weights = lax.all_gather(trainer_rows, "blk", axis=0, tiled=True)
-    head_width, model_width = head_weights.shape
-    block_cols = model_width // blk_size
-    server_q = lax.dynamic_slice_in_dim(
-        head_weights, lax.axis_index("blk") * block_cols, block_cols, axis=1
-    )
+    dp_size = lax.axis_size("dp")
+    quarter = lax.all_gather(trainer_q.astype(jnp.bfloat16), "blk", axis=0, tiled=True)
+    head_width, quarter_cols = quarter.shape
+    quarter = jnp.broadcast_to(quarter[None], (dp_size, head_width, quarter_cols))
+    quarters = lax.all_to_all(quarter, "dp", 0, 0, tiled=True)
+    block_cols = quarter_cols * dp_size // blk_size
+    blocks_per_quarter = quarter_cols // block_cols
+    b = lax.axis_index("blk")
+    server_q = lax.dynamic_slice(
+        quarters,
+        (b // blocks_per_quarter, 0, (b % blocks_per_quarter) * block_cols),
+        (1, head_width, block_cols),
+    )[0]
     group_rows, piece_cols = tokens.shape
     own_rows = group_rows // blk_size
     pieces = tokens.reshape(blk_size, 1, own_rows, piece_cols)
@@ -44,7 +50,10 @@
     pieces = lax.all_to_all(pieces, ("blk", "mp"), 0, 0, tiled=True)
     token_local = jnp.transpose(pieces, (1, 0, 2)).reshape(own_rows, -1)
     queries = jnp.einsum(
-        "td,hd->th", token_local, head_weights, preferred_element_type=jnp.float32
+        "tgd,ghd->th",
+        token_local.reshape(own_rows, dp_size, quarter_cols),
+        quarters,
+        preferred_element_type=jnp.float32,
     )
     queries = queries.astype(jnp.bfloat16)
     head_count = head_width // HD

time: 234 us -> 333 us (1.42)
  waiting for transfers between devices: 142 us -> 242 us
  blocking collectives: 12.5 us -> 0 us
  local copies, waits for them, and re-layouts: 27.1 us -> 32.6 us
    all_to_all x0 -> x1, waiting for transfers between devices: none -> 141 us  [body(): quarters = lax.all_to_all(quarter, 'dp', 0, 0, tiled=True)]
    all_gather x1, waiting for transfers between devices: 69.7 us -> 0.02 us  [body(): shard_piece = lax.all_gather(kv_pool, 'blk', axis=1, tiled=True)]
    all_to_all x1, waiting for transfers between devices: 0.01 us -> 58.6 us  [body(): pieces = lax.all_to_all(pieces, ('blk', 'mp'), 0, 0, tiled=True)]
    all_gather x1, waiting for transfers between devices: 71.3 us -> 42.2 us  [body(): lax.all_gather(trainer_q.astype(jnp.bfloat16), 'blk', axis=0, tiled=True)]
    all_gather x1 -> x0, blocking collectives: 12.5 us -> none  [body(): lax.all_gather(trainer_q.astype(jnp.bfloat16), 'dp', axis=1, tiled=True)]
    broadcast_in_dim x0 -> x1, local copies, waits for them, and re-layouts: none -> 7.05 us  [body(): jnp.broadcast_to(quarter[None], (dp_size, head_width, quarter_cols))]
    all_to_all x0 -> x1, starting transfers between devices: none -> 6.48 us  [body(): quarters = lax.all_to_all(quarter, 'dp', 0, 0, tiled=True)]
  transfers between devices with their start and end apart: 3 -> 4, of which waited for: 2 -> 3; matrix products, arithmetic and copies ran while one was open for 12% -> 7% of each run, Pallas kernels for 0% -> 0%
where the time goes in v3:
time: 333 us; the launch traced here: 329 us
  waiting for transfers between devices  242 us (73%)
  local copies, waits for them, and re-layouts  32.6 us (10%)
  starting transfers between devices  17.6 us (5%)
  matrix products  16.7 us (5%)
  between operations  15.6 us (5%)
  other arithmetic  4.59 us (1%)
    all_to_all x1, waiting for transfers between devices, body(): quarters = lax.all_to_all(quarter, 'dp', 0, 0, tiled=True)  141 us
    all_to_all x1, waiting for transfers between devices, body(): pieces = lax.all_to_all(pieces, ('blk', 'mp'), 0, 0, tiled=True)  58.6 us
    all_gather x1, waiting for transfers between devices, body(): lax.all_gather(trainer_q.astype(jnp.bfloat16), 'blk', axis=0, tiled=True)  42.2 us
    slice x2, local copies, waits for them, and re-layouts, body(): shard_piece[0].reshape(key_count, head_count, HD)  12.8 us
    all_to_all x1, starting transfers between devices, body(): pieces = lax.all_to_all(pieces, ('blk', 'mp'), 0, 0, tiled=True)  11 us
    dot_general x1, matrix products, body(): jnp.einsum('tgd,ghd->th', token_local.reshape(own_rows, dp_size, quarter_...  9.78 us
    broadcast_in_dim x1, local copies, waits for them, and re-layouts, body(): jnp.broadcast_to(quarter[None], (dp_size, head_width, quarter_cols))  7.05 us
  transfers between devices with their start and end apart: 4, of which 3 were waited for; matrix products, arithmetic and copies ran while one was open for 7% of the time, Pallas kernels for 0%

profile of v3, /device:TPU:25, one launch (start us, length us, event | category | flops | bytes accessed | tf_op | source)
XLA Modules:
  0.0 329.0 jit_solution(3836947053904768665)
XLA Ops:
  7.2 0.0 all-gather.3.cloned.1.call-start
  7.2 1.7 convert_element_type.18
  8.9 0.0 all-gather.3.cloned.1.call-update
  8.9 42.2 %all-gather.3.cloned.1.call-done = bf16[896,1792]{1,0:T(8,128)(2,1)} async-done(((bf16[56,1792]{1,0:T(8,128)(2,1)}), bf16[896,1792]{1,0:T(8,128)(2,1)}) %all-gather.3.cloned.1.call-update) | async-done | bytes 3211280 | tf_op jit(solution)/shard_map/all_gather | solution.py:33
  51.1 7.0 %broadcast_in_dim.84 = bf16[4,896,1792]{2,1,0:T(8,128)(2,1)} broadcast(bf16[896,1792]{1,0:T(8,128)(2,1)} %all-gather.3.cloned.1.call-done), dimensions={1,2} | broadcast | bytes 16056320 | tf_op jit(solution)/shard_map/broadcast_in_dim | solution.py:35
  58.2 0.0 copy-start.1
  58.2 6.5 %all-to-all-start = ((bf16[4,896,1792]{2,1,0:T(8,128)(2,1)}), bf16[4,896,1792]{2,1,0:T(8,128)(2,1)}, u32[]{:S(2)}, u32[]{:S(2)}) async-start(bf16[4,896,1792]{2,1,0:T(8,128)(2,1)} %broadcast_in_dim.84), calls=%async_computation | async-start | bytes 25690112 | tf_op jit(solution)/shard_map/all_to_all | solution.py:36
  64.7 0.0 copy-start.2
  64.7 0.0 all-gather.5.cloned.1.call-start
  64.7 0.7 all-gather.5.cloned.1.call-update
  65.4 0.0 copy-done.1
  65.4 0.0 copy-start.3
  65.4 0.1 copy.42
  65.5 140.6 %all-to-all-done = bf16[4,896,1792]{2,1,0:T(8,128)(2,1)} async-done(((bf16[4,896,1792]{2,1,0:T(8,128)(2,1)}), bf16[4,896,1792]{2,1,0:T(8,128)(2,1)}, u32[]{:S(2)}, u32[]{:S(2)}) %all-to-all-start) | async-done | bytes 12845088 | tf_op jit(solution)/shard_map/all_to_all | solution.py:36
  206.1 2.1 broadcast_in_dim.89
  208.2 11.0 %all-to-all-start.1 = ((bf16[64,256,112]{1,2,0:T(8,128)(2,1)}), bf16[64,256,112]{1,2,0:T(8,128)(2,1)}, u32[]{:S(2)}, u32[]{:S(2)}) async-start(bf16[64,256,112]{1,2,0:T(8,128)(2,1)} %bitcast.69), calls=%async_computation.1 | async-start | bytes 7340032 | tf_op jit(solution)/shard_map/all_to_all | solution.py:50
  219.9 0.0 copy-done.2
  219.9 0.1 fusion.38
  220.0 0.2 copy.32
  220.8 0.2 copy.33
  221.1 0.0 copy-done.3
  221.1 0.2 and_reduce_fusion
  221.3 0.1 fusion.23
  221.4 0.0 all-gather.5.cloned.1.call-done
  221.4 6.7 %fusion.37 = (bf16[1,2048,896]{2,1,0:T(8,128)(2,1)}, bf16[1,2048,896]{2,1,0:T(8,128)(2,1)}) fusion(bf16[2,2048,896]{2,1,0:T(8,128)(2,1)} %all-gather.5.cloned.1.call-done), kind=kLoop, calls=%fused_computation.53 | loop fusion | bytes 14680064 | tf_op jit(solution)/shard_map/slice | solution.py:86
  228.1 6.1 %copy.36 = bf16[1,2048,896]{1,2,0:T(8,128)(2,1)} copy(bf16[1,2048,896]{2,1,0:T(8,128)(2,1)} %get-tuple-element.11) | data formatting | bytes 7340032 | tf_op jit(solution)/shard_map/slice | solution.py:87
  234.2 6.1 %copy.35 = bf16[1,2048,896]{1,2,0:T(8,128)(2,1)} copy(bf16[1,2048,896]{2,1,0:T(8,128)(2,1)} %get-tuple-element.10) | data formatting | bytes 7340032 | tf_op jit(solution)/shard_map/slice | solution.py:86
  240.3 1.6 constant_dynamic-slice_fusion
  241.9 1.2 copy.28
  243.1 58.6 %all-to-all-done.1 = bf16[64,256,112]{1,2,0:T(8,128)(2,1)} async-done(((bf16[64,256,112]{1,2,0:T(8,128)(2,1)}), bf16[64,256,112]{1,2,0:T(8,128)(2,1)}, u32[]{:S(2)}, u32[]{:S(2)}) %all-to-all-start.1) | async-done | bytes 3670048 | tf_op jit(solution)/shard_map/all_to_all | solution.py:50
  301.7 9.8 %fusion.15 = bf16[256,896]{1,0:T(8,128)(2,1)S(1)} fusion(bf16[256,4,1792]{0,2,1:T(8,128)(2,1)} %bitcast.4, bf16[4,896,1792]{2,1,0:T(8,128)(2,1)} %all-to-all-done), kind=kOutput, calls=%fused_computation.17 | convolution fusion | flops 3288563712 | bytes 16973824 | tf_op jit(solution)/shard_map/tgd,ghd->th/dot_general | solution.py:52
  311.4 0.2 copy.31
  311.7 0.0 copy-start
  311.7 4.0 %fusion = (f32[4,256]{1,0:T(4,128)S(1)}, f32[4,256,2048]{2,1,0:T(8,128)S(1)}) fusion(pred[2048]{0:T(1024)(128)(4,1)S(1)} %and_reduce_fusion, bf16[256,4,224]{0,2,1:T(8,128)(2,1)S(1)} %bitcast.71, bf16[2048,4,224]{0,2,1:T(8,128)(2,1)} %bitcast.70), kind=kOutput, calls=%fused_computation.2 | convolution fusion | flops 945814528 | bytes 12523520 | tf_op jit(solution)/shard_map/thd,khd->htk/dot_general | solution.py:12
  315.6 0.4 fusion.39
  316.0 2.4 fusion.1
  318.4 0.0 copy-done
  318.4 2.1 fusion.7
  320.6 0.2 fusion.17
  320.8 0.4 fusion.16
  321.2 1.0 copy.37
  (5 shorter events, 0.0 us)
Async XLA Ops:
  7.2 44.0 %all-gather.3.cloned.1.call-start = ((), (), s32[]{:S(2)}) async-start(), calls=%async_computation.2 | async-start | bytes 3411968 | tf_op jit(solution)/shard_map/all_gather | solution.py:33
  58.2 7.3 %copy-start.1 = (bf16[4096,112]{0,1:T(8,128)(2,1)S(1)}, bf16[4096,112]{0,1:T(8,128)(2,1)}, u32[]{:S(2)}) copy-start(bf16[4096,112]{0,1:T(8,128)(2,1)} %param.7) | copy-start | bytes 2752516
  58.2 147.9 %all-to-all-start = ((bf16[4,896,1792]{2,1,0:T(8,128)(2,1)}), bf16[4,896,1792]{2,1,0:T(8,128)(2,1)}, u32[]{:S(2)}, u32[]{:S(2)}) async-start(bf16[4,896,1792]{2,1,0:T(8,128)(2,1)} %broadcast_in_dim.84), calls=%async_computation | async-start | bytes 25690112 | tf_op jit(solution)/shard_map/all_to_all | solution.py:36
  64.7 155.2 %copy-start.2 = (bf16[2,256,896]{2,1,0:T(8,128)(2,1)S(1)}, bf16[2,256,896]{2,1,0:T(8,128)(2,1)}, u32[]{:S(2)}) copy-start(bf16[2,256,896]{2,1,0:T(8,128)(2,1)} %param.10) | copy-start | bytes 2752516
  64.7 156.7 %all-gather.5.cloned.1.call-start = ((), (), s32[]{:S(2)}) async-start(), calls=%async_computation.3 | async-start | bytes 7798784 | tf_op jit(solution)/shard_map/all_gather | solution.py:78
  65.4 155.7 %copy-start.3 = (s32[1,64]{1,0:T(1,128)S(1)}, s32[1,64]{1,0:T(1,128)}, u32[]{:S(2)}) copy-start(s32[1,64]{1,0:T(1,128)} %param.11) | copy-start | bytes 772
  208.2 93.5 %all-to-all-start.1 = ((bf16[64,256,112]{1,2,0:T(8,128)(2,1)}), bf16[64,256,112]{1,2,0:T(8,128)(2,1)}, u32[]{:S(2)}, u32[]{:S(2)}) async-start(bf16[64,256,112]{1,2,0:T(8,128)(2,1)} %bitcast.69), calls=%async_computation.1 | async-start | bytes 7340032 | tf_op jit(solution)/shard_map/all_to_all | solution.py:50
  311.7 6.8 %copy-start = (bf16[1,2048,896]{1,2,0:T(8,128)(2,1)S(1)}, bf16[1,2048,896]{1,2,0:T(8,128)(2,1)}, u32[]{:S(2)}) copy-start(bf16[1,2048,896]{1,2,0:T(8,128)(2,1)} %copy.36) | copy-start | bytes 11010052
Sparse Core Ops, SparseCore 0:
  10.4 40.6 all-gather.2
  67.3 51.0 all-gather.4

commit v4 on v1

--- a/solution.py
+++ b/solution.py
@@ -66,7 +66,11 @@
         prompt_kv[1].reshape(own_rows, head_count, HD),
         own_mask,
     )
-    shard_piece = lax.all_gather(kv_pool, "blk", axis=1, tiled=True)
+    kv_pieces = jnp.broadcast_to(kv_pool[None], (blk_size,) + kv_pool.shape)
+    kv_pieces = lax.all_to_all(kv_pieces, "blk", 0, 0, tiled=True)
+    shard_piece = jnp.moveaxis(kv_pieces, 0, 1).reshape(
+        kv_pool.shape[0], blk_size * kv_pool.shape[1], kv_pool.shape[2]
+    )
     key_count = shard_piece.shape[1]
     page_ids = jnp.arange(key_count, dtype=jnp.int32) // PAGE
     page_used = jnp.any((row_pages[None, :] == page_ids[:, None]) & live_slots[None, :], axis=1)

time: 234 us -> 296 us (1.26)
  waiting for transfers between devices: 142 us -> 178 us
  local copies, waits for them, and re-layouts: 27.1 us -> 42.2 us
  starting transfers between devices: 14.4 us -> 23.2 us
    all_to_all x0 -> x1, waiting for transfers between devices: none -> 130 us  [body(): kv_pieces = lax.all_to_all(kv_pieces, 'blk', 0, 0, tiled=True)]
    all_gather x1, waiting for transfers between devices: 71.3 us -> 0.01 us  [body(): head_weights = lax.all_gather(trainer_rows, 'blk', axis=0, tiled=True)]
    all_gather x1 -> x0, waiting for transfers between devices: 69.7 us -> none  [body(): shard_piece = lax.all_gather(kv_pool, 'blk', axis=1, tiled=True)]
    all_to_all x1, waiting for transfers between devices: 0.01 us -> 48 us  [body(): pieces = lax.all_to_all(pieces, ('blk', 'mp'), 0, 0, tiled=True)]
    another operation x0 -> x2, local copies, waits for them, and re-layouts: none -> 13.4 us  [the longest x1 6.71 us: body(): shard_piece[0].reshape(key_count, head_count, HD)]
    all_to_all x0 -> x1, starting transfers between devices: none -> 9.23 us  [body(): kv_pieces = lax.all_to_all(kv_pieces, 'blk', 0, 0, tiled=True)]
    broadcast_in_dim x0 -> x1, local copies, waits for them, and re-layouts: none -> 4.68 us  [body(): kv_pieces = jnp.broadcast_to(kv_pool[None], (blk_size,) + kv_pool.shape)]
    slice x2, local copies, waits for them, and re-layouts: 12.9 us -> 9.86 us  [body(): shard_piece[0].reshape(key_count, head_count, HD)]
  transfers between devices with their start and end apart: 3 -> 3, of which waited for: 2 -> 2; matrix products, arithmetic and copies ran while one was open for 12% -> 14% of each run, Pallas kernels for 0% -> 0%
where the time goes in v4:
time: 296 us; the launch traced here: 292 us
  waiting for transfers between devices  178 us (60%)
  local copies, waits for them, and re-layouts  42.2 us (14%)
  starting transfers between devices  23.2 us (8%)
  matrix products  16.7 us (6%)
  between operations  15.5 us (5%)
  blocking collectives  12.5 us (4%)
  other arithmetic  3.74 us (1%)
    all_to_all x1, waiting for transfers between devices, body(): kv_pieces = lax.all_to_all(kv_pieces, 'blk', 0, 0, tiled=True)  130 us
    all_to_all x1, waiting for transfers between devices, body(): pieces = lax.all_to_all(pieces, ('blk', 'mp'), 0, 0, tiled=True)  48 us
    all_to_all x1, starting transfers between devices, body(): pieces = lax.all_to_all(pieces, ('blk', 'mp'), 0, 0, tiled=True)  14 us
    all_gather x1, blocking collectives, body(): lax.all_gather(trainer_q.astype(jnp.bfloat16), 'dp', axis=1, tiled=True)  12.5 us
    slice x2, local copies, waits for them, and re-layouts, body(): shard_piece[0].reshape(key_count, head_count, HD)  9.86 us
    dot_general x1, matrix products, body(): jnp.einsum('td,hd->th', token_local, head_weights, preferred_element_type...  9.78 us
    all_to_all x1, starting transfers between devices, body(): kv_pieces = lax.all_to_all(kv_pieces, 'blk', 0, 0, tiled=True)  9.23 us
    another operation x1, local copies, waits for them, and re-layouts, body(): shard_piece[0].reshape(key_count, head_count, HD)  6.71 us
  transfers between devices with their start and end apart: 3, of which 2 were waited for; matrix products, arithmetic and copies ran while one was open for 14% of the time, Pallas kernels for 0%

profile of v4, /device:TPU:25, one launch (start us, length us, event | category | flops | bytes accessed | tf_op | source)
XLA Modules:
  0.0 291.7 jit_solution(3913981569663224814)
XLA Ops:
  7.2 0.0 all-gather.2.cloned.1.call-start
  7.2 1.0 convert_element_type.18
  8.2 12.5 %all_gather.6 = bf16[56,7168]{1,0:T(8,128)(2,1)} all-gather(bf16[56,1792]{1,0:T(8,128)(2,1)S(1)} %convert_element_type.18), channel_id=1, replica_groups=mesh['dp'=4,'blk'=16,'mp'=4] {'dp'}, dimensions={1}, use_global_device_ids=true | all-gather | bytes 1003520 | tf_op jit(solution)/shard_map/all_gather | solution.py:32
  20.8 0.0 all-gather.2.cloned.1.call-update
  20.8 1.3 copy.41
  22.1 4.7 %broadcast_in_dim.94 = bf16[16,2,128,896]{2,3,1,0:T(8,128)(2,1)} broadcast(bf16[2,128,896]{1,2,0:T(8,128)(2,1)S(1)} %copy.41), dimensions={1,2,3} | broadcast | bytes 7798784 | tf_op jit(solution)/shard_map/broadcast_in_dim | solution.py:69
  26.8 0.0 copy-start.1
  26.8 9.2 %all-to-all-start.1 = ((bf16[16,2,128,896]{2,3,1,0:T(8,128)(2,1)}), bf16[16,2,128,896]{2,3,1,0:T(8,128)(2,1)}, u32[]{:S(2)}, u32[]{:S(2)}) async-start(bf16[16,2,128,896]{2,3,1,0:T(8,128)(2,1)} %broadcast_in_dim.94), calls=%async_computation.1 | async-start | bytes 14680064 | tf_op jit(solution)/shard_map/all_to_all | solution.py:70
  36.0 0.0 copy-start.2
  36.0 0.0 copy-done.1
  36.0 0.0 copy-start.3
  36.0 0.1 copy.49
  36.1 129.8 %all-to-all-done.1 = bf16[16,2,128,896]{2,3,1,0:T(8,128)(2,1)} async-done(((bf16[16,2,128,896]{2,3,1,0:T(8,128)(2,1)}), bf16[16,2,128,896]{2,3,1,0:T(8,128)(2,1)}, u32[]{:S(2)}, u32[]{:S(2)}) %all-to-all-start.1) | async-done | bytes 7340064 | tf_op jit(solution)/shard_map/all_to_all | solution.py:70
  165.9 2.2 broadcast_in_dim.88
  168.1 14.0 %all-to-all-start = ((bf16[64,256,112]{1,2,0:T(8,128)(2,1)}), bf16[64,256,112]{1,2,0:T(8,128)(2,1)}, u32[]{:S(2)}, u32[]{:S(2)}) async-start(bf16[64,256,112]{1,2,0:T(8,128)(2,1)} %bitcast.71), calls=%async_computation | async-start | bytes 7340032 | tf_op jit(solution)/shard_map/all_to_all | solution.py:44
  183.3 0.0 copy-done.2
  183.4 0.1 fusion.37
  183.4 0.2 copy.39
  183.7 0.2 copy.38
  183.9 0.0 copy-done.3
  183.9 0.2 and_reduce_fusion
  184.1 0.1 fusion.22
  184.2 5.7 %fusion.36 = (bf16[1,16,128,896]{2,3,0,1:T(8,128)(2,1)S(1)}, bf16[1,16,128,896]{2,3,0,1:T(8,128)(2,1)}) fusion(bf16[2,16,128,896]{2,3,0,1:T(8,128)(2,1)} %bitcast.11), kind=kLoop, calls=%fused_computation.52 | loop fusion | bytes 14680064 | tf_op jit(solution)/shard_map/slice | solution.py:81
  189.9 4.2 %copy.42 = bf16[1,16,128,896]{2,1,3,0:T(8,128)(2,1)} copy(bf16[1,16,128,896]{2,3,0,1:T(8,128)(2,1)S(1)} %get-tuple-element.12) | data formatting | bytes 7340032 | tf_op jit(solution)/shard_map/slice | solution.py:81
  194.1 6.7 %reshape_squeeze.14 = bf16[2048,4,224]{0,2,1:T(8,128)(2,1)} reshape(bf16[1,16,128,896]{2,1,3,0:T(8,128)(2,1)} %copy.42) | data formatting | bytes 7340032 | tf_op jit(solution)/shard_map/reshape;squeeze | solution.py:81
  200.8 6.2 %copy.43 = bf16[1,16,128,896]{2,1,3,0:T(8,128)(2,1)} copy(bf16[1,16,128,896]{2,3,0,1:T(8,128)(2,1)} %get-tuple-element.13) | data formatting | bytes 7340032 | tf_op jit(solution)/shard_map/slice | solution.py:82
  207.0 6.7 %reshape_squeeze.15 = bf16[2048,4,224]{0,2,1:T(8,128)(2,1)} reshape(bf16[1,16,128,896]{2,1,3,0:T(8,128)(2,1)} %copy.43) | data formatting | bytes 7340032 | tf_op jit(solution)/shard_map/reshape;squeeze | solution.py:82
  213.6 0.0 all-gather.2.cloned.1.call-done
  213.6 1.6 constant_dynamic-slice_fusion
  215.3 1.2 copy.44
  216.5 48.0 %all-to-all-done = bf16[64,256,112]{1,2,0:T(8,128)(2,1)} async-done(((bf16[64,256,112]{1,2,0:T(8,128)(2,1)}), bf16[64,256,112]{1,2,0:T(8,128)(2,1)}, u32[]{:S(2)}, u32[]{:S(2)}) %all-to-all-start) | async-done | bytes 3670048 | tf_op jit(solution)/shard_map/all_to_all | solution.py:44
  264.5 9.8 %convolution_convert_fusion = bf16[256,896]{1,0:T(8,128)(2,1)S(1)} fusion(bf16[256,7168]{0,1:T(8,128)(2,1)} %bitcast.3, bf16[896,7168]{1,0:T(8,128)(2,1)} %all-gather.2.cloned.1.call-done), kind=kOutput, calls=%fused_computation.16 | convolution fusion | flops 3288563712 | bytes 16973824 | tf_op jit(solution)/shard_map/td,hd->th/dot_general | solution.py:46
  274.3 0.2 copy.37
  274.5 0.4 fusion.38
  274.9 0.0 copy-start
  274.9 4.0 %fusion = (f32[4,256]{1,0:T(4,128)S(1)}, f32[4,256,2048]{2,1,0:T(8,128)S(1)}) fusion(pred[2048]{0:T(1024)(128)(4,1)S(1)} %and_reduce_fusion, bf16[256,4,224]{0,2,1:T(8,128)(2,1)S(1)} %bitcast.73, bf16[2048,4,224]{0,2,1:T(8,128)(2,1)} %reshape_squeeze.14), kind=kOutput, calls=%fused_computation.2 | convolution fusion | flops 945814528 | bytes 12523520 | tf_op jit(solution)/shard_map/thd,khd->htk/dot_general | solution.py:12
  278.9 2.2 fusion.1
  281.1 0.0 copy-done
  281.1 2.1 fusion.7
  283.2 0.2 fusion.16
  283.4 0.4 fusion.15
  283.9 1.0 copy.45
  (5 shorter events, 0.0 us)
Async XLA Ops:
  7.2 206.5 %all-gather.2.cloned.1.call-start = ((), (), s32[]{:S(2)}) async-start(), calls=%async_computation.2 | async-start | bytes 13647872 | tf_op jit(solution)/shard_map/all_gather | solution.py:33
  26.8 9.2 %copy-start.1 = (bf16[4096,112]{0,1:T(8,128)(2,1)S(1)}, bf16[4096,112]{0,1:T(8,128)(2,1)}, u32[]{:S(2)}) copy-start(bf16[4096,112]{0,1:T(8,128)(2,1)} %param.7) | copy-start | bytes 2752516
  26.8 139.2 %all-to-all-start.1 = ((bf16[16,2,128,896]{2,3,1,0:T(8,128)(2,1)}), bf16[16,2,128,896]{2,3,1,0:T(8,128)(2,1)}, u32[]{:S(2)}, u32[]{:S(2)}) async-start(bf16[16,2,128,896]{2,3,1,0:T(8,128)(2,1)} %broadcast_in_dim.94), calls=%async_computation.1 | async-start | bytes 14680064 | tf_op jit(solution)/shard_map/all_to_all | solution.py:70
  36.0 147.4 %copy-start.2 = (bf16[2,256,896]{2,1,0:T(8,128)(2,1)S(1)}, bf16[2,256,896]{2,1,0:T(8,128)(2,1)}, u32[]{:S(2)}) copy-start(bf16[2,256,896]{2,1,0:T(8,128)(2,1)} %param.10) | copy-start | bytes 2752516
  36.0 147.9 %copy-start.3 = (s32[1,64]{1,0:T(1,128)S(1)}, s32[1,64]{1,0:T(1,128)}, u32[]{:S(2)}) copy-start(s32[1,64]{1,0:T(1,128)} %param.11) | copy-start | bytes 772
  168.1 96.4 %all-to-all-start = ((bf16[64,256,112]{1,2,0:T(8,128)(2,1)}), bf16[64,256,112]{1,2,0:T(8,128)(2,1)}, u32[]{:S(2)}, u32[]{:S(2)}) async-start(bf16[64,256,112]{1,2,0:T(8,128)(2,1)} %bitcast.71), calls=%async_computation | async-start | bytes 7340032 | tf_op jit(solution)/shard_map/all_to_all | solution.py:44
  274.9 6.2 %copy-start = (bf16[2048,4,224]{0,2,1:T(8,128)(2,1)S(1)}, bf16[2048,4,224]{0,2,1:T(8,128)(2,1)}, u32[]{:S(2)}) copy-start(bf16[2048,4,224]{0,2,1:T(8,128)(2,1)} %reshape_squeeze.15) | copy-start | bytes 11010052
Sparse Core Ops, SparseCore 0:
  20.9 163.4 all-gather.1

commit v5 on v3

--- a/solution.py
+++ b/solution.py
@@ -30,16 +30,35 @@
     blk_size = lax.axis_size("blk")
     mp_size = lax.axis_size("mp")
     dp_size = lax.axis_size("dp")
-    quarter = lax.all_gather(trainer_q.astype(jnp.bfloat16), "blk", axis=0, tiled=True)
-    head_width, quarter_cols = quarter.shape
-    quarter = jnp.broadcast_to(quarter[None], (dp_size, head_width, quarter_cols))
-    quarters = lax.all_to_all(quarter, "dp", 0, 0, tiled=True)
+    g = lax.axis_index("dp")
+    b = lax.axis_index("blk")
+    core = b % 2
+    piece_rows, quarter_cols = trainer_q.shape
+    trainer_rows = lax.all_gather(trainer_q.astype(jnp.bfloat16), "dp", axis=1, tiled=True)
+    trainer_rows = trainer_rows.reshape(piece_rows, dp_size, quarter_cols)
+    chosen = jnp.stack(
+        [
+            lax.dynamic_index_in_dim(trainer_rows, g, 1, keepdims=False),
+            lax.dynamic_index_in_dim(trainer_rows, (g + 2) % dp_size, 1, keepdims=False),
+        ]
+    )
+    chosen = lax.all_gather(chosen, "blk", axis=1, tiled=True)
+    head_width = chosen.shape[1]
+    half_rows = head_width // 2
+    own_half = lax.dynamic_slice_in_dim(chosen[0], core * half_rows, half_rows, axis=0)
+    from_next = lax.ppermute(own_half, "dp", [(i, (i - 1) % dp_size) for i in range(dp_size)])
+    from_prev = lax.ppermute(own_half, "dp", [(i, (i + 1) % dp_size) for i in range(dp_size)])
+    fetched = jnp.stack([from_next, from_prev])
+    mate = lax.ppermute(fetched, "blk", [(i, i ^ 1) for i in range(blk_size)])
+    first = jnp.where(core == 0, fetched, mate)
+    second = jnp.where(core == 0, mate, fetched)
+    whole = jnp.concatenate([first, second], axis=1)
+    quarters = jnp.stack([chosen[0], whole[0], chosen[1], whole[1]])
     block_cols = quarter_cols * dp_size // blk_size
     blocks_per_quarter = quarter_cols // block_cols
-    b = lax.axis_index("blk")
     server_q = lax.dynamic_slice(
         quarters,
-        (b // blocks_per_quarter, 0, (b % blocks_per_quarter) * block_cols),
+        ((b // blocks_per_quarter - g) % dp_size, 0, (b % blocks_per_quarter) * block_cols),
         (1, head_width, block_cols),
     )[0]
     group_rows, piece_cols = tokens.shape
@@ -49,11 +68,11 @@
     pieces = pieces.reshape(blk_size * mp_size, own_rows, piece_cols)
     pieces = lax.all_to_all(pieces, ("blk", "mp"), 0, 0, tiled=True)
     token_local = jnp.transpose(pieces, (1, 0, 2)).reshape(own_rows, -1)
+    token_quarters = token_local.reshape(own_rows, dp_size, quarter_cols)
+    token_quarters = jnp.concatenate([token_quarters, token_quarters], axis=1)
+    token_quarters = lax.dynamic_slice_in_dim(token_quarters, g, dp_size, axis=1)
     queries = jnp.einsum(
-        "tgd,ghd->th",
-        token_local.reshape(own_rows, dp_size, quarter_cols),
-        quarters,
-        preferred_element_type=jnp.float32,
+        "tjd,jhd->th", token_quarters, quarters, preferred_element_type=jnp.float32
     )
     queries = queries.astype(jnp.bfloat16)
     head_count = head_width // HD

time: 333 us -> 259 us (0.78)
  waiting for transfers between devices: 242 us -> 133 us
  local copies, waits for them, and re-layouts: 32.6 us -> 49.7 us
  blocking collectives: 0 us -> 12.1 us
  other arithmetic: 4.59 us -> 11 us
    all_to_all x1 -> x0, waiting for transfers between devices: 141 us -> none  [body(): quarters = lax.all_to_all(quarter, 'dp', 0, 0, tiled=True)]
    all_to_all x1, waiting for transfers between devices: 58.6 us -> 0.01 us  [body(): pieces = lax.all_to_all(pieces, ('blk', 'mp'), 0, 0, tiled=True)]
    all_gather x1, waiting for transfers between devices: 42.2 us -> 97.2 us  [body(): chosen = lax.all_gather(chosen, 'blk', axis=1, tiled=True)]
    ppermute x0 -> x3, waiting for transfers between devices: none -> 35.6 us  [the longest x1 35 us: body(): lax.ppermute(own_half, 'dp', [(i, (i + 1) % dp_size) for i in range(dp_si...]
    all_gather x0 -> x1, blocking collectives: none -> 12.1 us  [body(): lax.all_gather(trainer_q.astype(jnp.bfloat16), 'dp', axis=1, tiled=True)]
    broadcast_in_dim x1 -> x0, local copies, waits for them, and re-layouts: 7.05 us -> none  [body(): jnp.broadcast_to(quarter[None], (dp_size, head_width, quarter_cols))]
    unnamed x9 -> x19, local copies, waits for them, and re-layouts: 1 us -> 7.72 us
    all_to_all x1 -> x0, starting transfers between devices: 6.48 us -> none  [body(): quarters = lax.all_to_all(quarter, 'dp', 0, 0, tiled=True)]
  transfers between devices with their start and end apart: 4 -> 6, of which waited for: 3 -> 3; matrix products, arithmetic and copies ran while one was open for 7% -> 16% of each run, Pallas kernels for 0% -> 0%
where the time goes in v5:
time: 259 us; the launch traced here: 256 us
  waiting for transfers between devices  133 us (51%)
  local copies, waits for them, and re-layouts  49.7 us (19%)
  starting transfers between devices  17.9 us (7%)
  matrix products  16.5 us (6%)
  between operations  15.6 us (6%)
  blocking collectives  12.1 us (5%)
  other arithmetic  11 us (4%)
    all_gather x1, waiting for transfers between devices, body(): chosen = lax.all_gather(chosen, 'blk', axis=1, tiled=True)  97.2 us
    ppermute x1, waiting for transfers between devices, body(): lax.ppermute(own_half, 'dp', [(i, (i + 1) % dp_size) for i in range(dp_si...  35 us
    all_to_all x1, starting transfers between devices, body(): pieces = lax.all_to_all(pieces, ('blk', 'mp'), 0, 0, tiled=True)  14 us
    slice x2, local copies, waits for them, and re-layouts, body(): shard_piece[0].reshape(key_count, head_count, HD)  13 us
    all_gather x1, blocking collectives, body(): lax.all_gather(trainer_q.astype(jnp.bfloat16), 'dp', axis=1, tiled=True)  12.1 us
    dot_general x1, matrix products, body(): jnp.einsum('tjd,jhd->th', token_quarters, quarters, preferred_element_typ...  9.74 us
    unnamed x19, local copies, waits for them, and re-layouts  7.72 us
    slice x1, local copies, waits for them, and re-layouts, body(): shard_piece[1].reshape(key_count, head_count, HD)  6.18 us
  transfers between devices with their start and end apart: 6, of which 3 were waited for; matrix products, arithmetic and copies ran while one was open for 16% of the time, Pallas kernels for 0%

profile of v5, /device:TPU:25, one launch (start us, length us, event | category | flops | bytes accessed | tf_op | source)
XLA Modules:
  0.0 256.3 jit_solution(112774894130883437)
XLA Ops:
  7.2 0.0 copy-start.6
  7.2 0.0 all-gather.3.cloned.1.call-start
  7.2 1.1 convert_element_type.18
  8.3 12.1 %all_gather.9 = bf16[56,7168]{1,0:T(8,128)(2,1)S(1)} all-gather(bf16[56,1792]{1,0:T(8,128)(2,1)S(1)} %convert_element_type.18), channel_id=1, replica_groups=mesh['dp'=4,'blk'=16,'mp'=4] {'dp'}, dimensions={1}, use_global_device_ids=true | all-gather | bytes 1003520 | tf_op jit(solution)/shard_map/all_gather | solution.py:37
  20.5 0.6 reshape.103
  21.1 0.8 constant_dynamic-slice_fusion.2
  21.9 0.1 copy_bitcast_fusion.1
  22.0 0.8 pad_maximum_fusion.1
  22.8 0.0 all-gather.3.cloned.1.call-update
  22.8 0.0 all-gather.5.cloned.1.call-start
  22.8 0.7 all-gather.5.cloned.1.call-update
  23.5 0.0 copy-done.6
  23.6 0.1 copy.53
  23.6 2.1 broadcast_in_dim.82
  25.7 14.0 %all-to-all-start = ((bf16[64,256,112]{1,2,0:T(8,128)(2,1)}), bf16[64,256,112]{1,2,0:T(8,128)(2,1)}, u32[]{:S(2)}, u32[]{:S(2)}) async-start(bf16[64,256,112]{1,2,0:T(8,128)(2,1)} %bitcast.76), calls=%async_computation | async-start | bytes 7340032 | tf_op jit(solution)/shard_map/all_to_all | solution.py:69
  39.7 97.2 %all-gather.3.cloned.1.call-done = bf16[2,896,1792]{2,1,0:T(8,128)(2,1)} async-done(((bf16[2,56,1792]{2,1,0:T(8,128)(2,1)}), bf16[2,896,1792]{2,1,0:T(8,128)(2,1)}) %all-gather.3.cloned.1.call-update) | async-done | bytes 6422544 | tf_op jit(solution)/shard_map/all_gather | solution.py:45
  136.9 5.0 %fusion.53 = (bf16[1,896,1792]{2,1,0:T(8,128)(2,1)}, bf16[1,896,1792]{2,1,0:T(8,128)(2,1)S(1)}) fusion(bf16[2,896,1792]{2,1,0:T(8,128)(2,1)} %all-gather.3.cloned.1.call-done), kind=kLoop, calls=%fused_computation.77 | loop fusion | bytes 12845056 | tf_op jit(solution)/shard_map/slice | solution.py:56
  141.9 0.0 copy-start.8
  141.9 0.1 dynamic-slice_bitcast_fusion
  142.0 0.6 collective-permute-start.1
  142.6 2.2 collective-permute-start
  144.8 35.0 %collective-permute-done.1 = bf16[448,1792]{1,0:T(8,128)(2,1)S(1)} collective-permute-done((bf16[448,1792]{1,0:T(8,128)(2,1)S(1)}, bf16[448,1792]{1,0:T(8,128)(2,1)S(1)}, u32[]{:S(2)}, u32[]{:S(2)}) %collective-permute-start.1) | collective-permute-done | bytes 1605664 | tf_op jit(solution)/shard_map/ppermute | solution.py:50
  179.7 0.0 copy-start.2
  179.7 0.6 collective-permute-done
  180.3 0.0 copy-start.3
  180.3 0.6 copy-done.2
  180.9 1.9 pad_maximum_fusion
  182.8 0.0 copy-done.3
  182.8 1.1 collective-permute-start.2
  184.6 2.2 fusion.54
  186.7 2.0 copy.40
  189.4 2.0 copy.41
  191.4 0.0 copy-done.8
  191.4 0.2 and_reduce_fusion
  191.6 0.1 fusion.36
  191.7 0.0 all-to-all-done
  191.7 6.0 %copy.37 = bf16[256,4,1792]{2,0,1:T(8,128)(2,1)} copy(bf16[256,4,1792]{0,2,1:T(8,128)(2,1)} %bitcast.9) | data formatting | bytes 7340032 | tf_op jit(solution)/shard_map/reshape;reshape | solution.py:71
  197.7 6.9 %fusion.52 = (bf16[1,2048,896]{2,1,0:T(8,128)(2,1)}, bf16[1,2048,896]{2,1,0:T(8,128)(2,1)}) fusion(bf16[2,2048,896]{2,1,0:T(8,128)(2,1)} %all-gather.5.cloned.1.call-done), kind=kLoop, calls=%fused_computation.76 | loop fusion | bytes 14680064 | tf_op jit(solution)/shard_map/slice | solution.py:105
  204.6 6.2 %copy.44 = bf16[1,2048,896]{1,2,0:T(8,128)(2,1)} copy(bf16[1,2048,896]{2,1,0:T(8,128)(2,1)} %get-tuple-element.11) | data formatting | bytes 7340032 | tf_op jit(solution)/shard_map/slice | solution.py:106
  210.8 6.1 %copy.43 = bf16[1,2048,896]{1,2,0:T(8,128)(2,1)} copy(bf16[1,2048,896]{2,1,0:T(8,128)(2,1)} %get-tuple-element.10) | data formatting | bytes 7340032 | tf_op jit(solution)/shard_map/slice | solution.py:105
  216.9 0.0 collective-permute-done.2
  216.9 3.1 %broadcast_select_fusion.1 = (bf16[2,448,1792]{2,1,0:T(8,128)(2,1)S(1)}, bf16[2,448,1792]{2,1,0:T(8,128)(2,1)S(1)}) fusion(bf16[2,448,1792]{2,1,0:T(8,128)(2,1)} %collective-permute-done.2, pred[]{:T(512)S(6)} %eq.24, bf16[1,448,1792]{2,1,0:T(8,128)(2,1)} %bitcast.79, bf16[1,448,1792]{2,1,0:T(8,128)(2,1)} %bitcast.81), kind=kLoop, calls=%fused_computation.21 | loop fusion | flops 4816896 | bytes 12845057 | tf_op jit(solution)/shard_map/jit(_where)/select_n | solution.py:53
  220.0 0.0 copy-start.1
  220.0 0.3 fusion.13
  220.3 1.6 copy-done.1
  221.9 0.9 fusion.3
  222.8 0.0 copy-start
  222.8 4.6 %copy-done = bf16[4,896,1792]{2,1,0:T(8,128)(2,1)} copy-done((bf16[4,896,1792]{2,1,0:T(8,128)(2,1)}, bf16[4,896,1792]{2,1,0:T(8,128)(2,1)S(1)}, u32[]{:S(2)}) %copy-start) | copy-done | bytes 12845080
  227.4 0.4 constant_dynamic-slice_fusion
  227.8 1.2 copy.35
  229.0 9.7 %fusion.26 = bf16[256,896]{1,0:T(8,128)(2,1)S(1)} fusion(bf16[4,896,1792]{2,1,0:T(8,128)(2,1)} %copy-done, s32[]{:T(128)S(6)} %select_n.95, bf16[256,4,1792]{2,0,1:T(8,128)(2,1)} %copy.37), kind=kOutput, calls=%fused_computation.33 | convolution fusion | flops 3290398720 | bytes 16973828 | tf_op jit(solution)/shard_map/tjd,jhd->th/dot_general | solution.py:74
  238.8 0.2 copy.39
  239.0 0.0 copy-start.5
  239.0 3.9 %fusion.4 = (f32[4,256]{1,0:T(4,128)S(1)}, f32[4,256,2048]{2,1,0:T(8,128)S(1)}) fusion(pred[2048]{0:T(1024)(128)(4,1)S(1)} %and_reduce_fusion, bf16[256,4,224]{0,2,1:T(8,128)(2,1)S(1)} %bitcast.82, bf16[2048,4,224]{0,2,1:T(8,128)(2,1)} %bitcast.77), kind=kOutput, calls=%fused_computation.7 | convolution fusion | flops 945814528 | bytes 12523520 | tf_op jit(solution)/shard_map/thd,khd->htk/dot_general | solution.py:12
  242.9 0.0 copy-done.5
  242.9 0.4 fusion.55
  243.3 2.4 fusion.5
  245.7 0.0 copy-done.4
  245.7 0.0 copy-start.7
  245.7 2.1 fusion.18
  247.9 0.2 fusion.30
  248.1 0.0 copy-done.7
  248.1 0.4 fusion.29
  248.5 1.0 copy.45
  (7 shorter events, 0.0 us)
Async XLA Ops:
  7.2 16.4 %copy-start.6 = (bf16[4096,112]{0,1:T(8,128)(2,1)S(1)}, bf16[4096,112]{0,1:T(8,128)(2,1)}, u32[]{:S(2)}) copy-start(bf16[4096,112]{0,1:T(8,128)(2,1)} %param.7) | copy-start | bytes 2752516
  7.2 129.7 %all-gather.3.cloned.1.call-start = ((), (), s32[]{:S(2)}) async-start(), calls=%async_computation.1 | async-start | bytes 6823936 | tf_op jit(solution)/shard_map/all_gather | solution.py:45
  22.8 174.9 %all-gather.5.cloned.1.call-start = ((), (), s32[]{:S(2)}) async-start(), calls=%async_computation.2 | async-start | bytes 7798784 | tf_op jit(solution)/shard_map/all_gather | solution.py:97
  25.7 166.0 %all-to-all-start = ((bf16[64,256,112]{1,2,0:T(8,128)(2,1)}), bf16[64,256,112]{1,2,0:T(8,128)(2,1)}, u32[]{:S(2)}, u32[]{:S(2)}) async-start(bf16[64,256,112]{1,2,0:T(8,128)(2,1)} %bitcast.76), calls=%async_computation | async-start | bytes 7340032 | tf_op jit(solution)/shard_map/all_to_all | solution.py:69
  141.9 49.5 %copy-start.8 = (s32[1,64]{1,0:T(1,128)S(1)}, s32[1,64]{1,0:T(1,128)}, u32[]{:S(2)}) copy-start(s32[1,64]{1,0:T(1,128)} %param.11) | copy-start | bytes 772
  142.0 37.7 %collective-permute-start.1 = (bf16[448,1792]{1,0:T(8,128)(2,1)S(1)}, bf16[448,1792]{1,0:T(8,128)(2,1)S(1)}, u32[]{:S(2)}, u32[]{:S(2)}) collective-permute-start(bf16[448,1792]{1,0:T(8,128)(2,1)S(1)} %dynamic-slice_bitcast_fusion), channel_id=1, source_target_pairs={{0,64},{64,128},{128,192},{192,0},{1,65},{65,129},{129,193},{193,1... | collective-permute-start | bytes 4816904 | tf_op jit(solution)/shard_map/ppermute | solution.py:50
  142.6 37.8 %collective-permute-start = (bf16[448,1792]{1,0:T(8,128)(2,1)S(1)}, bf16[448,1792]{1,0:T(8,128)(2,1)S(1)}, u32[]{:S(2)}, u32[]{:S(2)}) collective-permute-start(bf16[448,1792]{1,0:T(8,128)(2,1)S(1)} %dynamic-slice_bitcast_fusion), channel_id=1, source_target_pairs={{0,192},{64,0},{128,64},{192,128},{1,193},{65,1},{129,65},{193,129... | collective-permute-start | bytes 4816904 | tf_op jit(solution)/shard_map/ppermute | solution.py:49
  179.7 1.2 copy-start.2
  180.3 2.5 copy-start.3
  182.8 34.1 %collective-permute-start.2 = (bf16[2,448,1792]{2,1,0:T(8,128)(2,1)}, bf16[2,448,1792]{2,1,0:T(8,128)(2,1)}, u32[]{:S(2)}, u32[]{:S(2)}) collective-permute-start(bf16[2,448,1792]{2,1,0:T(8,128)(2,1)} %pad_maximum_fusion), channel_id=1, source_target_pairs={{0,4},{4,0},{8,12},{12,8},{16,20},{20,16},{24,28},{28,24},{32,36},... | collective-permute-start | bytes 9633800 | tf_op jit(solution)/shard_map/ppermute | solution.py:52
  220.0 1.9 copy-start.1
  222.8 4.6 %copy-start = (bf16[4,896,1792]{2,1,0:T(8,128)(2,1)}, bf16[4,896,1792]{2,1,0:T(8,128)(2,1)S(1)}, u32[]{:S(2)}) copy-start(bf16[4,896,1792]{2,1,0:T(8,128)(2,1)S(1)} %fusion.3) | copy-start | bytes 38535172
  239.0 3.9 %copy-start.5 = (bf16[1,256,896]{1,2,0:T(8,128)(2,1)S(1)}, bf16[1,256,896]{1,2,0:T(8,128)(2,1)}, u32[]{:S(2)}) copy-start(bf16[1,256,896]{1,2,0:T(8,128)(2,1)} %copy.40) | copy-start | bytes 1376260
  242.9 2.8 %copy-start.4 = (bf16[1,2048,896]{1,2,0:T(8,128)(2,1)S(1)}, bf16[1,2048,896]{1,2,0:T(8,128)(2,1)}, u32[]{:S(2)}) copy-start(bf16[1,2048,896]{1,2,0:T(8,128)(2,1)} %copy.44) | copy-start | bytes 11010052
  245.7 2.4 copy-start.7
Sparse Core Ops, SparseCore 0:
  22.9 113.9 all-gather.2
  138.7 51.3 all-gather.4

commit v6 on v5

--- a/solution.py
+++ b/solution.py
@@ -36,14 +36,16 @@
     piece_rows, quarter_cols = trainer_q.shape
     trainer_rows = lax.all_gather(trainer_q.astype(jnp.bfloat16), "dp", axis=1, tiled=True)
     trainer_rows = trainer_rows.reshape(piece_rows, dp_size, quarter_cols)
-    chosen = jnp.stack(
+    chosen = jnp.concatenate(
         [
             lax.dynamic_index_in_dim(trainer_rows, g, 1, keepdims=False),
             lax.dynamic_index_in_dim(trainer_rows, (g + 2) % dp_size, 1, keepdims=False),
-        ]
+        ],
+        axis=1,
     )
-    chosen = lax.all_gather(chosen, "blk", axis=1, tiled=True)
-    head_width = chosen.shape[1]
+    chosen = lax.all_gather(chosen, "blk", axis=0, tiled=True)
+    chosen = (chosen[:, :quarter_cols], chosen[:, quarter_cols:])
+    head_width = chosen[0].shape[0]
     half_rows = head_width // 2
     own_half = lax.dynamic_slice_in_dim(chosen[0], core * half_rows, half_rows, axis=0)
     from_next = lax.ppermute(own_half, "dp", [(i, (i - 1) % dp_size) for i in range(dp_size)])

time: 259 us -> 258 us (level)
    slice x1 -> x0, local copies, waits for them, and re-layouts: 5.02 us -> none  [body(): quarters = jnp.stack([chosen[0], whole[0], chosen[1], whole[1]])]
    another operation x1, local copies, waits for them, and re-layouts: 0.06 us -> 4.36 us  [body(): quarters = jnp.stack([chosen[0], whole[0], chosen[1], whole[1]])]
where the time goes in v6:
time: 258 us; the launch traced here: 256 us
  waiting for transfers between devices  133 us (52%)
  local copies, waits for them, and re-layouts  49 us (19%)
  starting transfers between devices  17.9 us (7%)
  matrix products  16.5 us (6%)
  between operations  15.6 us (6%)
  blocking collectives  12.1 us (5%)
  other arithmetic  11 us (4%)
    all_gather x1, waiting for transfers between devices, body(): chosen = lax.all_gather(chosen, 'blk', axis=0, tiled=True)  97.2 us
    ppermute x1, waiting for transfers between devices, body(): lax.ppermute(own_half, 'dp', [(i, (i + 1) % dp_size) for i in range(dp_si...  35 us
    all_to_all x1, starting transfers between devices, body(): pieces = lax.all_to_all(pieces, ('blk', 'mp'), 0, 0, tiled=True)  14 us
    slice x2, local copies, waits for them, and re-layouts, body(): shard_piece[0].reshape(key_count, head_count, HD)  13 us
    all_gather x1, blocking collectives, body(): lax.all_gather(trainer_q.astype(jnp.bfloat16), 'dp', axis=1, tiled=True)  12.1 us
    dot_general x1, matrix products, body(): jnp.einsum('tjd,jhd->th', token_quarters, quarters, preferred_element_typ...  9.75 us
    unnamed x19, local copies, waits for them, and re-layouts  7.72 us
    slice x1, local copies, waits for them, and re-layouts, body(): shard_piece[1].reshape(key_count, head_count, HD)  6.18 us
  transfers between devices with their start and end apart: 6, of which 3 were waited for; matrix products, arithmetic and copies ran while one was open for 16% of the time, Pallas kernels for 0%

profile of v6, /device:TPU:25, one launch (start us, length us, event | category | flops | bytes accessed | tf_op | source)
XLA Modules:
  0.0 255.6 jit_solution(6040250716486522846)
XLA Ops:
  7.2 0.0 copy-start.6
  7.2 0.0 all-gather.3.cloned.1.call-start
  7.2 1.1 convert_element_type.18
  8.3 12.1 %all_gather.9 = bf16[56,7168]{1,0:T(8,128)(2,1)S(1)} all-gather(bf16[56,1792]{1,0:T(8,128)(2,1)S(1)} %convert_element_type.18), channel_id=1, replica_groups=mesh['dp'=4,'blk'=16,'mp'=4] {'dp'}, dimensions={1}, use_global_device_ids=true | all-gather | bytes 1003520 | tf_op jit(solution)/shard_map/all_gather | solution.py:37
  20.5 0.6 reshape.100
  21.1 0.8 constant_dynamic-slice_fusion.3
  21.9 0.1 copy_bitcast_fusion.1
  22.0 0.8 pad_maximum_fusion.1
  22.8 0.0 all-gather.3.cloned.1.call-update
  22.8 0.0 all-gather.5.cloned.1.call-start
  22.8 0.7 all-gather.5.cloned.1.call-update
  23.5 0.0 copy-done.6
  23.5 0.1 copy.53
  23.6 2.1 broadcast_in_dim.82
  25.7 14.0 %all-to-all-start = ((bf16[64,256,112]{1,2,0:T(8,128)(2,1)}), bf16[64,256,112]{1,2,0:T(8,128)(2,1)}, u32[]{:S(2)}, u32[]{:S(2)}) async-start(bf16[64,256,112]{1,2,0:T(8,128)(2,1)} %bitcast.78), calls=%async_computation | async-start | bytes 7340032 | tf_op jit(solution)/shard_map/all_to_all | solution.py:71
  39.7 97.2 %all-gather.3.cloned.1.call-done = bf16[896,3584]{1,0:T(8,128)(2,1)} async-done(((bf16[56,3584]{1,0:T(8,128)(2,1)}), bf16[896,3584]{1,0:T(8,128)(2,1)}) %all-gather.3.cloned.1.call-update) | async-done | bytes 6422544 | tf_op jit(solution)/shard_map/all_gather | solution.py:46
  136.9 4.4 %slice_bitcast_fusion.1 = (bf16[1,896,1792]{2,1,0:T(8,128)(2,1)S(1)}, bf16[1,896,1792]{2,1,0:T(8,128)(2,1)}, bf16[896,1792]{1,0:T(8,128)(2,1)S(1)}) fusion(bf16[896,3584]{1,0:T(8,128)(2,1)} %all-gather.3.cloned.1.call-done), kind=kLoop, calls=%fused_computation.77 | loop fusion | bytes 16056320 | tf_op jit(solution)/shard_map/stack | solution.py:58
  141.2 0.1 constant_dynamic-slice_fusion.1
  141.3 0.6 collective-permute-start.1
  141.9 2.2 collective-permute-start
  144.1 35.0 %collective-permute-done.1 = bf16[448,1792]{1,0:T(8,128)(2,1)S(1)} collective-permute-done((bf16[448,1792]{1,0:T(8,128)(2,1)S(1)}, bf16[448,1792]{1,0:T(8,128)(2,1)S(1)}, u32[]{:S(2)}, u32[]{:S(2)}) %collective-permute-start.1) | collective-permute-done | bytes 1605664 | tf_op jit(solution)/shard_map/ppermute | solution.py:52
  179.0 0.0 copy-start.2
  179.0 0.6 collective-permute-done
  179.7 0.0 copy-start.3
  179.7 0.6 copy-done.2
  180.2 1.9 pad_maximum_fusion
  182.1 0.0 copy-done.3
  182.1 1.1 collective-permute-start.2
  183.9 2.2 fusion.53
  186.0 2.0 copy.40
  188.7 2.0 copy.41
  190.7 0.0 copy-done.8
  190.7 0.2 and_reduce_fusion
  190.9 0.1 fusion.36
  191.0 0.0 all-to-all-done
  191.0 6.0 %copy.37 = bf16[256,4,1792]{2,0,1:T(8,128)(2,1)} copy(bf16[256,4,1792]{0,2,1:T(8,128)(2,1)} %bitcast.10) | data formatting | bytes 7340032 | tf_op jit(solution)/shard_map/reshape;reshape | solution.py:73
  197.0 6.9 %fusion.52 = (bf16[1,2048,896]{2,1,0:T(8,128)(2,1)}, bf16[1,2048,896]{2,1,0:T(8,128)(2,1)}) fusion(bf16[2,2048,896]{2,1,0:T(8,128)(2,1)} %all-gather.5.cloned.1.call-done), kind=kLoop, calls=%fused_computation.78 | loop fusion | bytes 14680064 | tf_op jit(solution)/shard_map/slice | solution.py:107
  203.9 6.2 %copy.44 = bf16[1,2048,896]{1,2,0:T(8,128)(2,1)} copy(bf16[1,2048,896]{2,1,0:T(8,128)(2,1)} %get-tuple-element.11) | data formatting | bytes 7340032 | tf_op jit(solution)/shard_map/slice | solution.py:108
  210.1 6.1 %copy.43 = bf16[1,2048,896]{1,2,0:T(8,128)(2,1)} copy(bf16[1,2048,896]{2,1,0:T(8,128)(2,1)} %get-tuple-element.10) | data formatting | bytes 7340032 | tf_op jit(solution)/shard_map/slice | solution.py:107
  216.2 0.0 collective-permute-done.2
  216.2 3.1 %broadcast_select_fusion.1 = (bf16[2,448,1792]{2,1,0:T(8,128)(2,1)S(1)}, bf16[2,448,1792]{2,1,0:T(8,128)(2,1)S(1)}) fusion(bf16[2,448,1792]{2,1,0:T(8,128)(2,1)} %collective-permute-done.2, pred[]{:T(512)S(6)} %eq.24, bf16[1,448,1792]{2,1,0:T(8,128)(2,1)} %bitcast.81, bf16[1,448,1792]{2,1,0:T(8,128)(2,1)} %bitcast.83), kind=kLoop, calls=%fused_computation.22 | loop fusion | flops 4816896 | bytes 12845057 | tf_op jit(solution)/shard_map/jit(_where)/select_n | solution.py:55
  219.3 0.0 copy-start.1
  219.3 0.3 fusion.13
  219.6 1.6 copy-done.1
  221.2 0.9 fusion.3
  222.1 0.0 copy-start
  222.1 4.6 %copy-done = bf16[4,896,1792]{2,1,0:T(8,128)(2,1)} copy-done((bf16[4,896,1792]{2,1,0:T(8,128)(2,1)}, bf16[4,896,1792]{2,1,0:T(8,128)(2,1)S(1)}, u32[]{:S(2)}) %copy-start) | copy-done | bytes 12845080
  226.7 0.4 constant_dynamic-slice_fusion
  227.1 1.2 copy.35
  228.3 9.7 %fusion.26 = bf16[256,896]{1,0:T(8,128)(2,1)S(1)} fusion(bf16[4,896,1792]{2,1,0:T(8,128)(2,1)} %copy-done, s32[]{:T(128)S(6)} %select_n.95, bf16[256,4,1792]{2,0,1:T(8,128)(2,1)} %copy.37), kind=kOutput, calls=%fused_computation.33 | convolution fusion | flops 3290398720 | bytes 16973828 | tf_op jit(solution)/shard_map/tjd,jhd->th/dot_general | solution.py:76
  238.1 0.2 copy.39
  238.3 0.0 copy-start.5
  238.3 3.9 %fusion.4 = (f32[4,256]{1,0:T(4,128)S(1)}, f32[4,256,2048]{2,1,0:T(8,128)S(1)}) fusion(pred[2048]{0:T(1024)(128)(4,1)S(1)} %and_reduce_fusion, bf16[256,4,224]{0,2,1:T(8,128)(2,1)S(1)} %bitcast.84, bf16[2048,4,224]{0,2,1:T(8,128)(2,1)} %bitcast.79), kind=kOutput, calls=%fused_computation.7 | convolution fusion | flops 945814528 | bytes 12523520 | tf_op jit(solution)/shard_map/thd,khd->htk/dot_general | solution.py:12
  242.2 0.0 copy-done.5
  242.2 0.4 fusion.54
  242.6 0.0 copy-start.4
  242.6 2.4 fusion.5
  245.0 0.0 copy-done.4
  245.0 0.0 copy-start.7
  245.0 2.1 fusion.18
  247.2 0.2 fusion.30
  247.4 0.0 copy-done.7
  247.4 0.4 fusion.29
  247.8 1.0 copy.45
  (7 shorter events, 0.0 us)
Async XLA Ops:
  7.2 16.4 %copy-start.6 = (bf16[4096,112]{0,1:T(8,128)(2,1)S(1)}, bf16[4096,112]{0,1:T(8,128)(2,1)}, u32[]{:S(2)}) copy-start(bf16[4096,112]{0,1:T(8,128)(2,1)} %param.7) | copy-start | bytes 2752516
  7.2 129.7 %all-gather.3.cloned.1.call-start = ((), (), s32[]{:S(2)}) async-start(), calls=%async_computation.1 | async-start | bytes 6823936 | tf_op jit(solution)/shard_map/all_gather | solution.py:46
  22.8 174.2 %all-gather.5.cloned.1.call-start = ((), (), s32[]{:S(2)}) async-start(), calls=%async_computation.2 | async-start | bytes 7798784 | tf_op jit(solution)/shard_map/all_gather | solution.py:99
  25.7 165.3 %all-to-all-start = ((bf16[64,256,112]{1,2,0:T(8,128)(2,1)}), bf16[64,256,112]{1,2,0:T(8,128)(2,1)}, u32[]{:S(2)}, u32[]{:S(2)}) async-start(bf16[64,256,112]{1,2,0:T(8,128)(2,1)} %bitcast.78), calls=%async_computation | async-start | bytes 7340032 | tf_op jit(solution)/shard_map/all_to_all | solution.py:71
  141.3 37.7 %collective-permute-start.1 = (bf16[448,1792]{1,0:T(8,128)(2,1)S(1)}, bf16[448,1792]{1,0:T(8,128)(2,1)S(1)}, u32[]{:S(2)}, u32[]{:S(2)}) collective-permute-start(bf16[448,1792]{1,0:T(8,128)(2,1)S(1)} %constant_dynamic-slice_fusion.1), channel_id=1, source_target_pairs={{0,64},{64,128},{128,192},{192,0},{1,65},{65,129},{129,193},{193,1... | collective-permute-start | bytes 4816904 | tf_op jit(solution)/shard_map/ppermute | solution.py:52
  141.9 37.8 %collective-permute-start = (bf16[448,1792]{1,0:T(8,128)(2,1)S(1)}, bf16[448,1792]{1,0:T(8,128)(2,1)S(1)}, u32[]{:S(2)}, u32[]{:S(2)}) collective-permute-start(bf16[448,1792]{1,0:T(8,128)(2,1)S(1)} %constant_dynamic-slice_fusion.1), channel_id=1, source_target_pairs={{0,192},{64,0},{128,64},{192,128},{1,193},{65,1},{129,65},{193,129... | collective-permute-start | bytes 4816904 | tf_op jit(solution)/shard_map/ppermute | solution.py:51
  179.0 1.2 copy-start.2
  179.7 2.5 copy-start.3
  180.2 10.5 %copy-start.8 = (s32[1,64]{1,0:T(1,128)S(1)}, s32[1,64]{1,0:T(1,128)}, u32[]{:S(2)}) copy-start(s32[1,64]{1,0:T(1,128)} %param.11) | copy-start | bytes 772
  182.1 34.1 %collective-permute-start.2 = (bf16[2,448,1792]{2,1,0:T(8,128)(2,1)}, bf16[2,448,1792]{2,1,0:T(8,128)(2,1)}, u32[]{:S(2)}, u32[]{:S(2)}) collective-permute-start(bf16[2,448,1792]{2,1,0:T(8,128)(2,1)} %pad_maximum_fusion), channel_id=1, source_target_pairs={{0,4},{4,0},{8,12},{12,8},{16,20},{20,16},{24,28},{28,24},{32,36},... | collective-permute-start | bytes 9633800 | tf_op jit(solution)/shard_map/ppermute | solution.py:54
  219.3 1.9 copy-start.1
  222.1 4.6 %copy-start = (bf16[4,896,1792]{2,1,0:T(8,128)(2,1)}, bf16[4,896,1792]{2,1,0:T(8,128)(2,1)S(1)}, u32[]{:S(2)}) copy-start(bf16[4,896,1792]{2,1,0:T(8,128)(2,1)S(1)} %fusion.3) | copy-start | bytes 38535172
  238.3 3.9 %copy-start.5 = (bf16[1,256,896]{1,2,0:T(8,128)(2,1)S(1)}, bf16[1,256,896]{1,2,0:T(8,128)(2,1)}, u32[]{:S(2)}) copy-start(bf16[1,256,896]{1,2,0:T(8,128)(2,1)} %copy.40) | copy-start | bytes 1376260
  242.6 2.4 copy-start.4
  245.0 2.4 copy-start.7
Sparse Core Ops, SparseCore 0:
  22.9 113.9 all-gather.2
  138.7 50.8 all-gather.4

commit v7 on v1

--- a/solution.py
+++ b/solution.py
@@ -38,11 +38,11 @@
     )
     group_rows, piece_cols = tokens.shape
     own_rows = group_rows // blk_size
-    pieces = tokens.reshape(blk_size, 1, own_rows, piece_cols)
-    pieces = jnp.broadcast_to(pieces, (blk_size, mp_size, own_rows, piece_cols))
-    pieces = pieces.reshape(blk_size * mp_size, own_rows, piece_cols)
-    pieces = lax.all_to_all(pieces, ("blk", "mp"), 0, 0, tiled=True)
-    token_local = jnp.transpose(pieces, (1, 0, 2)).reshape(own_rows, -1)
+    pieces = tokens.reshape(blk_size, own_rows, piece_cols)
+    pieces = lax.all_to_all(pieces, "blk", 0, 0, tiled=True)
+    pieces = jnp.broadcast_to(pieces[None], (mp_size, blk_size, own_rows, piece_cols))
+    pieces = lax.all_to_all(pieces, "mp", 0, 0, tiled=True)
+    token_local = jnp.transpose(pieces, (2, 1, 0, 3)).reshape(own_rows, -1)
     queries = jnp.einsum(
         "td,hd->th", token_local, head_weights, preferred_element_type=jnp.float32
     )

time: 234 us -> 244 us (1.043)
  blocking collectives: 12.5 us -> 42.6 us
  waiting for transfers between devices: 142 us -> 124 us
  starting transfers between devices: 14.4 us -> 7.13 us
  local copies, waits for them, and re-layouts: 27.1 us -> 31.9 us
    all_to_all x1, waiting for transfers between devices: 0.01 us -> 102 us  [body(): pieces = lax.all_to_all(pieces, 'mp', 0, 0, tiled=True)]
    all_gather x1, waiting for transfers between devices: 69.7 us -> 0.01 us  [body(): shard_piece = lax.all_gather(kv_pool, 'blk', axis=1, tiled=True)]
    all_gather x1, waiting for transfers between devices: 71.3 us -> 20.8 us  [body(): head_weights = lax.all_gather(trainer_rows, 'blk', axis=0, tiled=True)]
    all_to_all x0 -> x1, blocking collectives: none -> 30 us  [body(): pieces = lax.all_to_all(pieces, 'blk', 0, 0, tiled=True)]
    all_to_all x1, starting transfers between devices: 14.3 us -> 7.05 us  [body(): pieces = lax.all_to_all(pieces, 'mp', 0, 0, tiled=True)]
    all_to_all x0 -> x1, local copies, waits for them, and re-layouts: none -> 4.44 us  [body(): pieces = lax.all_to_all(pieces, 'mp', 0, 0, tiled=True)]
where the time goes in v7:
time: 244 us; the launch traced here: 242 us
  waiting for transfers between devices  124 us (51%)
  blocking collectives  42.6 us (17%)
  local copies, waits for them, and re-layouts  31.9 us (13%)
  matrix products  16.7 us (7%)
  between operations  15.5 us (6%)
  starting transfers between devices  7.13 us (3%)
  other arithmetic  3.91 us (2%)
    all_to_all x1, waiting for transfers between devices, body(): pieces = lax.all_to_all(pieces, 'mp', 0, 0, tiled=True)  102 us
    all_to_all x1, blocking collectives, body(): pieces = lax.all_to_all(pieces, 'blk', 0, 0, tiled=True)  30 us
    all_gather x1, waiting for transfers between devices, body(): head_weights = lax.all_gather(trainer_rows, 'blk', axis=0, tiled=True)  20.8 us
    slice x2, local copies, waits for them, and re-layouts, body(): shard_piece[0].reshape(key_count, head_count, HD)  13.2 us
    all_gather x1, blocking collectives, body(): lax.all_gather(trainer_q.astype(jnp.bfloat16), 'dp', axis=1, tiled=True)  12.5 us
    dot_general x1, matrix products, body(): jnp.einsum('td,hd->th', token_local, head_weights, preferred_element_type...  9.78 us
    all_to_all x1, starting transfers between devices, body(): pieces = lax.all_to_all(pieces, 'mp', 0, 0, tiled=True)  7.05 us
    slice x1, local copies, waits for them, and re-layouts, body(): shard_piece[1].reshape(key_count, head_count, HD)  6.24 us
  transfers between devices with their start and end apart: 3, of which 2 were waited for; matrix products, arithmetic and copies ran while one was open for 12% of the time, Pallas kernels for 0%

profile of v7, /device:TPU:25, one launch (start us, length us, event | category | flops | bytes accessed | tf_op | source)
XLA Modules:
  0.0 241.7 jit_solution(1538727552209562522)
XLA Ops:
  7.2 0.0 all-gather.5.cloned.1.call-start
  7.2 0.7 all-gather.5.cloned.1.call-update
  7.9 0.0 all-gather.3.cloned.1.call-start
  7.9 1.0 convert_element_type.18
  9.0 12.5 %all_gather.9 = bf16[56,7168]{1,0:T(8,128)(2,1)} all-gather(bf16[56,1792]{1,0:T(8,128)(2,1)S(1)} %convert_element_type.18), channel_id=1, replica_groups=mesh['dp'=4,'blk'=16,'mp'=4] {'dp'}, dimensions={1}, use_global_device_ids=true | all-gather | bytes 1003520 | tf_op jit(solution)/shard_map/all_gather | solution.py:32
  21.5 0.0 copy-start.1
  21.5 0.0 all-gather.3.cloned.1.call-update
  21.5 1.3 copy.51
  22.9 0.0 copy-start.2
  22.9 30.0 %all_to_all.10 = bf16[16,256,112]{1,2,0:T(8,128)(2,1)S(1)} all-to-all(bf16[16,256,112]{1,2,0:T(8,128)(2,1)S(1)} %bitcast.68), channel_id=1, replica_groups=mesh['dp'=4,'blk'=16,'mp'=4] {'blk'}, dimensions={0} | all-to-all | bytes 1835008 | tf_op jit(solution)/shard_map/all_to_all | solution.py:42
  52.9 2.2 broadcast_in_dim.80
  55.1 7.1 %all-to-all-start.1 = ((bf16[4,16,256,112]{2,3,1,0:T(8,128)(2,1)}), bf16[4,16,256,112]{2,3,1,0:T(8,128)(2,1)}, u32[]{:S(2)}, u32[]{:S(2)}) async-start(bf16[4,16,256,112]{2,3,1,0:T(8,128)(2,1)} %broadcast_in_dim.80), calls=%async_computation.1 | async-start | bytes 7340032 | tf_op jit(solution)/shard_map/all_to_all | solution.py:44
  62.8 0.0 copy-done.1
  62.8 0.1 fusion.37
  62.9 0.2 copy.41
  63.7 0.2 copy.42
  64.0 0.0 copy-done.2
  64.0 0.2 and_reduce_fusion
  64.2 0.1 fusion.22
  64.3 102.5 %all-to-all-done.1 = bf16[4,16,256,112]{2,3,1,0:T(8,128)(2,1)} async-done(((bf16[4,16,256,112]{2,3,1,0:T(8,128)(2,1)}), bf16[4,16,256,112]{2,3,1,0:T(8,128)(2,1)}, u32[]{:S(2)}, u32[]{:S(2)}) %all-to-all-start.1) | async-done | bytes 3670048 | tf_op jit(solution)/shard_map/all_to_all | solution.py:44
  166.7 4.4 %copy.39 = bf16[4,16,256,112]{2,3,0,1:T(8,128)(2,1)} copy(bf16[4,16,256,112]{2,3,1,0:T(8,128)(2,1)} %all-to-all-done.1) | data formatting | bytes 7340032 | tf_op jit(solution)/shard_map/all_to_all | solution.py:44
  171.2 0.0 all-gather.5.cloned.1.call-done
  171.2 7.0 %fusion.36 = (bf16[1,2048,896]{2,1,0:T(8,128)(2,1)}, bf16[1,2048,896]{2,1,0:T(8,128)(2,1)}) fusion(bf16[2,2048,896]{2,1,0:T(8,128)(2,1)} %all-gather.5.cloned.1.call-done), kind=kLoop, calls=%fused_computation.52 | loop fusion | bytes 14680064 | tf_op jit(solution)/shard_map/slice | solution.py:77
  178.2 6.2 %copy.45 = bf16[1,2048,896]{1,2,0:T(8,128)(2,1)} copy(bf16[1,2048,896]{2,1,0:T(8,128)(2,1)} %get-tuple-element.13) | data formatting | bytes 7340032 | tf_op jit(solution)/shard_map/slice | solution.py:78
  184.4 6.2 %copy.44 = bf16[1,2048,896]{1,2,0:T(8,128)(2,1)} copy(bf16[1,2048,896]{2,1,0:T(8,128)(2,1)} %get-tuple-element.12) | data formatting | bytes 7340032 | tf_op jit(solution)/shard_map/slice | solution.py:77
  190.6 20.8 %all-gather.3.cloned.1.call-done = bf16[896,7168]{1,0:T(8,128)(2,1)} async-done(((bf16[56,7168]{1,0:T(8,128)(2,1)}), bf16[896,7168]{1,0:T(8,128)(2,1)}) %all-gather.3.cloned.1.call-update) | async-done | bytes 12845072 | tf_op jit(solution)/shard_map/all_gather | solution.py:33
  211.4 1.6 constant_dynamic-slice_fusion
  213.1 1.2 copy.46
  214.3 9.8 %convolution_convert_fusion = bf16[256,896]{1,0:T(8,128)(2,1)S(1)} fusion(bf16[256,7168]{0,1:T(8,128)(2,1)} %bitcast.67, bf16[896,7168]{1,0:T(8,128)(2,1)} %all-gather.3.cloned.1.call-done), kind=kOutput, calls=%fused_computation.16 | convolution fusion | flops 3288563712 | bytes 16973824 | tf_op jit(solution)/shard_map/td,hd->th/dot_general | solution.py:46
  224.1 0.2 copy.40
  224.3 0.0 copy-start
  224.3 4.0 %fusion = (f32[4,256]{1,0:T(4,128)S(1)}, f32[4,256,2048]{2,1,0:T(8,128)S(1)}) fusion(pred[2048]{0:T(1024)(128)(4,1)S(1)} %and_reduce_fusion, bf16[256,4,224]{0,2,1:T(8,128)(2,1)S(1)} %bitcast.64, bf16[2048,4,224]{0,2,1:T(8,128)(2,1)} %bitcast.63), kind=kOutput, calls=%fused_computation.2 | convolution fusion | flops 945814528 | bytes 12523520 | tf_op jit(solution)/shard_map/thd,khd->htk/dot_general | solution.py:12
  228.3 0.4 fusion.38
  228.7 2.4 fusion.1
  231.1 0.0 copy-done
  231.1 2.1 fusion.7
  233.2 0.2 fusion.16
  233.4 0.4 fusion.15
  233.9 1.0 copy.47
  (5 shorter events, 0.0 us)
Async XLA Ops:
  7.2 164.0 %all-gather.5.cloned.1.call-start = ((), (), s32[]{:S(2)}) async-start(), calls=%async_computation.3 | async-start | bytes 7798784 | tf_op jit(solution)/shard_map/all_gather | solution.py:69
  7.9 203.5 %all-gather.3.cloned.1.call-start = ((), (), s32[]{:S(2)}) async-start(), calls=%async_computation.2 | async-start | bytes 13647872 | tf_op jit(solution)/shard_map/all_gather | solution.py:33
  21.5 41.3 %copy-start.1 = (bf16[2,256,896]{2,1,0:T(8,128)(2,1)S(1)}, bf16[2,256,896]{2,1,0:T(8,128)(2,1)}, u32[]{:S(2)}) copy-start(bf16[2,256,896]{2,1,0:T(8,128)(2,1)} %param.10) | copy-start | bytes 2752516
  22.9 41.1 %copy-start.2 = (s32[1,64]{1,0:T(1,128)S(1)}, s32[1,64]{1,0:T(1,128)}, u32[]{:S(2)}) copy-start(s32[1,64]{1,0:T(1,128)} %param.11) | copy-start | bytes 772
  55.1 111.7 %all-to-all-start.1 = ((bf16[4,16,256,112]{2,3,1,0:T(8,128)(2,1)}), bf16[4,16,256,112]{2,3,1,0:T(8,128)(2,1)}, u32[]{:S(2)}, u32[]{:S(2)}) async-start(bf16[4,16,256,112]{2,3,1,0:T(8,128)(2,1)} %broadcast_in_dim.80), calls=%async_computation.1 | async-start | bytes 7340032 | tf_op jit(solution)/shard_map/all_to_all | solution.py:44
  224.3 6.8 %copy-start = (bf16[1,2048,896]{1,2,0:T(8,128)(2,1)S(1)}, bf16[1,2048,896]{1,2,0:T(8,128)(2,1)}, u32[]{:S(2)}) copy-start(bf16[1,2048,896]{1,2,0:T(8,128)(2,1)} %copy.45) | copy-start | bytes 11010052
Sparse Core Ops, SparseCore 0:
  9.8 89.1 all-gather.4
  100.8 110.5 all-gather.2

commit v8 on v1

--- a/solution.py
+++ b/solution.py
@@ -1,6 +1,8 @@
 import jax
 import jax.numpy as jnp
 from jax import lax
+from jax.experimental import pallas as pl
+from jax.experimental.pallas import tpu as pltpu
 from jax.sharding import PartitionSpec as P
 
 HD = 224
@@ -26,10 +28,67 @@
     return (new_max, row_total, weighted)
 
 
+def dp_exchange_kernel(piece_ref, out_ref, local_sem, send_sems, recv_sems):
+    n = lax.axis_size("dp")
+    g = lax.axis_index("dp")
+    b = lax.axis_index("blk")
+    m = lax.axis_index("mp")
+    barrier = pltpu.get_barrier_semaphore()
+    for j in range(1, n):
+        pl.semaphore_signal(
+            barrier, inc=1, device_id=((g + j) % n, b, m), device_id_type=pl.DeviceIdType.MESH
+        )
+    pl.semaphore_wait(barrier, n - 1)
+    local = pltpu.make_async_copy(piece_ref, out_ref.at[g], local_sem)
+    local.start()
+    sends = []
+    for j in range(1, n):
+        copy = pltpu.make_async_remote_copy(
+            src_ref=piece_ref,
+            dst_ref=out_ref.at[g],
+            send_sem=send_sems.at[j - 1],
+            recv_sem=recv_sems.at[j - 1],
+            device_id=((g + j) % n, b, m),
+            device_id_type=pl.DeviceIdType.MESH,
+        )
+        copy.start()
+        sends.append(copy)
+    local.wait()
+    for copy in sends:
+        copy.wait_send()
+    for j in range(1, n):
+        pltpu.make_async_remote_copy(
+            src_ref=piece_ref,
+            dst_ref=out_ref.at[(g - j) % n],
+            send_sem=send_sems.at[j - 1],
+            recv_sem=recv_sems.at[j - 1],
+            device_id=((g - j) % n, b, m),
+            device_id_type=pl.DeviceIdType.MESH,
+        ).wait_recv()
+
+
+def gather_dp(piece):
+    n = lax.axis_size("dp")
+    rows, cols = piece.shape
+    out = pl.pallas_call(
+        dp_exchange_kernel,
+        out_shape=jax.ShapeDtypeStruct((n, rows, cols), piece.dtype),
+        in_specs=[pl.BlockSpec(memory_space=pl.ANY)],
+        out_specs=pl.BlockSpec(memory_space=pl.ANY),
+        scratch_shapes=[
+            pltpu.SemaphoreType.DMA(()),
+            pltpu.SemaphoreType.DMA((n - 1,)),
+            pltpu.SemaphoreType.DMA((n - 1,)),
+        ],
+        compiler_params=pltpu.CompilerParams(collective_id=0, has_side_effects=True),
+    )(piece)
+    return jnp.transpose(out, (1, 0, 2)).reshape(rows, n * cols)
+
+
 def body(tokens, trainer_q, kv_pool, prompt_kv, page_table, page_count, prompt_len):
     blk_size = lax.axis_size("blk")
     mp_size = lax.axis_size("mp")
-    trainer_rows = lax.all_gather(trainer_q.astype(jnp.bfloat16), "dp", axis=1, tiled=True)
+    trainer_rows = gather_dp(trainer_q.astype(jnp.bfloat16))
     head_weights = lax.all_gather(trainer_rows, "blk", axis=0, tiled=True)
     head_width, model_width = head_weights.shape
     block_cols = model_width // blk_size

time: 234 us -> 234 us (level)
  Pallas kernels: 0 us -> 12.7 us
  blocking collectives: 12.5 us -> 0 us
    pallas_call x0 -> x1, Pallas kernels: none -> 12.7 us  [gather_dp(): pl.pallas_call(dp_exchange_kernel, out_shape=jax.ShapeDtypeStruct((n, row...]
    all_gather x1 -> x0, blocking collectives: 12.5 us -> none  [body(): lax.all_gather(trainer_q.astype(jnp.bfloat16), 'dp', axis=1, tiled=True)]
    all_gather x1, waiting for transfers between devices: 69.7 us -> 64.8 us  [body(): shard_piece = lax.all_gather(kv_pool, 'blk', axis=1, tiled=True)]
    all_gather x1, waiting for transfers between devices: 71.3 us -> 74.3 us  [body(): head_weights = lax.all_gather(trainer_rows, 'blk', axis=0, tiled=True)]
  transfers between devices with their start and end apart: 3 -> 3, of which waited for: 2 -> 2; matrix products, arithmetic and copies ran while one was open for 12% -> 13% of each run, Pallas kernels for 0% -> 5%
where the time goes in v8:
time: 234 us; the launch traced here: 232 us
  waiting for transfers between devices  140 us (60%)
  local copies, waits for them, and re-layouts  29.2 us (12%)
  matrix products  16.7 us (7%)
  between operations  15.5 us (7%)
  starting transfers between devices  13.3 us (6%)
  Pallas kernels  12.7 us (5%)
  other arithmetic  4.59 us (2%)
    all_gather x1, waiting for transfers between devices, body(): head_weights = lax.all_gather(trainer_rows, 'blk', axis=0, tiled=True)  74.3 us
    all_gather x1, waiting for transfers between devices, body(): shard_piece = lax.all_gather(kv_pool, 'blk', axis=1, tiled=True)  64.8 us
    all_to_all x1, starting transfers between devices, body(): pieces = lax.all_to_all(pieces, ('blk', 'mp'), 0, 0, tiled=True)  13.2 us
    slice x2, local copies, waits for them, and re-layouts, body(): shard_piece[0].reshape(key_count, head_count, HD)  12.9 us
    pallas_call x1, Pallas kernels, gather_dp(): pl.pallas_call(dp_exchange_kernel, out_shape=jax.ShapeDtypeStruct((n, row...  12.7 us
    dot_general x1, matrix products, body(): jnp.einsum('td,hd->th', token_local, head_weights, preferred_element_type...  9.78 us
    slice x1, local copies, waits for them, and re-layouts, body(): shard_piece[1].reshape(key_count, head_count, HD)  6.21 us
  transfers between devices with their start and end apart: 3, of which 2 were waited for; matrix products, arithmetic and copies ran while one was open for 13% of the time, Pallas kernels for 5%

profile of v8, /device:TPU:25, one launch (start us, length us, event | category | flops | bytes accessed | tf_op | source)
XLA Modules:
  0.0 231.8 jit_solution(5456008157024100835)
XLA Ops:
  7.2 0.0 all-gather.5.cloned.1.call-start
  7.2 0.7 all-gather.5.cloned.1.call-update
  7.9 0.0 all-gather.3.cloned.1.call-start
  7.9 1.7 convert_element_type.18.piece_ref
  9.6 0.0 copy-start.1
  9.6 12.7 %shard_map.86 = bf16[4,56,1792]{2,1,0:T(8,128)(2,1)} custom-call(bf16[56,1792]{1,0:T(8,128)(2,1)} %convert_element_type.18.piece_ref), custom_call_target="tpu_custom_call" | custom-call | tf_op jit(solution)/shard_map/pallas_call | solution.py:73
  22.4 2.1 copy.40
  24.5 0.0 all-gather.3.cloned.1.call-update
  24.5 0.0 copy-start.2
  24.5 1.3 copy.42
  25.8 2.2 broadcast_in_dim.82
  28.0 13.2 %all-to-all-start = ((bf16[64,256,112]{1,2,0:T(8,128)(2,1)}), bf16[64,256,112]{1,2,0:T(8,128)(2,1)}, u32[]{:S(2)}, u32[]{:S(2)}) async-start(bf16[64,256,112]{1,2,0:T(8,128)(2,1)} %bitcast.67), calls=%async_computation | async-start | bytes 7340032 | tf_op jit(solution)/shard_map/all_to_all | solution.py:103
  41.9 0.0 copy-done.1
  41.9 0.1 fusion.37
  42.0 0.2 copy.31
  42.8 0.2 copy.32
  43.1 0.0 copy-done.2
  43.1 0.2 and_reduce_fusion
  43.2 0.1 fusion.22
  43.4 64.8 %all-gather.5.cloned.1.call-done = bf16[2,2048,896]{2,1,0:T(8,128)(2,1)} async-done(((bf16[2,128,896]{2,1,0:T(8,128)(2,1)}), bf16[2,2048,896]{2,1,0:T(8,128)(2,1)}) %all-gather.5.cloned.1.call-update) | async-done | bytes 7340048 | tf_op jit(solution)/shard_map/all_gather | solution.py:128
  108.2 6.7 %fusion.36 = (bf16[1,2048,896]{2,1,0:T(8,128)(2,1)}, bf16[1,2048,896]{2,1,0:T(8,128)(2,1)}) fusion(bf16[2,2048,896]{2,1,0:T(8,128)(2,1)} %all-gather.5.cloned.1.call-done), kind=kLoop, calls=%fused_computation.52 | loop fusion | bytes 14680064 | tf_op jit(solution)/shard_map/slice | solution.py:136
  114.9 6.2 %copy.35 = bf16[1,2048,896]{1,2,0:T(8,128)(2,1)} copy(bf16[1,2048,896]{2,1,0:T(8,128)(2,1)} %get-tuple-element.11) | data formatting | bytes 7340032 | tf_op jit(solution)/shard_map/slice | solution.py:137
  121.1 6.2 %copy.34 = bf16[1,2048,896]{1,2,0:T(8,128)(2,1)} copy(bf16[1,2048,896]{2,1,0:T(8,128)(2,1)} %get-tuple-element.10) | data formatting | bytes 7340032 | tf_op jit(solution)/shard_map/slice | solution.py:136
  127.3 74.3 %all-gather.3.cloned.1.call-done = bf16[896,7168]{1,0:T(8,128)(2,1)} async-done(((bf16[56,7168]{1,0:T(8,128)(2,1)}), bf16[896,7168]{1,0:T(8,128)(2,1)}) %all-gather.3.cloned.1.call-update) | async-done | bytes 12845072 | tf_op jit(solution)/shard_map/all_gather | solution.py:92
  201.6 1.6 constant_dynamic-slice_fusion
  203.2 1.2 copy.36
  204.5 0.0 all-to-all-done
  204.5 9.8 %convolution_convert_fusion = bf16[256,896]{1,0:T(8,128)(2,1)S(1)} fusion(bf16[256,7168]{0,1:T(8,128)(2,1)} %bitcast.4, bf16[896,7168]{1,0:T(8,128)(2,1)} %all-gather.3.cloned.1.call-done), kind=kOutput, calls=%fused_computation.16 | convolution fusion | flops 3288563712 | bytes 16973824 | tf_op jit(solution)/shard_map/td,hd->th/dot_general | solution.py:105
  214.3 0.2 copy.30
  214.5 0.0 copy-start
  214.5 4.0 %fusion = (f32[4,256]{1,0:T(4,128)S(1)}, f32[4,256,2048]{2,1,0:T(8,128)S(1)}) fusion(pred[2048]{0:T(1024)(128)(4,1)S(1)} %and_reduce_fusion, bf16[256,4,224]{0,2,1:T(8,128)(2,1)S(1)} %bitcast.69, bf16[2048,4,224]{0,2,1:T(8,128)(2,1)} %bitcast.68), kind=kOutput, calls=%fused_computation.2 | convolution fusion | flops 945814528 | bytes 12523520 | tf_op jit(solution)/shard_map/thd,khd->htk/dot_general | solution.py:14
  218.4 0.4 fusion.38
  218.9 2.4 %fusion.1 = f32[4,256]{1,0:T(4,128)S(1)} fusion(f32[4,256,2048]{2,1,0:T(8,128)S(1)} %get-tuple-element.20, f32[4,256]{1,0:T(4,128)S(1)} %get-tuple-element.16, pred[2048]{0:T(1024)(128)(4,1)S(1)} %and_reduce_fusion), kind=kLoop, calls=%fused_computation.3 | loop fusion | flops 10484736 | bytes 8398848 | tf_op jit(solution)/shard_map/reduce_sum | solution.py:21
  221.2 0.0 copy-done
  221.3 2.1 fusion.7
  223.4 0.2 fusion.16
  223.6 0.4 fusion.15
  224.0 1.0 copy.37
  (5 shorter events, 0.0 us)
Async XLA Ops:
  7.2 101.0 %all-gather.5.cloned.1.call-start = ((), (), s32[]{:S(2)}) async-start(), calls=%async_computation.2 | async-start | bytes 7798784 | tf_op jit(solution)/shard_map/all_gather | solution.py:128
  7.9 193.7 %all-gather.3.cloned.1.call-start = ((), (), s32[]{:S(2)}) async-start(), calls=%async_computation.1 | async-start | bytes 13647872 | tf_op jit(solution)/shard_map/all_gather | solution.py:92
  9.6 32.2 %copy-start.1 = (bf16[2,256,896]{2,1,0:T(8,128)(2,1)S(1)}, bf16[2,256,896]{2,1,0:T(8,128)(2,1)}, u32[]{:S(2)}) copy-start(bf16[2,256,896]{2,1,0:T(8,128)(2,1)} %param.10) | copy-start | bytes 2752516
  24.5 18.6 %copy-start.2 = (s32[1,64]{1,0:T(1,128)S(1)}, s32[1,64]{1,0:T(1,128)}, u32[]{:S(2)}) copy-start(s32[1,64]{1,0:T(1,128)} %param.11) | copy-start | bytes 772
  28.0 176.5 %all-to-all-start = ((bf16[64,256,112]{1,2,0:T(8,128)(2,1)}), bf16[64,256,112]{1,2,0:T(8,128)(2,1)}, u32[]{:S(2)}, u32[]{:S(2)}) async-start(bf16[64,256,112]{1,2,0:T(8,128)(2,1)} %bitcast.67), calls=%async_computation | async-start | bytes 7340032 | tf_op jit(solution)/shard_map/all_to_all | solution.py:103
  214.5 6.8 %copy-start = (bf16[1,2048,896]{1,2,0:T(8,128)(2,1)S(1)}, bf16[1,2048,896]{1,2,0:T(8,128)(2,1)}, u32[]{:S(2)}) copy-start(bf16[1,2048,896]{1,2,0:T(8,128)(2,1)} %copy.35) | copy-start | bytes 11010052
Sparse Core Ops, SparseCore 0:
  9.8 98.3 all-gather.4
  110.6 90.9 all-gather.2

commit v9 on v8

--- a/solution.py
+++ b/solution.py
@@ -95,6 +95,8 @@
     server_q = lax.dynamic_slice_in_dim(
         head_weights, lax.axis_index("blk") * block_cols, block_cols, axis=1
     )
+    shard_piece = lax.all_gather(kv_pool, "blk", axis=1, tiled=True)
+    tokens, shard_piece = lax.optimization_barrier((tokens, shard_piece))
     group_rows, piece_cols = tokens.shape
     own_rows = group_rows // blk_size
     pieces = tokens.reshape(blk_size, 1, own_rows, piece_cols)
@@ -125,7 +127,6 @@
         prompt_kv[1].reshape(own_rows, head_count, HD),
         own_mask,
     )
-    shard_piece = lax.all_gather(kv_pool, "blk", axis=1, tiled=True)
     key_count = shard_piece.shape[1]
     page_ids = jnp.arange(key_count, dtype=jnp.int32) // PAGE
     page_used = jnp.any((row_pages[None, :] == page_ids[:, None]) & live_slots[None, :], axis=1)

time: 234 us -> 251 us (1.073)
  waiting for transfers between devices: 140 us -> 161 us
  starting transfers between devices: 13.3 us -> 10.4 us
    all_gather x1, waiting for transfers between devices: 74.3 us -> 122 us  [body(): head_weights = lax.all_gather(trainer_rows, 'blk', axis=0, tiled=True)]
    all_gather x1, waiting for transfers between devices: 64.8 us -> 38.2 us  [body(): shard_piece = lax.all_gather(kv_pool, 'blk', axis=1, tiled=True)]
    all_to_all x1, starting transfers between devices: 13.2 us -> 10.3 us  [body(): pieces = lax.all_to_all(pieces, ('blk', 'mp'), 0, 0, tiled=True)]
  transfers between devices with their start and end apart: 3 -> 3, of which waited for: 2 -> 2; matrix products, arithmetic and copies ran while one was open for 13% -> 12% of each run, Pallas kernels for 5% -> 5%
where the time goes in v9:
time: 251 us; the launch traced here: 250 us
  waiting for transfers between devices  161 us (64%)
  local copies, waits for them, and re-layouts  29.2 us (12%)
  matrix products  16.7 us (7%)
  between operations  15.5 us (6%)
  Pallas kernels  12.7 us (5%)
  starting transfers between devices  10.4 us (4%)
  other arithmetic  4.59 us (2%)
    all_gather x1, waiting for transfers between devices, body(): head_weights = lax.all_gather(trainer_rows, 'blk', axis=0, tiled=True)  122 us
    all_gather x1, waiting for transfers between devices, body(): shard_piece = lax.all_gather(kv_pool, 'blk', axis=1, tiled=True)  38.2 us
    slice x2, local copies, waits for them, and re-layouts, body(): shard_piece[0].reshape(key_count, head_count, HD)  12.9 us
    pallas_call x1, Pallas kernels, gather_dp(): pl.pallas_call(dp_exchange_kernel, out_shape=jax.ShapeDtypeStruct((n, row...  12.7 us
    all_to_all x1, starting transfers between devices, body(): pieces = lax.all_to_all(pieces, ('blk', 'mp'), 0, 0, tiled=True)  10.3 us
    dot_general x1, matrix products, body(): jnp.einsum('td,hd->th', token_local, head_weights, preferred_element_type...  9.78 us
    slice x1, local copies, waits for them, and re-layouts, body(): shard_piece[1].reshape(key_count, head_count, HD)  6.21 us
  transfers between devices with their start and end apart: 3, of which 2 were waited for; matrix products, arithmetic and copies ran while one was open for 12% of the time, Pallas kernels for 5%

profile of v9, /device:TPU:25, one launch (start us, length us, event | category | flops | bytes accessed | tf_op | source)
XLA Modules:
  0.0 249.6 jit_solution(1721553573545247659)
XLA Ops:
  7.2 0.0 all-gather.5.cloned.1.call-start
  7.2 0.7 all-gather.5.cloned.1.call-update
  7.9 0.0 all-gather.3.cloned.1.call-start
  7.9 1.7 convert_element_type.18.piece_ref
  9.6 0.0 copy-start.1
  9.6 12.7 %shard_map.86 = bf16[4,56,1792]{2,1,0:T(8,128)(2,1)} custom-call(bf16[56,1792]{1,0:T(8,128)(2,1)} %convert_element_type.18.piece_ref), custom_call_target="tpu_custom_call" | custom-call | tf_op jit(solution)/shard_map/pallas_call | solution.py:73
  22.4 2.1 copy.40
  24.5 0.0 all-gather.3.cloned.1.call-update
  24.5 38.2 %all-gather.5.cloned.1.call-done = bf16[2,2048,896]{2,1,0:T(8,128)(2,1)} async-done(((bf16[2,128,896]{2,1,0:T(8,128)(2,1)}), bf16[2,2048,896]{2,1,0:T(8,128)(2,1)}) %all-gather.5.cloned.1.call-update) | async-done | bytes 7340048 | tf_op jit(solution)/shard_map/all_gather | solution.py:98
  62.7 0.0 copy-start.2
  62.7 1.3 copy.42
  63.9 2.2 broadcast_in_dim.82
  66.1 10.3 %all-to-all-start = ((bf16[64,256,112]{1,2,0:T(8,128)(2,1)}), bf16[64,256,112]{1,2,0:T(8,128)(2,1)}, u32[]{:S(2)}, u32[]{:S(2)}) async-start(bf16[64,256,112]{1,2,0:T(8,128)(2,1)} %bitcast.67), calls=%async_computation | async-start | bytes 7340032 | tf_op jit(solution)/shard_map/all_to_all | solution.py:105
  77.0 0.0 copy-done.1
  77.0 0.1 fusion.37
  77.1 0.2 copy.31
  78.0 0.2 copy.32
  78.3 0.0 copy-done.2
  78.3 0.2 and_reduce_fusion
  78.4 0.1 fusion.22
  78.5 6.7 %fusion.36 = (bf16[1,2048,896]{2,1,0:T(8,128)(2,1)}, bf16[1,2048,896]{2,1,0:T(8,128)(2,1)}) fusion(bf16[2,2048,896]{2,1,0:T(8,128)(2,1)} %all-gather.5.cloned.1.call-done), kind=kLoop, calls=%fused_computation.52 | loop fusion | bytes 14680064 | tf_op jit(solution)/shard_map/slice | solution.py:137
  85.3 6.2 %copy.35 = bf16[1,2048,896]{1,2,0:T(8,128)(2,1)} copy(bf16[1,2048,896]{2,1,0:T(8,128)(2,1)} %get-tuple-element.15) | data formatting | bytes 7340032 | tf_op jit(solution)/shard_map/slice | solution.py:138
  91.5 6.2 %copy.34 = bf16[1,2048,896]{1,2,0:T(8,128)(2,1)} copy(bf16[1,2048,896]{2,1,0:T(8,128)(2,1)} %get-tuple-element.14) | data formatting | bytes 7340032 | tf_op jit(solution)/shard_map/slice | solution.py:137
  97.6 121.7 %all-gather.3.cloned.1.call-done = bf16[896,7168]{1,0:T(8,128)(2,1)} async-done(((bf16[56,7168]{1,0:T(8,128)(2,1)}), bf16[896,7168]{1,0:T(8,128)(2,1)}) %all-gather.3.cloned.1.call-update) | async-done | bytes 12845072 | tf_op jit(solution)/shard_map/all_gather | solution.py:92
  219.4 1.6 constant_dynamic-slice_fusion
  221.0 1.2 copy.36
  222.3 0.0 all-to-all-done
  222.3 9.8 %convolution_convert_fusion = bf16[256,896]{1,0:T(8,128)(2,1)S(1)} fusion(bf16[256,7168]{0,1:T(8,128)(2,1)} %bitcast.4, bf16[896,7168]{1,0:T(8,128)(2,1)} %all-gather.3.cloned.1.call-done), kind=kOutput, calls=%fused_computation.16 | convolution fusion | flops 3288563712 | bytes 16973824 | tf_op jit(solution)/shard_map/td,hd->th/dot_general | solution.py:107
  232.0 0.2 copy.30
  232.3 0.0 copy-start
  232.3 4.0 %fusion = (f32[4,256]{1,0:T(4,128)S(1)}, f32[4,256,2048]{2,1,0:T(8,128)S(1)}) fusion(pred[2048]{0:T(1024)(128)(4,1)S(1)} %and_reduce_fusion, bf16[256,4,224]{0,2,1:T(8,128)(2,1)S(1)} %bitcast.69, bf16[2048,4,224]{0,2,1:T(8,128)(2,1)} %bitcast.68), kind=kOutput, calls=%fused_computation.2 | convolution fusion | flops 945814528 | bytes 12523520 | tf_op jit(solution)/shard_map/thd,khd->htk/dot_general | solution.py:14
  236.2 0.4 fusion.38
  236.6 2.4 fusion.1
  239.0 0.0 copy-done
  239.0 2.1 fusion.7
  241.2 0.2 fusion.16
  241.4 0.4 fusion.15
  241.8 1.0 copy.37
  (5 shorter events, 0.0 us)
Async XLA Ops:
  7.2 55.5 %all-gather.5.cloned.1.call-start = ((), (), s32[]{:S(2)}) async-start(), calls=%async_computation.2 | async-start | bytes 7798784 | tf_op jit(solution)/shard_map/all_gather | solution.py:98
  7.9 211.5 %all-gather.3.cloned.1.call-start = ((), (), s32[]{:S(2)}) async-start(), calls=%async_computation.1 | async-start | bytes 13647872 | tf_op jit(solution)/shard_map/all_gather | solution.py:92
  9.6 67.4 %copy-start.1 = (bf16[2,256,896]{2,1,0:T(8,128)(2,1)S(1)}, bf16[2,256,896]{2,1,0:T(8,128)(2,1)}, u32[]{:S(2)}) copy-start(bf16[2,256,896]{2,1,0:T(8,128)(2,1)} %param.10) | copy-start | bytes 2752516
  62.7 15.6 %copy-start.2 = (s32[1,64]{1,0:T(1,128)S(1)}, s32[1,64]{1,0:T(1,128)}, u32[]{:S(2)}) copy-start(s32[1,64]{1,0:T(1,128)} %param.11) | copy-start | bytes 772
  66.1 156.2 %all-to-all-start = ((bf16[64,256,112]{1,2,0:T(8,128)(2,1)}), bf16[64,256,112]{1,2,0:T(8,128)(2,1)}, u32[]{:S(2)}, u32[]{:S(2)}) async-start(bf16[64,256,112]{1,2,0:T(8,128)(2,1)} %bitcast.67), calls=%async_computation | async-start | bytes 7340032 | tf_op jit(solution)/shard_map/all_to_all | solution.py:105
  232.3 6.8 %copy-start = (bf16[1,2048,896]{1,2,0:T(8,128)(2,1)S(1)}, bf16[1,2048,896]{1,2,0:T(8,128)(2,1)}, u32[]{:S(2)}) copy-start(bf16[1,2048,896]{1,2,0:T(8,128)(2,1)} %copy.35) | copy-start | bytes 11010052
Sparse Core Ops, SparseCore 0:
  9.8 52.8 all-gather.4
  65.1 154.2 all-gather.2

commit v10 on v8

--- a/solution.py
+++ b/solution.py
@@ -89,11 +89,23 @@
     blk_size = lax.axis_size("blk")
     mp_size = lax.axis_size("mp")
     trainer_rows = gather_dp(trainer_q.astype(jnp.bfloat16))
-    head_weights = lax.all_gather(trainer_rows, "blk", axis=0, tiled=True)
-    head_width, model_width = head_weights.shape
+    half_cols = trainer_rows.shape[1] // 2
+    weight_halves = [
+        lax.all_gather(trainer_rows[:, :half_cols], "blk", axis=0, tiled=True),
+        lax.all_gather(trainer_rows[:, half_cols:], "blk", axis=0, tiled=True),
+    ]
+    head_width, model_width = weight_halves[0].shape[0], trainer_rows.shape[1]
     block_cols = model_width // blk_size
-    server_q = lax.dynamic_slice_in_dim(
-        head_weights, lax.axis_index("blk") * block_cols, block_cols, axis=1
+    b = lax.axis_index("blk")
+    halves_per_blocks = blk_size // 2
+    server_q = jnp.where(
+        b < halves_per_blocks,
+        lax.dynamic_slice_in_dim(
+            weight_halves[0], (b % halves_per_blocks) * block_cols, block_cols, axis=1
+        ),
+        lax.dynamic_slice_in_dim(
+            weight_halves[1], (b % halves_per_blocks) * block_cols, block_cols, axis=1
+        ),
     )
     group_rows, piece_cols = tokens.shape
     own_rows = group_rows // blk_size
@@ -103,7 +115,9 @@
     pieces = lax.all_to_all(pieces, ("blk", "mp"), 0, 0, tiled=True)
     token_local = jnp.transpose(pieces, (1, 0, 2)).reshape(own_rows, -1)
     queries = jnp.einsum(
-        "td,hd->th", token_local, head_weights, preferred_element_type=jnp.float32
+        "td,hd->th", token_local[:, :half_cols], weight_halves[0], preferred_element_type=jnp.float32
+    ) + jnp.einsum(
+        "td,hd->th", token_local[:, half_cols:], weight_halves[1], preferred_element_type=jnp.float32
     )
     queries = queries.astype(jnp.bfloat16)
     head_count = head_width // HD

time: 234 us -> 274 us (1.17)
  waiting for transfers between devices: 140 us -> 179 us
  local copies, waits for them, and re-layouts: 29.2 us -> 26.4 us
    all_gather x1 -> x2, waiting for transfers between devices: 74.3 us -> 141 us  [the longest x1 90.4 us: body(): lax.all_gather(trainer_rows[:, half_cols:], 'blk', axis=0, tiled=True)]
    all_gather x1, waiting for transfers between devices: 64.8 us -> 37.2 us  [body(): shard_piece = lax.all_gather(kv_pool, 'blk', axis=1, tiled=True)]
    dot_general x1 -> x2, matrix products: 9.78 us -> 11 us  [the longest x1 5.51 us: body(): jnp.einsum('td,hd->th', token_local[:, :half_cols], weight_halves[0], pre...]
  transfers between devices with their start and end apart: 3 -> 4, of which waited for: 2 -> 3; matrix products, arithmetic and copies ran while one was open for 13% -> 7% of each run, Pallas kernels for 5% -> 0%
where the time goes in v10:
time: 274 us; the launch traced here: 272 us
  waiting for transfers between devices  179 us (65%)
  local copies, waits for them, and re-layouts  26.4 us (10%)
  matrix products  17.7 us (6%)
  between operations  15.3 us (6%)
  starting transfers between devices  13.5 us (5%)
  Pallas kernels  12.7 us (5%)
  other arithmetic  7.13 us (3%)
    all_gather x1, waiting for transfers between devices, body(): lax.all_gather(trainer_rows[:, half_cols:], 'blk', axis=0, tiled=True)  90.4 us
    all_gather x1, waiting for transfers between devices, body(): lax.all_gather(trainer_rows[:, :half_cols], 'blk', axis=0, tiled=True)  50.4 us
    all_gather x1, waiting for transfers between devices, body(): shard_piece = lax.all_gather(kv_pool, 'blk', axis=1, tiled=True)  37.2 us
    all_to_all x1, starting transfers between devices, body(): pieces = lax.all_to_all(pieces, ('blk', 'mp'), 0, 0, tiled=True)  13.4 us
    slice x2, local copies, waits for them, and re-layouts, body(): shard_piece[0].reshape(key_count, head_count, HD)  12.9 us
    pallas_call x1, Pallas kernels, gather_dp(): pl.pallas_call(dp_exchange_kernel, out_shape=jax.ShapeDtypeStruct((n, row...  12.7 us
    slice x1, local copies, waits for them, and re-layouts, body(): shard_piece[1].reshape(key_count, head_count, HD)  6.16 us
    dot_general x1, matrix products, body(): jnp.einsum('td,hd->th', token_local[:, :half_cols], weight_halves[0], pre...  5.51 us
  transfers between devices with their start and end apart: 4, of which 3 were waited for; matrix products, arithmetic and copies ran while one was open for 7% of the time, Pallas kernels for 0%

profile of v10, /device:TPU:25, one launch (start us, length us, event | category | flops | bytes accessed | tf_op | source)
XLA Modules:
  0.0 272.0 jit_solution(6166015738734465113)
XLA Ops:
  7.2 0.0 copy-start.1
  7.2 0.0 all-gather.6.cloned.1.call-start
  7.2 1.8 convert_element_type.18.piece_ref
  9.0 12.7 %shard_map.86 = bf16[4,56,1792]{2,1,0:T(8,128)(2,1)} custom-call(bf16[56,1792]{1,0:T(8,128)(2,1)} %convert_element_type.18.piece_ref), custom_call_target="tpu_custom_call" | custom-call | tf_op jit(solution)/shard_map/pallas_call | solution.py:73
  21.7 1.2 copy.40
  22.9 0.9 fusion.48
  23.9 0.0 all-gather.6.cloned.1.call-update
  23.9 0.0 all-gather.4.cloned.1.call-start
  23.9 0.7 all-gather.4.cloned.1.call-update
  24.6 0.0 all-gather.8.cloned.1.call-start
  24.7 0.7 all-gather.8.cloned.1.call-update
  25.4 0.0 copy-done.1
  25.4 0.1 copy.42
  25.5 0.0 copy-start.2
  25.5 2.2 broadcast_in_dim.82
  27.7 0.0 copy-start.3
  27.7 13.4 %all-to-all-start = ((bf16[64,256,112]{1,2,0:T(8,128)(2,1)}), bf16[64,256,112]{1,2,0:T(8,128)(2,1)}, u32[]{:S(2)}, u32[]{:S(2)}) async-start(bf16[64,256,112]{1,2,0:T(8,128)(2,1)} %bitcast.67), calls=%async_computation | async-start | bytes 7340032 | tf_op jit(solution)/shard_map/all_to_all | solution.py:115
  41.7 0.0 copy-done.2
  41.8 0.1 fusion.47
  41.8 0.2 copy.31
  42.7 0.2 copy.32
  43.0 0.0 copy-done.3
  43.0 0.2 and_reduce_fusion
  43.1 0.1 fusion.32
  43.2 90.4 %all-gather.6.cloned.1.call-done = bf16[896,3584]{1,0:T(8,128)(2,1)} async-done(((bf16[56,3584]{1,0:T(8,128)(2,1)}), bf16[896,3584]{1,0:T(8,128)(2,1)}) %all-gather.6.cloned.1.call-update) | async-done | bytes 6422544 | tf_op jit(solution)/shard_map/all_gather | solution.py:95
  133.6 50.4 %all-gather.4.cloned.1.call-done = bf16[896,3584]{1,0:T(8,128)(2,1)} async-done(((bf16[56,3584]{1,0:T(8,128)(2,1)}), bf16[896,3584]{1,0:T(8,128)(2,1)}) %all-gather.4.cloned.1.call-update) | async-done | bytes 6422544 | tf_op jit(solution)/shard_map/all_gather | solution.py:94
  184.0 2.5 dynamic-slice_select_fusion
  186.5 1.2 copy.36
  187.7 0.0 all-to-all-done
  187.7 5.5 %fusion.6 = f32[256,896]{1,0:T(8,128)S(1)} fusion(bf16[896,3584]{1,0:T(8,128)(2,1)} %all-gather.6.cloned.1.call-done, bf16[256,7168]{0,1:T(8,128)(2,1)} %bitcast.4), kind=kOutput, calls=%fused_computation.7 | convolution fusion | flops 1644167168 | bytes 9175040 | tf_op jit(solution)/shard_map/td,hd->th/dot_general | solution.py:119
  193.2 5.5 %fusion.22 = bf16[256,896]{1,0:T(8,128)(2,1)S(1)} fusion(f32[256,896]{1,0:T(8,128)S(1)} %fusion.6, bf16[896,3584]{1,0:T(8,128)(2,1)} %all-gather.4.cloned.1.call-done, bf16[256,7168]{0,1:T(8,128)(2,1)} %bitcast.4), kind=kOutput, calls=%fused_computation.21 | convolution fusion | flops 1644625920 | bytes 9633792 | tf_op jit(solution)/shard_map/td,hd->th/dot_general | solution.py:117
  198.7 0.2 copy.30
  198.9 0.4 fusion.49
  199.3 37.2 %all-gather.8.cloned.1.call-done = bf16[2,2048,896]{2,1,0:T(8,128)(2,1)} async-done(((bf16[2,128,896]{2,1,0:T(8,128)(2,1)}), bf16[2,2048,896]{2,1,0:T(8,128)(2,1)}) %all-gather.8.cloned.1.call-update) | async-done | bytes 7340048 | tf_op jit(solution)/shard_map/all_gather | solution.py:142
  236.5 6.7 %fusion.46 = (bf16[1,2048,896]{2,1,0:T(8,128)(2,1)}, bf16[1,2048,896]{2,1,0:T(8,128)(2,1)}) fusion(bf16[2,2048,896]{2,1,0:T(8,128)(2,1)} %all-gather.8.cloned.1.call-done), kind=kLoop, calls=%fused_computation.57 | loop fusion | bytes 14680064 | tf_op jit(solution)/shard_map/slice | solution.py:150
  243.2 6.2 %copy.35 = bf16[1,2048,896]{1,2,0:T(8,128)(2,1)} copy(bf16[1,2048,896]{2,1,0:T(8,128)(2,1)} %get-tuple-element.11) | data formatting | bytes 7340032 | tf_op jit(solution)/shard_map/slice | solution.py:151
  249.4 6.1 %copy.34 = bf16[1,2048,896]{1,2,0:T(8,128)(2,1)} copy(bf16[1,2048,896]{2,1,0:T(8,128)(2,1)} %get-tuple-element.10) | data formatting | bytes 7340032 | tf_op jit(solution)/shard_map/slice | solution.py:150
  255.5 3.8 %fusion = (f32[4,256]{1,0:T(4,128)S(1)}, f32[4,256,2048]{2,1,0:T(8,128)S(1)}) fusion(pred[2048]{0:T(1024)(128)(4,1)S(1)} %and_reduce_fusion, bf16[256,4,224]{0,2,1:T(8,128)(2,1)S(1)} %bitcast.70, bf16[2048,4,224]{0,2,1:T(8,128)(2,1)} %bitcast.68), kind=kOutput, calls=%fused_computation.2 | convolution fusion | flops 945814528 | bytes 12523520 | tf_op jit(solution)/shard_map/thd,khd->htk/dot_general | solution.py:14
  259.3 0.0 copy-start
  259.4 2.4 fusion.1
  261.7 0.0 copy-done
  261.8 2.1 fusion.11
  263.9 0.2 fusion.26
  264.1 0.4 fusion.25
  264.5 1.0 copy.37
  (5 shorter events, 0.0 us)
Async XLA Ops:
  7.2 18.2 %copy-start.1 = (bf16[4096,112]{0,1:T(8,128)(2,1)S(1)}, bf16[4096,112]{0,1:T(8,128)(2,1)}, u32[]{:S(2)}) copy-start(bf16[4096,112]{0,1:T(8,128)(2,1)} %param.7) | copy-start | bytes 2752516
  7.2 126.4 %all-gather.6.cloned.1.call-start = ((), (), s32[]{:S(2)}) async-start(), calls=%async_computation.2 | async-start | bytes 6823936 | tf_op jit(solution)/shard_map/all_gather | solution.py:95
  23.9 160.1 %all-gather.4.cloned.1.call-start = ((), (), s32[]{:S(2)}) async-start(), calls=%async_computation.1 | async-start | bytes 6823936 | tf_op jit(solution)/shard_map/all_gather | solution.py:94
  24.6 211.8 %all-gather.8.cloned.1.call-start = ((), (), s32[]{:S(2)}) async-start(), calls=%async_computation.3 | async-start | bytes 7798784 | tf_op jit(solution)/shard_map/all_gather | solution.py:142
  25.5 16.3 %copy-start.2 = (bf16[2,256,896]{2,1,0:T(8,128)(2,1)S(1)}, bf16[2,256,896]{2,1,0:T(8,128)(2,1)}, u32[]{:S(2)}) copy-start(bf16[2,256,896]{2,1,0:T(8,128)(2,1)} %param.10) | copy-start | bytes 2752516
  27.7 15.3 %copy-start.3 = (s32[1,64]{1,0:T(1,128)S(1)}, s32[1,64]{1,0:T(1,128)}, u32[]{:S(2)}) copy-start(s32[1,64]{1,0:T(1,128)} %param.11) | copy-start | bytes 772
  27.7 160.0 %all-to-all-start = ((bf16[64,256,112]{1,2,0:T(8,128)(2,1)}), bf16[64,256,112]{1,2,0:T(8,128)(2,1)}, u32[]{:S(2)}, u32[]{:S(2)}) async-start(bf16[64,256,112]{1,2,0:T(8,128)(2,1)} %bitcast.67), calls=%async_computation | async-start | bytes 7340032 | tf_op jit(solution)/shard_map/all_to_all | solution.py:115
  259.3 2.4 copy-start
Sparse Core Ops, SparseCore 0:
  24.0 109.5 all-gather.5
  136.0 47.9 all-gather.3
  185.8 50.6 all-gather.7

commit v11 on v5

--- a/solution.py
+++ b/solution.py
@@ -36,16 +36,17 @@
     piece_rows, quarter_cols = trainer_q.shape
     trainer_rows = lax.all_gather(trainer_q.astype(jnp.bfloat16), "dp", axis=1, tiled=True)
     trainer_rows = trainer_rows.reshape(piece_rows, dp_size, quarter_cols)
-    chosen = jnp.stack(
-        [
-            lax.dynamic_index_in_dim(trainer_rows, g, 1, keepdims=False),
-            lax.dynamic_index_in_dim(trainer_rows, (g + 2) % dp_size, 1, keepdims=False),
-        ]
-    )
-    chosen = lax.all_gather(chosen, "blk", axis=1, tiled=True)
-    head_width = chosen.shape[1]
+    shard_piece = lax.all_gather(kv_pool, "blk", axis=1, tiled=True)
+    own_piece = lax.dynamic_index_in_dim(trainer_rows, g, 1, keepdims=False)
+    far_piece = lax.dynamic_index_in_dim(trainer_rows, (g + 2) % dp_size, 1, keepdims=False)
+    own_piece, shard_piece = lax.optimization_barrier((own_piece, shard_piece))
+    own_quarter = lax.all_gather(own_piece, "blk", axis=0, tiled=True)
+    far_piece, own_quarter = lax.optimization_barrier((far_piece, own_quarter))
+    far_quarter = lax.all_gather(far_piece, "blk", axis=0, tiled=True)
+    chosen = (own_quarter, far_quarter)
+    head_width = own_quarter.shape[0]
     half_rows = head_width // 2
-    own_half = lax.dynamic_slice_in_dim(chosen[0], core * half_rows, half_rows, axis=0)
+    own_half = lax.dynamic_slice_in_dim(own_quarter, core * half_rows, half_rows, axis=0)
     from_next = lax.ppermute(own_half, "dp", [(i, (i - 1) % dp_size) for i in range(dp_size)])
     from_prev = lax.ppermute(own_half, "dp", [(i, (i + 1) % dp_size) for i in range(dp_size)])
     fetched = jnp.stack([from_next, from_prev])
@@ -94,7 +95,6 @@
         prompt_kv[1].reshape(own_rows, head_count, HD),
         own_mask,
     )
-    shard_piece = lax.all_gather(kv_pool, "blk", axis=1, tiled=True)
     key_count = shard_piece.shape[1]
     page_ids = jnp.arange(key_count, dtype=jnp.int32) // PAGE
     page_used = jnp.any((row_pages[None, :] == page_ids[:, None]) & live_slots[None, :], axis=1)

time: 259 us -> 269 us (1.039)
  other arithmetic: 11 us -> 23.1 us
  waiting for transfers between devices: 133 us -> 141 us
  local copies, waits for them, and re-layouts: 49.7 us -> 44.5 us
  starting transfers between devices: 17.9 us -> 14.2 us
    all_gather x1, waiting for transfers between devices: 0.01 us -> 39.4 us  [body(): shard_piece = lax.all_gather(kv_pool, 'blk', axis=1, tiled=True)]
    ppermute x1, waiting for transfers between devices: 0.62 us -> 34.5 us  [body(): lax.ppermute(own_half, 'dp', [(i, (i - 1) % dp_size) for i in range(dp_si...]
    all_gather x1 -> x2, waiting for transfers between devices: 97.2 us -> 63.5 us  [the longest x1 63.5 us: body(): own_quarter = lax.all_gather(own_piece, 'blk', axis=0, tiled=True)]
    ppermute x1, waiting for transfers between devices: 35 us -> 2.99 us  [body(): lax.ppermute(own_half, 'dp', [(i, (i + 1) % dp_size) for i in range(dp_si...]
    another operation x1, other arithmetic: 0.92 us -> 11.9 us  [body(): quarters = jnp.stack([chosen[0], whole[0], chosen[1], whole[1]])]
    slice x1 -> x0, local copies, waits for them, and re-layouts: 5.02 us -> none  [body(): quarters = jnp.stack([chosen[0], whole[0], chosen[1], whole[1]])]
    all_to_all x1, starting transfers between devices: 14 us -> 10.3 us  [body(): pieces = lax.all_to_all(pieces, ('blk', 'mp'), 0, 0, tiled=True)]
    unnamed x19, local copies, waits for them, and re-layouts: 7.72 us -> 4.06 us
  transfers between devices with their start and end apart: 6 -> 7, of which waited for: 3 -> 4; matrix products, arithmetic and copies ran while one was open for 16% -> 18% of each run, Pallas kernels for 0% -> 0%
where the time goes in v11:
time: 269 us; the launch traced here: 267 us
  waiting for transfers between devices  141 us (52%)
  local copies, waits for them, and re-layouts  44.5 us (17%)
  other arithmetic  23.1 us (9%)
  matrix products  16.5 us (6%)
  between operations  15.3 us (6%)
  starting transfers between devices  14.2 us (5%)
  blocking collectives  12.1 us (4%)
    all_gather x1, waiting for transfers between devices, body(): own_quarter = lax.all_gather(own_piece, 'blk', axis=0, tiled=True)  63.5 us
    all_gather x1, waiting for transfers between devices, body(): shard_piece = lax.all_gather(kv_pool, 'blk', axis=1, tiled=True)  39.4 us
    ppermute x1, waiting for transfers between devices, body(): lax.ppermute(own_half, 'dp', [(i, (i - 1) % dp_size) for i in range(dp_si...  34.5 us
    slice x2, local copies, waits for them, and re-layouts, body(): shard_piece[0].reshape(key_count, head_count, HD)  12.9 us
    all_gather x1, blocking collectives, body(): lax.all_gather(trainer_q.astype(jnp.bfloat16), 'dp', axis=1, tiled=True)  12.1 us
    another operation x1, other arithmetic, body(): quarters = jnp.stack([chosen[0], whole[0], chosen[1], whole[1]])  11.9 us
    all_to_all x1, starting transfers between devices, body(): pieces = lax.all_to_all(pieces, ('blk', 'mp'), 0, 0, tiled=True)  10.3 us
    dot_general x1, matrix products, body(): jnp.einsum('tjd,jhd->th', token_quarters, quarters, preferred_element_typ...  9.74 us
  transfers between devices with their start and end apart: 7, of which 4 were waited for; matrix products, arithmetic and copies ran while one was open for 18% of the time, Pallas kernels for 0%

profile of v11, /device:TPU:25, one launch (start us, length us, event | category | flops | bytes accessed | tf_op | source)
XLA Modules:
  0.0 266.8 jit_solution(5927608644401771161)
XLA Ops:
  7.2 0.0 copy-start.5
  7.2 0.0 all-gather.4.cloned.1.call-start
  7.2 0.7 all-gather.4.cloned.1.call-update
  7.9 0.0 all-gather.6.cloned.1.call-start
  8.0 1.0 convert_element_type.18
  9.0 12.1 %all_gather.12 = bf16[56,7168]{1,0:T(8,128)(2,1)S(1)} all-gather(bf16[56,1792]{1,0:T(8,128)(2,1)S(1)} %convert_element_type.18), channel_id=1, replica_groups=mesh['dp'=4,'blk'=16,'mp'=4] {'dp'}, dimensions={1}, use_global_device_ids=true | all-gather | bytes 1003520 | tf_op jit(solution)/shard_map/all_gather | solution.py:37
  21.1 0.6 reshape.100
  21.7 0.8 constant_dynamic-slice_fusion.2
  22.6 0.7 copy.54
  23.3 39.4 %all-gather.4.cloned.1.call-done = bf16[2,2048,896]{2,1,0:T(8,128)(2,1)} async-done(((bf16[2,128,896]{2,1,0:T(8,128)(2,1)}), bf16[2,2048,896]{2,1,0:T(8,128)(2,1)}) %all-gather.4.cloned.1.call-update) | async-done | bytes 7340048 | tf_op jit(solution)/shard_map/all_gather | solution.py:39
  62.7 0.0 all-gather.6.cloned.1.call-update
  62.7 0.0 copy-done.5
  62.7 0.1 copy.53
  62.8 2.1 broadcast_in_dim.82
  64.8 10.3 %all-to-all-start = ((bf16[64,256,112]{1,2,0:T(8,128)(2,1)}), bf16[64,256,112]{1,2,0:T(8,128)(2,1)}, u32[]{:S(2)}, u32[]{:S(2)}) async-start(bf16[64,256,112]{1,2,0:T(8,128)(2,1)} %bitcast.78), calls=%async_computation | async-start | bytes 7340032 | tf_op jit(solution)/shard_map/all_to_all | solution.py:70
  75.1 0.0 all-gather.8.cloned.1.call-start
  75.2 0.7 copy.55
  75.9 63.5 %all-gather.6.cloned.1.call-done = bf16[896,1792]{1,0:T(8,128)(2,1)} async-done(((bf16[56,1792]{1,0:T(8,128)(2,1)}), bf16[896,1792]{1,0:T(8,128)(2,1)}) %all-gather.6.cloned.1.call-update) | async-done | bytes 3211280 | tf_op jit(solution)/shard_map/all_gather | solution.py:43
  139.4 0.0 copy-start.7
  139.4 2.7 %constant_dynamic-slice_fusion.1 = bf16[448,1792]{1,0:T(8,128)(2,1)} fusion(bf16[896,1792]{1,0:T(8,128)(2,1)} %all-gather.6.cloned.1.call-done, s32[]{:T(128)S(6)} %select_n.87), kind=kLoop, calls=%fused_computation.64 | loop fusion | bytes 3211268 | tf_op jit(solution)/shard_map/dynamic_slice | solution.py:49
  142.1 2.4 collective-permute-start
  144.5 0.0 collective-permute-start.1
  144.5 0.0 all-gather.8.cloned.1.call-update
  144.5 34.5 %collective-permute-done = bf16[448,1792]{1,0:T(8,128)(2,1)S(1)} collective-permute-done((bf16[448,1792]{1,0:T(8,128)(2,1)}, bf16[448,1792]{1,0:T(8,128)(2,1)S(1)}, u32[]{:S(2)}, u32[]{:S(2)}) %collective-permute-start) | collective-permute-done | bytes 1605664 | tf_op jit(solution)/shard_map/ppermute | solution.py:50
  179.0 0.0 copy-start.1
  179.0 3.0 %collective-permute-done.1 = bf16[448,1792]{1,0:T(8,128)(2,1)S(1)} collective-permute-done((bf16[448,1792]{1,0:T(8,128)(2,1)}, bf16[448,1792]{1,0:T(8,128)(2,1)S(1)}, u32[]{:S(2)}, u32[]{:S(2)}) %collective-permute-start.1) | collective-permute-done | bytes 1605664 | tf_op jit(solution)/shard_map/ppermute | solution.py:51
  182.0 0.0 copy-start.2
  182.0 2.3 pad_maximum_fusion
  184.3 1.4 collective-permute-start.2
  187.0 2.2 fusion.53
  189.1 2.0 copy.40
  191.1 2.0 copy.41
  193.1 0.0 copy-done.7
  193.2 0.2 and_reduce_fusion
  193.3 0.1 fusion.36
  193.4 0.0 all-to-all-done
  193.4 6.0 %copy.37 = bf16[256,4,1792]{2,0,1:T(8,128)(2,1)} copy(bf16[256,4,1792]{0,2,1:T(8,128)(2,1)} %bitcast.10) | data formatting | bytes 7340032 | tf_op jit(solution)/shard_map/reshape;reshape | solution.py:72
  199.5 0.0 copy-done.1
  199.5 0.0 copy-done.2
  199.5 6.7 %fusion.52 = (bf16[1,2048,896]{2,1,0:T(8,128)(2,1)}, bf16[1,2048,896]{2,1,0:T(8,128)(2,1)}) fusion(bf16[2,2048,896]{2,1,0:T(8,128)(2,1)} %all-gather.4.cloned.1.call-done), kind=kLoop, calls=%fused_computation.75 | loop fusion | bytes 14680064 | tf_op jit(solution)/shard_map/slice | solution.py:105
  206.2 6.1 %copy.43 = bf16[1,2048,896]{1,2,0:T(8,128)(2,1)} copy(bf16[1,2048,896]{2,1,0:T(8,128)(2,1)} %get-tuple-element.18) | data formatting | bytes 7340032 | tf_op jit(solution)/shard_map/slice | solution.py:105
  212.3 6.1 %copy.44 = bf16[1,2048,896]{1,2,0:T(8,128)(2,1)} copy(bf16[1,2048,896]{2,1,0:T(8,128)(2,1)} %get-tuple-element.19) | data formatting | bytes 7340032 | tf_op jit(solution)/shard_map/slice | solution.py:106
  218.5 0.0 collective-permute-done.2
  218.5 3.1 %broadcast_select_fusion.1 = (bf16[2,448,1792]{2,1,0:T(8,128)(2,1)S(1)}, bf16[2,448,1792]{2,1,0:T(8,128)(2,1)S(1)}) fusion(bf16[2,448,1792]{2,1,0:T(8,128)(2,1)} %collective-permute-done.2, pred[]{:T(512)S(6)} %eq.24, bf16[1,448,1792]{2,1,0:T(8,128)(2,1)} %bitcast.84, bf16[1,448,1792]{2,1,0:T(8,128)(2,1)} %bitcast.82), kind=kLoop, calls=%fused_computation.21 | loop fusion | flops 4816896 | bytes 12845057 | tf_op jit(solution)/shard_map/jit(_where)/select_n | solution.py:54
  221.5 0.0 copy-start
  221.5 1.6 copy-done
  223.2 1.9 fusion.13
  225.1 11.9 %fusion.3 = bf16[4,896,1792]{2,1,0:T(8,128)(2,1)} fusion(bf16[2,448,1792]{2,1,0:T(8,128)(2,1)} %copy-done, bf16[2,448,1792]{2,1,0:T(8,128)(2,1)S(1)} %get-tuple-element.20, bf16[1,896,1792]{2,1,0:T(8,128)(2,1)} %bitcast.89, bf16[1,896,1792]{2,1,0:T(8,128)(2,1)} %fusion.13, bf16[1,896,1792]{2,1,0:T(8,128)(2,1)} %bitcast.80), kind=kLoop, calls=%fused_computation.4 | loop fusion | flops 83492864 | bytes 28901376 | tf_op jit(solution)/shard_map/stack | solution.py:57
  237.0 9.7 %fusion.26 = bf16[256,896]{1,0:T(8,128)(2,1)S(1)} fusion(bf16[4,896,1792]{2,1,0:T(8,128)(2,1)} %fusion.3, s32[]{:T(128)S(6)} %select_n.95, bf16[256,4,1792]{2,0,1:T(8,128)(2,1)} %copy.37), kind=kOutput, calls=%fused_computation.32 | convolution fusion | flops 3290398720 | bytes 16973828 | tf_op jit(solution)/shard_map/tjd,jhd->th/dot_general | solution.py:75
  246.7 0.2 copy.39
  247.0 0.0 copy-start.4
  247.0 3.9 %fusion.4 = (f32[4,256]{1,0:T(4,128)S(1)}, f32[4,256,2048]{2,1,0:T(8,128)S(1)}) fusion(pred[2048]{0:T(1024)(128)(4,1)S(1)} %and_reduce_fusion, bf16[256,4,224]{0,2,1:T(8,128)(2,1)S(1)} %bitcast.85, bf16[2048,4,224]{0,2,1:T(8,128)(2,1)} %bitcast.79), kind=kOutput, calls=%fused_computation.7 | convolution fusion | flops 945814528 | bytes 12523520 | tf_op jit(solution)/shard_map/thd,khd->htk/dot_general | solution.py:12
  250.8 0.0 copy-done.4
  250.8 0.4 fusion.54
  251.2 2.4 fusion.5
  253.7 0.0 copy-done.3
  253.7 0.0 copy-start.6
  253.7 2.1 fusion.18
  255.8 0.2 fusion.30
  256.1 0.0 copy-done.6
  256.1 0.4 fusion.29
  256.5 1.0 copy.45
  257.5 1.6 constant_dynamic-slice_fusion
  259.0 1.2 copy.35
  (7 shorter events, 0.0 us)
Async XLA Ops:
  7.2 55.5 %copy-start.5 = (bf16[4096,112]{0,1:T(8,128)(2,1)S(1)}, bf16[4096,112]{0,1:T(8,128)(2,1)}, u32[]{:S(2)}) copy-start(bf16[4096,112]{0,1:T(8,128)(2,1)} %param.7) | copy-start | bytes 2752516
  7.2 55.5 %all-gather.4.cloned.1.call-start = ((), (), s32[]{:S(2)}) async-start(), calls=%async_computation.1 | async-start | bytes 7798784 | tf_op jit(solution)/shard_map/all_gather | solution.py:39
  7.9 131.5 %all-gather.6.cloned.1.call-start = ((), (), s32[]{:S(2)}) async-start(), calls=%async_computation.2 | async-start | bytes 3411968 | tf_op jit(solution)/shard_map/all_gather | solution.py:43
  64.8 128.6 %all-to-all-start = ((bf16[64,256,112]{1,2,0:T(8,128)(2,1)}), bf16[64,256,112]{1,2,0:T(8,128)(2,1)}, u32[]{:S(2)}, u32[]{:S(2)}) async-start(bf16[64,256,112]{1,2,0:T(8,128)(2,1)} %bitcast.78), calls=%async_computation | async-start | bytes 7340032 | tf_op jit(solution)/shard_map/all_to_all | solution.py:70
  75.1 150.0 %all-gather.8.cloned.1.call-start = ((), (), s32[]{:S(2)}) async-start(), calls=%async_computation.3 | async-start | bytes 3411968 | tf_op jit(solution)/shard_map/all_gather | solution.py:45
  139.4 53.8 %copy-start.7 = (s32[1,64]{1,0:T(1,128)S(1)}, s32[1,64]{1,0:T(1,128)}, u32[]{:S(2)}) copy-start(s32[1,64]{1,0:T(1,128)} %param.11) | copy-start | bytes 772
  142.1 36.9 %collective-permute-start = (bf16[448,1792]{1,0:T(8,128)(2,1)}, bf16[448,1792]{1,0:T(8,128)(2,1)S(1)}, u32[]{:S(2)}, u32[]{:S(2)}) collective-permute-start(bf16[448,1792]{1,0:T(8,128)(2,1)} %constant_dynamic-slice_fusion.1), channel_id=1, source_target_pairs={{0,192},{64,0},{128,64},{192,128},{1,193},{65,1},{129,65},{193,129... | collective-permute-start | bytes 4816904 | tf_op jit(solution)/shard_map/ppermute | solution.py:50
  144.5 37.5 %collective-permute-start.1 = (bf16[448,1792]{1,0:T(8,128)(2,1)}, bf16[448,1792]{1,0:T(8,128)(2,1)S(1)}, u32[]{:S(2)}, u32[]{:S(2)}) collective-permute-start(bf16[448,1792]{1,0:T(8,128)(2,1)} %constant_dynamic-slice_fusion.1), channel_id=1, source_target_pairs={{0,64},{64,128},{128,192},{192,0},{1,65},{65,129},{129,193},{193,1... | collective-permute-start | bytes 4816904 | tf_op jit(solution)/shard_map/ppermute | solution.py:51
  179.0 20.5 %copy-start.1 = (bf16[448,1792]{1,0:T(8,128)(2,1)}, bf16[448,1792]{1,0:T(8,128)(2,1)S(1)}, u32[]{:S(2)}) copy-start(bf16[448,1792]{1,0:T(8,128)(2,1)S(1)} %collective-permute-done) | copy-start | bytes 4816900
  182.0 17.5 %copy-start.2 = (bf16[448,1792]{1,0:T(8,128)(2,1)}, bf16[448,1792]{1,0:T(8,128)(2,1)S(1)}, u32[]{:S(2)}) copy-start(bf16[448,1792]{1,0:T(8,128)(2,1)S(1)} %collective-permute-done.1) | copy-start | bytes 4816900
  184.3 34.2 %collective-permute-start.2 = (bf16[2,448,1792]{2,1,0:T(8,128)(2,1)}, bf16[2,448,1792]{2,1,0:T(8,128)(2,1)}, u32[]{:S(2)}, u32[]{:S(2)}) collective-permute-start(bf16[2,448,1792]{2,1,0:T(8,128)(2,1)} %pad_maximum_fusion), channel_id=1, source_target_pairs={{0,4},{4,0},{8,12},{12,8},{16,20},{20,16},{24,28},{28,24},{32,36},... | collective-permute-start | bytes 9633800 | tf_op jit(solution)/shard_map/ppermute | solution.py:53
  221.5 1.7 copy-start
  247.0 3.9 %copy-start.4 = (bf16[1,256,896]{1,2,0:T(8,128)(2,1)S(1)}, bf16[1,256,896]{1,2,0:T(8,128)(2,1)}, u32[]{:S(2)}) copy-start(bf16[1,256,896]{1,2,0:T(8,128)(2,1)} %copy.40) | copy-start | bytes 1376260
  250.8 2.8 %copy-start.3 = (bf16[1,2048,896]{1,2,0:T(8,128)(2,1)S(1)}, bf16[1,2048,896]{1,2,0:T(8,128)(2,1)}, u32[]{:S(2)}) copy-start(bf16[1,2048,896]{1,2,0:T(8,128)(2,1)} %copy.44) | copy-start | bytes 11010052
  253.7 2.4 copy-start.6
Sparse Core Ops, SparseCore 0:
  9.8 52.8 all-gather.3
  65.1 74.2 all-gather.5
  144.6 46.9 all-gather.7

commit v12 on v11

--- a/solution.py
+++ b/solution.py
@@ -1,6 +1,8 @@
 import jax
 import jax.numpy as jnp
 from jax import lax
+from jax.experimental import pallas as pl
+from jax.experimental.pallas import tpu as pltpu
 from jax.sharding import PartitionSpec as P
 
 HD = 224
@@ -26,6 +28,37 @@
     return (new_max, row_total, weighted)
 
 
+def mate_swap_kernel(x_ref, out_ref, send_sem, recv_sem):
+    g = lax.axis_index("dp")
+    b = lax.axis_index("blk")
+    m = lax.axis_index("mp")
+    mate = b + 1 - 2 * (b % 2)
+    barrier = pltpu.get_barrier_semaphore()
+    pl.semaphore_signal(barrier, inc=1, device_id=(g, mate, m), device_id_type=pl.DeviceIdType.MESH)
+    pl.semaphore_wait(barrier, 1)
+    copy = pltpu.make_async_remote_copy(
+        src_ref=x_ref,
+        dst_ref=out_ref,
+        send_sem=send_sem,
+        recv_sem=recv_sem,
+        device_id=(g, mate, m),
+        device_id_type=pl.DeviceIdType.MESH,
+    )
+    copy.start()
+    copy.wait()
+
+
+def swap_with_mate(x):
+    return pl.pallas_call(
+        mate_swap_kernel,
+        out_shape=jax.ShapeDtypeStruct(x.shape, x.dtype),
+        in_specs=[pl.BlockSpec(memory_space=pl.ANY)],
+        out_specs=pl.BlockSpec(memory_space=pl.ANY),
+        scratch_shapes=[pltpu.SemaphoreType.DMA(()), pltpu.SemaphoreType.DMA(())],
+        compiler_params=pltpu.CompilerParams(collective_id=0, has_side_effects=True),
+    )(x)
+
+
 def body(tokens, trainer_q, kv_pool, prompt_kv, page_table, page_count, prompt_len):
     blk_size = lax.axis_size("blk")
     mp_size = lax.axis_size("mp")
@@ -39,7 +72,13 @@
     shard_piece = lax.all_gather(kv_pool, "blk", axis=1, tiled=True)
     own_piece = lax.dynamic_index_in_dim(trainer_rows, g, 1, keepdims=False)
     far_piece = lax.dynamic_index_in_dim(trainer_rows, (g + 2) % dp_size, 1, keepdims=False)
-    own_piece, shard_piece = lax.optimization_barrier((own_piece, shard_piece))
+    group_rows, piece_cols = tokens.shape
+    own_rows = group_rows // blk_size
+    pieces = tokens.reshape(blk_size, 1, own_rows, piece_cols)
+    pieces = jnp.broadcast_to(pieces, (blk_size, mp_size, own_rows, piece_cols))
+    pieces = pieces.reshape(blk_size * mp_size, own_rows, piece_cols)
+    pieces = lax.all_to_all(pieces, ("blk", "mp"), 0, 0, tiled=True)
+    own_piece, shard_piece, pieces = lax.optimization_barrier((own_piece, shard_piece, pieces))
     own_quarter = lax.all_gather(own_piece, "blk", axis=0, tiled=True)
     far_piece, own_quarter = lax.optimization_barrier((far_piece, own_quarter))
     far_quarter = lax.all_gather(far_piece, "blk", axis=0, tiled=True)
@@ -50,7 +89,7 @@
     from_next = lax.ppermute(own_half, "dp", [(i, (i - 1) % dp_size) for i in range(dp_size)])
     from_prev = lax.ppermute(own_half, "dp", [(i, (i + 1) % dp_size) for i in range(dp_size)])
     fetched = jnp.stack([from_next, from_prev])
-    mate = lax.ppermute(fetched, "blk", [(i, i ^ 1) for i in range(blk_size)])
+    mate = swap_with_mate(fetched)
     first = jnp.where(core == 0, fetched, mate)
     second = jnp.where(core == 0, mate, fetched)
     whole = jnp.concatenate([first, second], axis=1)
@@ -62,12 +101,6 @@
         ((b // blocks_per_quarter - g) % dp_size, 0, (b % blocks_per_quarter) * block_cols),
         (1, head_width, block_cols),
     )[0]
-    group_rows, piece_cols = tokens.shape
-    own_rows = group_rows // blk_size
-    pieces = tokens.reshape(blk_size, 1, own_rows, piece_cols)
-    pieces = jnp.broadcast_to(pieces, (blk_size, mp_size, own_rows, piece_cols))
-    pieces = pieces.reshape(blk_size * mp_size, own_rows, piece_cols)
-    pieces = lax.all_to_all(pieces, ("blk", "mp"), 0, 0, tiled=True)
     token_local = jnp.transpose(pieces, (1, 0, 2)).reshape(own_rows, -1)
     token_quarters = token_local.reshape(own_rows, dp_size, quarter_cols)
     token_quarters = jnp.concatenate([token_quarters, token_quarters], axis=1)

time: 269 us -> 282 us (1.048)
  Pallas kernels: 0 us -> 7.14 us
  waiting for transfers between devices: 141 us -> 144 us
    all_to_all x1, waiting for transfers between devices: 0.01 us -> 100 us  [body(): pieces = lax.all_to_all(pieces, ('blk', 'mp'), 0, 0, tiled=True)]
    all_gather x1, waiting for transfers between devices: 39.4 us -> 0.01 us  [body(): shard_piece = lax.all_gather(kv_pool, 'blk', axis=1, tiled=True)]
    ppermute x1, waiting for transfers between devices: 34.5 us -> 2.75 us  [body(): lax.ppermute(own_half, 'dp', [(i, (i - 1) % dp_size) for i in range(dp_si...]
    all_gather x1, waiting for transfers between devices: 63.5 us -> 37.6 us  [body(): own_quarter = lax.all_gather(own_piece, 'blk', axis=0, tiled=True)]
    pallas_call x0 -> x1, Pallas kernels: none -> 7.14 us  [swap_with_mate(): pl.pallas_call(mate_swap_kernel, out_shape=jax.ShapeDtypeStruct(x.shape,...]
  transfers between devices with their start and end apart: 7 -> 6, of which waited for: 4 -> 4; matrix products, arithmetic and copies ran while one was open for 18% -> 17% of each run, Pallas kernels for 0% -> 3%
where the time goes in v12:
time: 282 us; the launch traced here: 279 us
  waiting for transfers between devices  144 us (51%)
  local copies, waits for them, and re-layouts  46.1 us (16%)
  other arithmetic  22.1 us (8%)
  matrix products  16.5 us (6%)
  between operations  15.3 us (5%)
  starting transfers between devices  14.9 us (5%)
  blocking collectives  12.5 us (4%)
  Pallas kernels  7.14 us (3%)
    all_to_all x1, waiting for transfers between devices, body(): pieces = lax.all_to_all(pieces, ('blk', 'mp'), 0, 0, tiled=True)  100 us
    all_gather x1, waiting for transfers between devices, body(): own_quarter = lax.all_gather(own_piece, 'blk', axis=0, tiled=True)  37.6 us
    slice x2, local copies, waits for them, and re-layouts, body(): shard_piece[0].reshape(key_count, head_count, HD)  13.1 us
    all_gather x1, blocking collectives, body(): lax.all_gather(trainer_q.astype(jnp.bfloat16), 'dp', axis=1, tiled=True)  12.5 us
    all_to_all x1, starting transfers between devices, body(): pieces = lax.all_to_all(pieces, ('blk', 'mp'), 0, 0, tiled=True)  12.4 us
    another operation x1, other arithmetic, body(): quarters = jnp.stack([chosen[0], whole[0], chosen[1], whole[1]])  11.9 us
    dot_general x1, matrix products, body(): jnp.einsum('tjd,jhd->th', token_quarters, quarters, preferred_element_typ...  9.75 us
    pallas_call x1, Pallas kernels, swap_with_mate(): pl.pallas_call(mate_swap_kernel, out_shape=jax.ShapeDtypeStruct(x.shape,...  7.14 us
  transfers between devices with their start and end apart: 6, of which 4 were waited for; matrix products, arithmetic and copies ran while one was open for 17% of the time, Pallas kernels for 3%

profile of v12, /device:TPU:25, one launch (start us, length us, event | category | flops | bytes accessed | tf_op | source)
XLA Modules:
  0.0 278.8 jit_solution(300950074495948162)
XLA Ops:
  7.2 0.0 all-gather.4.cloned.1.call-start
  7.2 0.7 all-gather.4.cloned.1.call-update
  7.9 1.2 copy.53
  9.1 0.0 copy-start.6
  9.2 2.2 broadcast_in_dim.79
  11.3 12.4 %all-to-all-start = ((bf16[64,256,112]{1,2,0:T(8,128)(2,1)}), bf16[64,256,112]{1,2,0:T(8,128)(2,1)}, u32[]{:S(2)}, u32[]{:S(2)}) async-start(bf16[64,256,112]{1,2,0:T(8,128)(2,1)} %bitcast.78), calls=%async_computation | async-start | bytes 7340032 | tf_op jit(solution)/shard_map/all_to_all | solution.py:80
  23.7 0.0 all-gather.6.cloned.1.call-start
  23.8 0.0 copy-done.6
  23.8 0.0 copy-start.7
  23.9 12.5 %all_gather.12 = bf16[56,7168]{1,0:T(8,128)(2,1)S(1)} all-gather(bf16[56,1792]{1,0:T(8,128)(2,1)S(1)} %convert_element_type.18), channel_id=1, replica_groups=mesh['dp'=4,'blk'=16,'mp'=4] {'dp'}, dimensions={1}, use_global_device_ids=true | all-gather | bytes 1003520 | tf_op jit(solution)/shard_map/all_gather | solution.py:70
  36.3 0.6 reshape.100
  36.9 0.8 constant_dynamic-slice_fusion.2
  37.8 0.7 copy.54
  38.5 100.2 %all-to-all-done = bf16[64,256,112]{1,2,0:T(8,128)(2,1)} async-done(((bf16[64,256,112]{1,2,0:T(8,128)(2,1)}), bf16[64,256,112]{1,2,0:T(8,128)(2,1)}, u32[]{:S(2)}, u32[]{:S(2)}) %all-to-all-start) | async-done | bytes 3670048 | tf_op jit(solution)/shard_map/all_to_all | solution.py:80
  138.7 0.0 all-gather.4.cloned.1.call-done
  138.7 0.0 all-gather.6.cloned.1.call-update
  138.7 0.0 all-gather.8.cloned.1.call-start
  138.7 0.7 copy.55
  139.5 37.6 %all-gather.6.cloned.1.call-done = bf16[896,1792]{1,0:T(8,128)(2,1)} async-done(((bf16[56,1792]{1,0:T(8,128)(2,1)}), bf16[896,1792]{1,0:T(8,128)(2,1)}) %all-gather.6.cloned.1.call-update) | async-done | bytes 3211280 | tf_op jit(solution)/shard_map/all_gather | solution.py:82
  177.0 0.0 all-gather.8.cloned.1.call-update
  178.4 2.7 constant_dynamic-slice_fusion.1
  181.1 2.4 collective-permute-start
  183.5 0.0 collective-permute-start.1
  183.5 2.1 fusion.53
  185.7 2.0 copy.40
  187.7 2.0 copy.41
  189.7 0.0 copy-done.7
  189.7 0.2 and_reduce_fusion
  189.9 0.1 fusion.36
  190.0 6.0 %copy.37 = bf16[256,4,1792]{2,0,1:T(8,128)(2,1)} copy(bf16[256,4,1792]{0,2,1:T(8,128)(2,1)} %bitcast.10) | data formatting | bytes 7340032 | tf_op jit(solution)/shard_map/reshape;reshape | solution.py:105
  196.0 7.0 %fusion.52 = (bf16[1,2048,896]{2,1,0:T(8,128)(2,1)}, bf16[1,2048,896]{2,1,0:T(8,128)(2,1)}) fusion(bf16[2,2048,896]{2,1,0:T(8,128)(2,1)} %all-gather.4.cloned.1.call-done), kind=kLoop, calls=%fused_computation.75 | loop fusion | bytes 14680064 | tf_op jit(solution)/shard_map/slice | solution.py:138
  203.0 6.1 %copy.43 = bf16[1,2048,896]{1,2,0:T(8,128)(2,1)} copy(bf16[1,2048,896]{2,1,0:T(8,128)(2,1)} %get-tuple-element.20) | data formatting | bytes 7340032 | tf_op jit(solution)/shard_map/slice | solution.py:138
  209.1 6.2 %copy.44 = bf16[1,2048,896]{1,2,0:T(8,128)(2,1)} copy(bf16[1,2048,896]{2,1,0:T(8,128)(2,1)} %get-tuple-element.21) | data formatting | bytes 7340032 | tf_op jit(solution)/shard_map/slice | solution.py:139
  215.3 2.7 collective-permute-done
  218.1 0.0 copy-start.1
  218.1 3.0 %collective-permute-done.1 = bf16[448,1792]{1,0:T(8,128)(2,1)S(1)} collective-permute-done((bf16[448,1792]{1,0:T(8,128)(2,1)}, bf16[448,1792]{1,0:T(8,128)(2,1)S(1)}, u32[]{:S(2)}, u32[]{:S(2)}) %collective-permute-start.1) | collective-permute-done | bytes 1605664 | tf_op jit(solution)/shard_map/ppermute | solution.py:90
  221.1 0.0 copy-start.2
  221.1 2.3 pad_maximum_fusion.x_ref
  223.4 0.0 copy-done.1
  223.4 0.1 copy-done.2
  223.4 7.1 %shard_map.86 = bf16[2,448,1792]{2,1,0:T(8,128)(2,1)} custom-call(bf16[2,448,1792]{2,1,0:T(8,128)(2,1)} %pad_maximum_fusion.x_ref), custom_call_target="tpu_custom_call" | custom-call | tf_op jit(solution)/shard_map/pallas_call | solution.py:52
  230.6 3.1 %broadcast_select_fusion.1 = (bf16[2,448,1792]{2,1,0:T(8,128)(2,1)S(1)}, bf16[2,448,1792]{2,1,0:T(8,128)(2,1)S(1)}) fusion(bf16[2,448,1792]{2,1,0:T(8,128)(2,1)} %shard_map.86, pred[]{:T(512)S(6)} %eq.24, bf16[1,448,1792]{2,1,0:T(8,128)(2,1)} %bitcast.84, bf16[1,448,1792]{2,1,0:T(8,128)(2,1)} %bitcast.82), kind=kLoop, calls=%fused_computation.21 | loop fusion | flops 4816896 | bytes 12845057 | tf_op jit(solution)/shard_map/jit(_where)/select_n | solution.py:93
  233.7 0.0 copy-start
  233.7 1.6 copy-done
  235.3 1.8 fusion.13
  237.1 0.0 all-gather.8.cloned.1.call-done
  237.1 11.9 %fusion.3 = bf16[4,896,1792]{2,1,0:T(8,128)(2,1)} fusion(bf16[2,448,1792]{2,1,0:T(8,128)(2,1)} %copy-done, bf16[2,448,1792]{2,1,0:T(8,128)(2,1)S(1)} %get-tuple-element.22, bf16[1,896,1792]{2,1,0:T(8,128)(2,1)} %bitcast.89, bf16[1,896,1792]{2,1,0:T(8,128)(2,1)} %fusion.13, bf16[1,896,1792]{2,1,0:T(8,128)(2,1)} %bitcast.80), kind=kLoop, calls=%fused_computation.4 | loop fusion | flops 83492864 | bytes 28901376 | tf_op jit(solution)/shard_map/stack | solution.py:96
  249.0 9.7 %fusion.26 = bf16[256,896]{1,0:T(8,128)(2,1)S(1)} fusion(bf16[4,896,1792]{2,1,0:T(8,128)(2,1)} %fusion.3, s32[]{:T(128)S(6)} %select_n.95, bf16[256,4,1792]{2,0,1:T(8,128)(2,1)} %copy.37), kind=kOutput, calls=%fused_computation.32 | convolution fusion | flops 3290398720 | bytes 16973828 | tf_op jit(solution)/shard_map/tjd,jhd->th/dot_general | solution.py:108
  258.8 0.2 copy.39
  259.0 0.0 copy-start.4
  259.0 3.9 %fusion.4 = (f32[4,256]{1,0:T(4,128)S(1)}, f32[4,256,2048]{2,1,0:T(8,128)S(1)}) fusion(pred[2048]{0:T(1024)(128)(4,1)S(1)} %and_reduce_fusion, bf16[256,4,224]{0,2,1:T(8,128)(2,1)S(1)} %bitcast.85, bf16[2048,4,224]{0,2,1:T(8,128)(2,1)} %bitcast.79), kind=kOutput, calls=%fused_computation.7 | convolution fusion | flops 945814528 | bytes 12523520 | tf_op jit(solution)/shard_map/thd,khd->htk/dot_general | solution.py:14
  262.9 0.0 copy-start.3
  262.9 0.0 copy-done.4
  262.9 0.4 fusion.54
  263.3 2.4 fusion.5
  265.7 0.0 copy-done.3
  265.7 0.0 copy-start.5
  265.7 2.1 fusion.18
  267.9 0.2 fusion.30
  268.1 0.0 copy-done.5
  268.1 0.4 fusion.29
  268.5 1.0 copy.45
  269.5 1.6 constant_dynamic-slice_fusion
  271.1 1.2 copy.36
  (6 shorter events, 0.1 us)
Async XLA Ops:
  7.2 131.5 %all-gather.4.cloned.1.call-start = ((), (), s32[]{:S(2)}) async-start(), calls=%async_computation.1 | async-start | bytes 7798784 | tf_op jit(solution)/shard_map/all_gather | solution.py:72
  9.1 14.7 %copy-start.6 = (f32[56,1792]{1,0:T(8,128)S(1)}, f32[56,1792]{1,0:T(8,128)}, u32[]{:S(2)}) copy-start(f32[56,1792]{1,0:T(8,128)} %param.8) | copy-start | bytes 1204228
  11.3 127.3 %all-to-all-start = ((bf16[64,256,112]{1,2,0:T(8,128)(2,1)}), bf16[64,256,112]{1,2,0:T(8,128)(2,1)}, u32[]{:S(2)}, u32[]{:S(2)}) async-start(bf16[64,256,112]{1,2,0:T(8,128)(2,1)} %bitcast.78), calls=%async_computation | async-start | bytes 7340032 | tf_op jit(solution)/shard_map/all_to_all | solution.py:80
  23.7 153.3 %all-gather.6.cloned.1.call-start = ((), (), s32[]{:S(2)}) async-start(), calls=%async_computation.2 | async-start | bytes 3411968 | tf_op jit(solution)/shard_map/all_gather | solution.py:82
  23.8 165.9 %copy-start.7 = (s32[1,64]{1,0:T(1,128)S(1)}, s32[1,64]{1,0:T(1,128)}, u32[]{:S(2)}) copy-start(s32[1,64]{1,0:T(1,128)} %param.11) | copy-start | bytes 772
  138.7 98.4 %all-gather.8.cloned.1.call-start = ((), (), s32[]{:S(2)}) async-start(), calls=%async_computation.3 | async-start | bytes 3411968 | tf_op jit(solution)/shard_map/all_gather | solution.py:84
  181.1 37.0 %collective-permute-start = (bf16[448,1792]{1,0:T(8,128)(2,1)}, bf16[448,1792]{1,0:T(8,128)(2,1)S(1)}, u32[]{:S(2)}, u32[]{:S(2)}) collective-permute-start(bf16[448,1792]{1,0:T(8,128)(2,1)} %constant_dynamic-slice_fusion.1), channel_id=1, source_target_pairs={{0,192},{64,0},{128,64},{192,128},{1,193},{65,1},{129,65},{193,129... | collective-permute-start | bytes 4816904 | tf_op jit(solution)/shard_map/ppermute | solution.py:89
  183.5 37.5 %collective-permute-start.1 = (bf16[448,1792]{1,0:T(8,128)(2,1)}, bf16[448,1792]{1,0:T(8,128)(2,1)S(1)}, u32[]{:S(2)}, u32[]{:S(2)}) collective-permute-start(bf16[448,1792]{1,0:T(8,128)(2,1)} %constant_dynamic-slice_fusion.1), channel_id=1, source_target_pairs={{0,64},{64,128},{128,192},{192,0},{1,65},{65,129},{129,193},{193,1... | collective-permute-start | bytes 4816904 | tf_op jit(solution)/shard_map/ppermute | solution.py:90
  218.1 5.3 %copy-start.1 = (bf16[448,1792]{1,0:T(8,128)(2,1)}, bf16[448,1792]{1,0:T(8,128)(2,1)S(1)}, u32[]{:S(2)}) copy-start(bf16[448,1792]{1,0:T(8,128)(2,1)S(1)} %collective-permute-done) | copy-start | bytes 4816900
  221.1 2.4 copy-start.2
  233.7 1.6 copy-start
  259.0 3.9 %copy-start.4 = (bf16[1,256,896]{1,2,0:T(8,128)(2,1)S(1)}, bf16[1,256,896]{1,2,0:T(8,128)(2,1)}, u32[]{:S(2)}) copy-start(bf16[1,256,896]{1,2,0:T(8,128)(2,1)} %copy.40) | copy-start | bytes 1376260
  262.9 2.8 %copy-start.3 = (bf16[1,2048,896]{1,2,0:T(8,128)(2,1)S(1)}, bf16[1,2048,896]{1,2,0:T(8,128)(2,1)}, u32[]{:S(2)}) copy-start(bf16[1,2048,896]{1,2,0:T(8,128)(2,1)} %copy.44) | copy-start | bytes 11010052
  265.7 2.4 copy-start.5
Sparse Core Ops, SparseCore 0:
  9.8 123.3 all-gather.3
  138.8 38.1 all-gather.5
  178.9 38.3 all-gather.7

commit v13 on v1

--- a/solution.py
+++ b/solution.py
@@ -1,6 +1,8 @@
 import jax
 import jax.numpy as jnp
 from jax import lax
+from jax.experimental import pallas as pl
+from jax.experimental.pallas import tpu as pltpu
 from jax.sharding import PartitionSpec as P
 
 HD = 224
@@ -24,6 +26,93 @@
         preferred_element_type=jnp.float32,
     )
     return (new_max, row_total, weighted)
+
+
+def kv_gather_kernel(piece_ref, out_ref, local_sem, send_sems, recv_sems, fwd_send, fwd_recv):
+    chips = lax.axis_size("blk") // 2
+    g = lax.axis_index("dp")
+    b = lax.axis_index("blk")
+    m = lax.axis_index("mp")
+    c = b // 2
+    k = b % 2
+    mate = 2 * c + 1 - k
+
+    def peer(j):
+        return (g, 2 * ((c + j) % chips) + k, m)
+
+    def source(j):
+        return 2 * ((c + chips - j) % chips) + k
+
+    def mate_slot(j):
+        return 2 * ((c + chips - j) % chips) + 1 - k
+
+    barrier = pltpu.get_barrier_semaphore()
+    for j in range(1, chips):
+        pl.semaphore_signal(barrier, inc=1, device_id=peer(j), device_id_type=pl.DeviceIdType.MESH)
+    pl.semaphore_signal(barrier, inc=1, device_id=(g, mate, m), device_id_type=pl.DeviceIdType.MESH)
+    pl.semaphore_wait(barrier, chips)
+    local = pltpu.make_async_copy(piece_ref, out_ref.at[b], local_sem)
+    local.start()
+    sends = []
+    for j in range(1, chips):
+        copy = pltpu.make_async_remote_copy(
+            src_ref=piece_ref, dst_ref=out_ref.at[b], send_sem=send_sems.at[j],
+            recv_sem=recv_sems.at[j], device_id=peer(j), device_id_type=pl.DeviceIdType.MESH,
+        )
+        copy.start()
+        sends.append(copy)
+    to_mate = pltpu.make_async_remote_copy(
+        src_ref=piece_ref, dst_ref=out_ref.at[b], send_sem=send_sems.at[0],
+        recv_sem=recv_sems.at[0], device_id=(g, mate, m), device_id_type=pl.DeviceIdType.MESH,
+    )
+    to_mate.start()
+    forwards = []
+    for j in range(1, chips):
+        pltpu.make_async_remote_copy(
+            src_ref=piece_ref, dst_ref=out_ref.at[source(j)], send_sem=send_sems.at[j],
+            recv_sem=recv_sems.at[j], device_id=peer(j), device_id_type=pl.DeviceIdType.MESH,
+        ).wait_recv()
+        copy = pltpu.make_async_remote_copy(
+            src_ref=out_ref.at[source(j)], dst_ref=out_ref.at[source(j)], send_sem=fwd_send.at[j],
+            recv_sem=fwd_recv.at[j], device_id=(g, mate, m), device_id_type=pl.DeviceIdType.MESH,
+        )
+        copy.start()
+        forwards.append(copy)
+    local.wait()
+    for copy in sends:
+        copy.wait_send()
+    to_mate.wait_send()
+    pltpu.make_async_remote_copy(
+        src_ref=piece_ref, dst_ref=out_ref.at[mate], send_sem=send_sems.at[0],
+        recv_sem=recv_sems.at[0], device_id=(g, mate, m), device_id_type=pl.DeviceIdType.MESH,
+    ).wait_recv()
+    for copy in forwards:
+        copy.wait_send()
+    for j in range(1, chips):
+        pltpu.make_async_remote_copy(
+            src_ref=out_ref.at[mate_slot(j)], dst_ref=out_ref.at[mate_slot(j)], send_sem=fwd_send.at[j],
+            recv_sem=fwd_recv.at[j], device_id=(g, mate, m), device_id_type=pl.DeviceIdType.MESH,
+        ).wait_recv()
+
+
+def gather_kv(piece):
+    n = lax.axis_size("blk")
+    chips = n // 2
+    out = pl.pallas_call(
+        kv_gather_kernel,
+        out_shape=jax.ShapeDtypeStruct((n,) + piece.shape, piece.dtype),
+        in_specs=[pl.BlockSpec(memory_space=pl.ANY)],
+        out_specs=pl.BlockSpec(memory_space=pl.ANY),
+        scratch_shapes=[
+            pltpu.SemaphoreType.DMA(()),
+            pltpu.SemaphoreType.DMA((chips,)),
+            pltpu.SemaphoreType.DMA((chips,)),
+            pltpu.SemaphoreType.DMA((chips,)),
+            pltpu.SemaphoreType.DMA((chips,)),
+        ],
+        compiler_params=pltpu.CompilerParams(collective_id=0, has_side_effects=True),
+    )(piece)
+    return jnp.moveaxis(out, 0, 1).reshape(piece.shape[0], n * piece.shape[1], piece.shape[2])
 
 
 def body(tokens, trainer_q, kv_pool, prompt_kv, page_table, page_count, prompt_len):
@@ -66,7 +155,7 @@
         prompt_kv[1].reshape(own_rows, head_count, HD),
         own_mask,
     )
-    shard_piece = lax.all_gather(kv_pool, "blk", axis=1, tiled=True)
+    shard_piece = gather_kv(kv_pool)
     key_count = shard_piece.shape[1]
     page_ids = jnp.arange(key_count, dtype=jnp.int32) // PAGE
     page_used = jnp.any((row_pages[None, :] == page_ids[:, None]) & live_slots[None, :], axis=1)

time: 234 us -> 282 us (1.21)
  Pallas kernels: 0 us -> 182 us
  waiting for transfers between devices: 142 us -> 0.04 us
  local copies, waits for them, and re-layouts: 27.1 us -> 35.5 us
    pallas_call x0 -> x1, Pallas kernels: none -> 182 us  [gather_kv(): pl.pallas_call(kv_gather_kernel, out_shape=jax.ShapeDtypeStruct((n,) + pi...]
    all_gather x1, waiting for transfers between devices: 71.3 us -> 0.02 us  [body(): head_weights = lax.all_gather(trainer_rows, 'blk', axis=0, tiled=True)]
    all_gather x1 -> x0, waiting for transfers between devices: 69.7 us -> none  [body(): shard_piece = lax.all_gather(kv_pool, 'blk', axis=1, tiled=True)]
    another operation x0 -> x2, local copies, waits for them, and re-layouts: none -> 20.3 us  [the longest x1 10.2 us: body(): shard_piece[0].reshape(key_count, head_count, HD)]
    slice x1 -> x0, local copies, waits for them, and re-layouts: 6.21 us -> none  [body(): shard_piece[1].reshape(key_count, head_count, HD)]
    slice x2 -> x1, local copies, waits for them, and re-layouts: 12.9 us -> 7.13 us  [body(): shard_piece[0].reshape(key_count, head_count, HD)]
  transfers between devices with their start and end apart: 3 -> 2, of which waited for: 2 -> 0; matrix products, arithmetic and copies ran while one was open for 12% -> 12% of each run, Pallas kernels for 0% -> 65%
where the time goes in v13:
time: 282 us
  Pallas kernels  182 us (65%)
  local copies, waits for them, and re-layouts  35.5 us (13%)
  matrix products  18.1 us (6%)
  between operations  15.5 us (5%)
  starting transfers between devices  14.3 us (5%)
  blocking collectives  12.5 us (4%)
  other arithmetic  3.99 us (1%)
    pallas_call x1, Pallas kernels, gather_kv(): pl.pallas_call(kv_gather_kernel, out_shape=jax.ShapeDtypeStruct((n,) + pi...  182 us
    all_to_all x1, starting transfers between devices, body(): pieces = lax.all_to_all(pieces, ('blk', 'mp'), 0, 0, tiled=True)  14.3 us
    all_gather x1, blocking collectives, body(): lax.all_gather(trainer_q.astype(jnp.bfloat16), 'dp', axis=1, tiled=True)  12.5 us
    another operation x1, local copies, waits for them, and re-layouts, body(): shard_piece[0].reshape(key_count, head_count, HD)  10.2 us
    another operation x1, local copies, waits for them, and re-layouts, body(): shard_piece[1].reshape(key_count, head_count, HD)  10.2 us
    dot_general x1, matrix products, body(): jnp.einsum('td,hd->th', token_local, head_weights, preferred_element_type...  9.78 us
    slice x1, local copies, waits for them, and re-layouts, body(): shard_piece[0].reshape(key_count, head_count, HD)  7.13 us
  transfers between devices with their start and end apart: 2, of which 0 were waited for; matrix products, arithmetic and copies ran while one was open for 12% of the time, Pallas kernels for 65%

profile of v13, /device:TPU:25, one launch (start us, length us, event | category | flops | bytes accessed | tf_op | source)
XLA Modules:
  0.0 281.8 jit_solution(11467602925996344100)
XLA Ops:
  7.2 0.0 copy-start.1
  7.2 0.0 all-gather.2.cloned.1.call-start
  7.2 1.1 convert_element_type.18
  8.3 12.5 %all_gather.6 = bf16[56,7168]{1,0:T(8,128)(2,1)} all-gather(bf16[56,1792]{1,0:T(8,128)(2,1)S(1)} %convert_element_type.18), channel_id=1, replica_groups=mesh['dp'=4,'blk'=16,'mp'=4] {'dp'}, dimensions={1}, use_global_device_ids=true | all-gather | bytes 1003520 | tf_op jit(solution)/shard_map/all_gather | solution.py:121
  20.9 0.0 all-gather.2.cloned.1.call-update
  20.9 1.2 copy.59
  22.1 2.2 broadcast_in_dim.82
  24.3 14.3 %all-to-all-start = ((bf16[64,256,112]{1,2,0:T(8,128)(2,1)}), bf16[64,256,112]{1,2,0:T(8,128)(2,1)}, u32[]{:S(2)}, u32[]{:S(2)}) async-start(bf16[64,256,112]{1,2,0:T(8,128)(2,1)} %bitcast.70), calls=%async_computation | async-start | bytes 7340032 | tf_op jit(solution)/shard_map/all_to_all | solution.py:133
  39.9 0.0 copy-done.1
  39.9 0.1 fusion.46
  40.0 0.2 copy.40
  40.2 0.2 copy.39
  40.4 181.8 %shard_map.86 = bf16[16,2,128,896]{3,2,1,0:T(8,128)(2,1)} custom-call(bf16[2,128,896]{2,1,0:T(8,128)(2,1)} %piece_ref.1), custom_call_target="tpu_custom_call" | custom-call | tf_op jit(solution)/shard_map/pallas_call | solution.py:101
  222.3 7.1 %fusion.45 = (bf16[1,16,128,896]{3,2,0,1:T(8,128)(2,1)}, bf16[1,16,128,896]{3,2,0,1:T(8,128)(2,1)}) fusion(bf16[2,16,128,896]{3,2,0,1:T(8,128)(2,1)} %bitcast.69), kind=kLoop, calls=%fused_computation.59 | loop fusion | bytes 14680064 | tf_op jit(solution)/shard_map/slice | solution.py:166
  229.4 0.0 copy-start.2
  229.4 10.2 %reshape.108 = bf16[2048,4,224]{2,1,0:T(4,128)(2,1)} reshape(bf16[1,16,128,896]{3,2,0,1:T(8,128)(2,1)} %get-tuple-element.12) | data formatting | bytes 7340032 | tf_op jit(solution)/shard_map/reshape;squeeze | solution.py:166
  239.6 10.2 %reshape.109 = bf16[2048,4,224]{2,1,0:T(4,128)(2,1)} reshape(bf16[1,16,128,896]{3,2,0,1:T(8,128)(2,1)} %get-tuple-element.13) | data formatting | bytes 7340032 | tf_op jit(solution)/shard_map/reshape;squeeze | solution.py:167
  249.8 0.0 copy-done.2
  249.8 0.2 and_reduce_fusion
  250.0 0.1 fusion.31
  250.1 0.0 all-gather.2.cloned.1.call-done
  250.1 1.6 constant_dynamic-slice_fusion
  251.7 1.2 copy.44
  253.0 0.0 all-to-all-done
  253.0 9.8 %convolution_convert_fusion = bf16[256,896]{1,0:T(8,128)(2,1)S(1)} fusion(bf16[256,7168]{0,1:T(8,128)(2,1)} %bitcast.3, bf16[896,7168]{1,0:T(8,128)(2,1)} %all-gather.2.cloned.1.call-done), kind=kOutput, calls=%fused_computation.23 | convolution fusion | flops 3288563712 | bytes 16973824 | tf_op jit(solution)/shard_map/td,hd->th/dot_general | solution.py:135
  262.8 0.2 copy.38
  263.0 0.4 fusion.47
  263.4 4.8 %fusion = (f32[4,256]{1,0:T(4,128)S(1)}, f32[4,256,2048]{2,1,0:T(8,128)S(1)}) fusion(pred[2048]{0:T(1024)(128)(4,1)S(1)} %and_reduce_fusion, bf16[256,4,224]{0,2,1:T(8,128)(2,1)S(1)} %bitcast.74, bf16[2048,4,224]{2,1,0:T(4,128)(2,1)} %reshape.108), kind=kOutput, calls=%fused_computation.2 | convolution fusion | flops 945814528 | bytes 12523520 | tf_op jit(solution)/shard_map/thd,khd->htk/dot_general | solution.py:14
  268.2 0.0 copy-start
  268.2 2.4 fusion.1
  270.6 0.0 copy-done
  270.6 2.7 fusion.14
  273.3 0.2 fusion.25
  273.5 0.4 fusion.24
  274.0 1.0 copy.45
  (5 shorter events, 0.0 us)
Async XLA Ops:
  7.2 32.8 %copy-start.1 = (bf16[2,256,896]{2,1,0:T(8,128)(2,1)S(1)}, bf16[2,256,896]{2,1,0:T(8,128)(2,1)}, u32[]{:S(2)}) copy-start(bf16[2,256,896]{2,1,0:T(8,128)(2,1)} %param.10) | copy-start | bytes 2752516
  7.2 242.9 %all-gather.2.cloned.1.call-start = ((), (), s32[]{:S(2)}) async-start(), calls=%async_computation.1 | async-start | bytes 13647872 | tf_op jit(solution)/shard_map/all_gather | solution.py:122
  24.3 228.7 %all-to-all-start = ((bf16[64,256,112]{1,2,0:T(8,128)(2,1)}), bf16[64,256,112]{1,2,0:T(8,128)(2,1)}, u32[]{:S(2)}, u32[]{:S(2)}) async-start(bf16[64,256,112]{1,2,0:T(8,128)(2,1)} %bitcast.70), calls=%async_computation | async-start | bytes 7340032 | tf_op jit(solution)/shard_map/all_to_all | solution.py:133
  229.4 20.4 %copy-start.2 = (s32[1,64]{1,0:T(1,128)S(1)}, s32[1,64]{1,0:T(1,128)}, u32[]{:S(2)}) copy-start(s32[1,64]{1,0:T(1,128)} %param.11) | copy-start | bytes 772
  268.2 2.4 copy-start
Sparse Core Ops, SparseCore 0:
  21.0 179.8 all-gather.1

commit v14 on v13

--- a/solution.py
+++ b/solution.py
@@ -28,8 +28,15 @@
     return (new_max, row_total, weighted)
 
 
-def kv_gather_kernel(piece_ref, out_ref, local_sem, send_sems, recv_sems, fwd_send, fwd_recv):
+def kv_gather_kernel(piece_ref, out_full, local_sem, send_sems, recv_sems, fwd_send, fwd_recv):
     chips = lax.axis_size("blk") // 2
+    rows = piece_ref.shape[1]
+
+    class Slots:
+        def at(self, i):
+            return out_full.at[:, pl.ds(i * rows, rows)]
+
+    out_ref = Slots()
     g = lax.axis_index("dp")
     b = lax.axis_index("blk")
     m = lax.axis_index("mp")
@@ -51,29 +58,29 @@
         pl.semaphore_signal(barrier, inc=1, device_id=peer(j), device_id_type=pl.DeviceIdType.MESH)
     pl.semaphore_signal(barrier, inc=1, device_id=(g, mate, m), device_id_type=pl.DeviceIdType.MESH)
     pl.semaphore_wait(barrier, chips)
-    local = pltpu.make_async_copy(piece_ref, out_ref.at[b], local_sem)
+    local = pltpu.make_async_copy(piece_ref, out_ref.at(b), local_sem)
     local.start()
     sends = []
     for j in range(1, chips):
         copy = pltpu.make_async_remote_copy(
-            src_ref=piece_ref, dst_ref=out_ref.at[b], send_sem=send_sems.at[j],
+            src_ref=piece_ref, dst_ref=out_ref.at(b), send_sem=send_sems.at[j],
             recv_sem=recv_sems.at[j], device_id=peer(j), device_id_type=pl.DeviceIdType.MESH,
         )
         copy.start()
         sends.append(copy)
     to_mate = pltpu.make_async_remote_copy(
-        src_ref=piece_ref, dst_ref=out_ref.at[b], send_sem=send_sems.at[0],
+        src_ref=piece_ref, dst_ref=out_ref.at(b), send_sem=send_sems.at[0],
         recv_sem=recv_sems.at[0], device_id=(g, mate, m), device_id_type=pl.DeviceIdType.MESH,
     )
     to_mate.start()
     forwards = []
     for j in range(1, chips):
         pltpu.make_async_remote_copy(
-            src_ref=piece_ref, dst_ref=out_ref.at[source(j)], send_sem=send_sems.at[j],
+            src_ref=piece_ref, dst_ref=out_ref.at(source(j)), send_sem=send_sems.at[j],
             recv_sem=recv_sems.at[j], device_id=peer(j), device_id_type=pl.DeviceIdType.MESH,
         ).wait_recv()
         copy = pltpu.make_async_remote_copy(
-            src_ref=out_ref.at[source(j)], dst_ref=out_ref.at[source(j)], send_sem=fwd_send.at[j],
+            src_ref=out_ref.at(source(j)), dst_ref=out_ref.at(source(j)), send_sem=fwd_send.at[j],
             recv_sem=fwd_recv.at[j], device_id=(g, mate, m), device_id_type=pl.DeviceIdType.MESH,
         )
         copy.start()
@@ -83,14 +90,14 @@
         copy.wait_send()
     to_mate.wait_send()
     pltpu.make_async_remote_copy(
-        src_ref=piece_ref, dst_ref=out_ref.at[mate], send_sem=send_sems.at[0],
+        src_ref=piece_ref, dst_ref=out_ref.at(mate), send_sem=send_sems.at[0],
         recv_sem=recv_sems.at[0], device_id=(g, mate, m), device_id_type=pl.DeviceIdType.MESH,
     ).wait_recv()
     for copy in forwards:
         copy.wait_send()
     for j in range(1, chips):
         pltpu.make_async_remote_copy(
-            src_ref=out_ref.at[mate_slot(j)], dst_ref=out_ref.at[mate_slot(j)], send_sem=fwd_send.at[j],
+            src_ref=out_ref.at(mate_slot(j)), dst_ref=out_ref.at(mate_slot(j)), send_sem=fwd_send.at[j],
             recv_sem=fwd_recv.at[j], device_id=(g, mate, m), device_id_type=pl.DeviceIdType.MESH,
         ).wait_recv()
 
@@ -100,7 +107,9 @@
     chips = n // 2
     out = pl.pallas_call(
         kv_gather_kernel,
-        out_shape=jax.ShapeDtypeStruct((n,) + piece.shape, piece.dtype),
+        out_shape=jax.ShapeDtypeStruct(
+            (piece.shape[0], n * piece.shape[1], piece.shape[2]), piece.dtype
+        ),
         in_specs=[pl.BlockSpec(memory_space=pl.ANY)],
         out_specs=pl.BlockSpec(memory_space=pl.ANY),
         scratch_shapes=[
@@ -112,25 +121,29 @@
         ],
         compiler_params=pltpu.CompilerParams(collective_id=0, has_side_effects=True),
     )(piece)
-    return jnp.moveaxis(out, 0, 1).reshape(piece.shape[0], n * piece.shape[1], piece.shape[2])
+    return out
 
 
 def body(tokens, trainer_q, kv_pool, prompt_kv, page_table, page_count, prompt_len):
     blk_size = lax.axis_size("blk")
     mp_size = lax.axis_size("mp")
-    trainer_rows = lax.all_gather(trainer_q.astype(jnp.bfloat16), "dp", axis=1, tiled=True)
+    group_rows, piece_cols = tokens.shape
+    own_rows = group_rows // blk_size
+    pieces = tokens.reshape(blk_size, 1, own_rows, piece_cols)
+    pieces = jnp.broadcast_to(pieces, (blk_size, mp_size, own_rows, piece_cols))
+    pieces = pieces.reshape(blk_size * mp_size, own_rows, piece_cols)
+    pieces = lax.all_to_all(pieces, ("blk", "mp"), 0, 0, tiled=True)
+    shard_piece = gather_kv(kv_pool)
+    trainer_piece, shard_piece, pieces = lax.optimization_barrier(
+        (trainer_q.astype(jnp.bfloat16), shard_piece, pieces)
+    )
+    trainer_rows = lax.all_gather(trainer_piece, "dp", axis=1, tiled=True)
     head_weights = lax.all_gather(trainer_rows, "blk", axis=0, tiled=True)
     head_width, model_width = head_weights.shape
     block_cols = model_width // blk_size
     server_q = lax.dynamic_slice_in_dim(
         head_weights, lax.axis_index("blk") * block_cols, block_cols, axis=1
     )
-    group_rows, piece_cols = tokens.shape
-    own_rows = group_rows // blk_size
-    pieces = tokens.reshape(blk_size, 1, own_rows, piece_cols)
-    pieces = jnp.broadcast_to(pieces, (blk_size, mp_size, own_rows, piece_cols))
-    pieces = pieces.reshape(blk_size * mp_size, own_rows, piece_cols)
-    pieces = lax.all_to_all(pieces, ("blk", "mp"), 0, 0, tiled=True)
     token_local = jnp.transpose(pieces, (1, 0, 2)).reshape(own_rows, -1)
     queries = jnp.einsum(
         "td,hd->th", token_local, head_weights, preferred_element_type=jnp.float32
@@ -155,7 +168,6 @@
         prompt_kv[1].reshape(own_rows, head_count, HD),
         own_mask,
     )
-    shard_piece = gather_kv(kv_pool)
     key_count = shard_piece.shape[1]
     page_ids = jnp.arange(key_count, dtype=jnp.int32) // PAGE
     page_used = jnp.any((row_pages[None, :] == page_ids[:, None]) & live_slots[None, :], axis=1)

time: 282 us -> 285 us (1.011)
  waiting for transfers between devices: 0.04 us -> 55.6 us
  Pallas kernels: 182 us -> 141 us
  local copies, waits for them, and re-layouts: 35.5 us -> 27.1 us
    all_gather x1, waiting for transfers between devices: 0.02 us -> 55.6 us  [body(): head_weights = lax.all_gather(trainer_rows, 'blk', axis=0, tiled=True)]
    pallas_call x1, Pallas kernels: 182 us -> 141 us  [gather_kv(): pl.pallas_call(kv_gather_kernel, out_shape=jax.ShapeDtypeStruct((piece.sh...]
    another operation x2 -> x0, local copies, waits for them, and re-layouts: 20.3 us -> none  [the longest x1 10.2 us: body(): shard_piece[0].reshape(key_count, head_count, HD)]
    slice x0 -> x1, local copies, waits for them, and re-layouts: none -> 6.18 us  [body(): shard_piece[1].reshape(key_count, head_count, HD)]
    slice x1 -> x2, local copies, waits for them, and re-layouts: 7.13 us -> 13 us  [body(): shard_piece[0].reshape(key_count, head_count, HD)]
  transfers between devices with their start and end apart: 2 -> 2, of which waited for: 0 -> 1; matrix products, arithmetic and copies ran while one was open for 12% -> 7% of each run, Pallas kernels for 65% -> 50%
where the time goes in v14:
time: 285 us; the launch traced here: 284 us
  Pallas kernels  141 us (49%)
  waiting for transfers between devices  55.6 us (20%)
  local copies, waits for them, and re-layouts  27.1 us (10%)
  matrix products  16.7 us (6%)
  between operations  15.5 us (5%)
  blocking collectives  12.8 us (4%)
  starting transfers between devices  12.6 us (4%)
    pallas_call x1, Pallas kernels, gather_kv(): pl.pallas_call(kv_gather_kernel, out_shape=jax.ShapeDtypeStruct((piece.sh...  141 us
    all_gather x1, waiting for transfers between devices, body(): head_weights = lax.all_gather(trainer_rows, 'blk', axis=0, tiled=True)  55.6 us
    slice x2, local copies, waits for them, and re-layouts, body(): shard_piece[0].reshape(key_count, head_count, HD)  13 us
    all_gather x1, blocking collectives, body(): trainer_rows = lax.all_gather(trainer_piece, 'dp', axis=1, tiled=True)  12.8 us
    all_to_all x1, starting transfers between devices, body(): pieces = lax.all_to_all(pieces, ('blk', 'mp'), 0, 0, tiled=True)  12.5 us
    dot_general x1, matrix products, body(): jnp.einsum('td,hd->th', token_local, head_weights, preferred_element_type...  9.78 us
    slice x1, local copies, waits for them, and re-layouts, body(): shard_piece[1].reshape(key_count, head_count, HD)  6.18 us
  transfers between devices with their start and end apart: 2, of which 1 were waited for; matrix products, arithmetic and copies ran while one was open for 7% of the time, Pallas kernels for 50%

profile of v14, /device:TPU:25, one launch (start us, length us, event | category | flops | bytes accessed | tf_op | source)
XLA Modules:
  0.0 283.6 jit_solution(5851494318265686400)
XLA Ops:
  7.2 0.0 copy-start.2
  7.2 1.3 copy.49
  8.5 2.1 broadcast_in_dim.79
  10.5 0.0 copy-start.1
  10.5 12.5 %all-to-all-start = ((bf16[64,256,112]{1,2,0:T(8,128)(2,1)}), bf16[64,256,112]{1,2,0:T(8,128)(2,1)}, u32[]{:S(2)}, u32[]{:S(2)}) async-start(bf16[64,256,112]{1,2,0:T(8,128)(2,1)} %bitcast.64), calls=%async_computation | async-start | bytes 7340032 | tf_op jit(solution)/shard_map/all_to_all | solution.py:135
  23.1 0.0 copy-start.3
  23.1 0.0 all-gather.2.cloned.1.call-start
  23.1 0.0 copy-done.2
  23.2 140.6 %shard_map.86 = bf16[2,2048,896]{2,1,0:T(8,128)(2,1)} custom-call(bf16[2,128,896]{2,1,0:T(8,128)(2,1)} %piece_ref.1), custom_call_target="tpu_custom_call" | custom-call | tf_op jit(solution)/shard_map/pallas_call | solution.py:108
  163.8 0.0 all-to-all-done
  163.8 12.8 %all_gather.6 = bf16[56,7168]{1,0:T(8,128)(2,1)} all-gather(bf16[56,1792]{1,0:T(8,128)(2,1)S(1)} %convert_element_type.18), channel_id=1, replica_groups=mesh['dp'=4,'blk'=16,'mp'=4] {'dp'}, dimensions={1}, use_global_device_ids=true | all-gather | bytes 1003520 | tf_op jit(solution)/shard_map/all_gather | solution.py:140
  176.6 0.0 all-gather.2.cloned.1.call-update
  177.9 0.0 copy-done.1
  177.9 0.1 fusion.37
  178.0 0.2 copy.40
  178.2 0.2 copy.39
  178.5 0.0 copy-done.3
  178.5 0.2 and_reduce_fusion
  178.6 0.1 fusion.22
  178.7 6.7 %fusion.36 = (bf16[1,2048,896]{2,1,0:T(8,128)(2,1)}, bf16[1,2048,896]{2,1,0:T(8,128)(2,1)}) fusion(bf16[2,2048,896]{2,1,0:T(8,128)(2,1)} %shard_map.86), kind=kLoop, calls=%fused_computation.52 | loop fusion | bytes 14680064 | tf_op jit(solution)/shard_map/slice | solution.py:178
  185.5 6.3 %copy.42 = bf16[1,2048,896]{1,2,0:T(8,128)(2,1)} copy(bf16[1,2048,896]{2,1,0:T(8,128)(2,1)} %get-tuple-element.18) | data formatting | bytes 7340032 | tf_op jit(solution)/shard_map/slice | solution.py:178
  191.7 6.2 %copy.43 = bf16[1,2048,896]{1,2,0:T(8,128)(2,1)} copy(bf16[1,2048,896]{2,1,0:T(8,128)(2,1)} %get-tuple-element.19) | data formatting | bytes 7340032 | tf_op jit(solution)/shard_map/slice | solution.py:179
  197.9 55.6 %all-gather.2.cloned.1.call-done = bf16[896,7168]{1,0:T(8,128)(2,1)} async-done(((bf16[56,7168]{1,0:T(8,128)(2,1)}), bf16[896,7168]{1,0:T(8,128)(2,1)}) %all-gather.2.cloned.1.call-update) | async-done | bytes 12845072 | tf_op jit(solution)/shard_map/all_gather | solution.py:141
  253.5 1.6 constant_dynamic-slice_fusion
  255.1 1.2 copy.44
  256.4 9.8 %convolution_convert_fusion = bf16[256,896]{1,0:T(8,128)(2,1)S(1)} fusion(bf16[256,7168]{0,1:T(8,128)(2,1)} %bitcast.3, bf16[896,7168]{1,0:T(8,128)(2,1)} %all-gather.2.cloned.1.call-done), kind=kOutput, calls=%fused_computation.16 | convolution fusion | flops 3288563712 | bytes 16973824 | tf_op jit(solution)/shard_map/td,hd->th/dot_general | solution.py:148
  266.2 0.2 copy.38
  266.4 0.4 fusion.38
  266.8 0.0 copy-start
  266.8 4.0 %fusion = (f32[4,256]{1,0:T(4,128)S(1)}, f32[4,256,2048]{2,1,0:T(8,128)S(1)}) fusion(pred[2048]{0:T(1024)(128)(4,1)S(1)} %and_reduce_fusion, bf16[256,4,224]{0,2,1:T(8,128)(2,1)S(1)} %bitcast.67, bf16[2048,4,224]{0,2,1:T(8,128)(2,1)} %bitcast.65), kind=kOutput, calls=%fused_computation.2 | convolution fusion | flops 945814528 | bytes 12523520 | tf_op jit(solution)/shard_map/thd,khd->htk/dot_general | solution.py:14
  270.8 2.2 fusion.1
  273.0 0.0 copy-done
  273.0 2.1 fusion.7
  275.1 0.2 fusion.16
  275.3 0.4 fusion.15
  275.7 1.0 copy.45
  (6 shorter events, 0.1 us)
Async XLA Ops:
  7.2 16.0 %copy-start.2 = (f32[56,1792]{1,0:T(8,128)S(1)}, f32[56,1792]{1,0:T(8,128)}, u32[]{:S(2)}) copy-start(f32[56,1792]{1,0:T(8,128)} %param.8) | copy-start | bytes 1204228
  10.5 167.4 %copy-start.1 = (bf16[2,256,896]{2,1,0:T(8,128)(2,1)S(1)}, bf16[2,256,896]{2,1,0:T(8,128)(2,1)}, u32[]{:S(2)}) copy-start(bf16[2,256,896]{2,1,0:T(8,128)(2,1)} %param.10) | copy-start | bytes 2752516
  10.5 153.2 %all-to-all-start = ((bf16[64,256,112]{1,2,0:T(8,128)(2,1)}), bf16[64,256,112]{1,2,0:T(8,128)(2,1)}, u32[]{:S(2)}, u32[]{:S(2)}) async-start(bf16[64,256,112]{1,2,0:T(8,128)(2,1)} %bitcast.64), calls=%async_computation | async-start | bytes 7340032 | tf_op jit(solution)/shard_map/all_to_all | solution.py:135
  23.1 155.4 %copy-start.3 = (s32[1,64]{1,0:T(1,128)S(1)}, s32[1,64]{1,0:T(1,128)}, u32[]{:S(2)}) copy-start(s32[1,64]{1,0:T(1,128)} %param.11) | copy-start | bytes 772
  23.1 230.4 %all-gather.2.cloned.1.call-start = ((), (), s32[]{:S(2)}) async-start(), calls=%async_computation.1 | async-start | bytes 13647872 | tf_op jit(solution)/shard_map/all_gather | solution.py:141
  266.8 6.2 %copy-start = (bf16[1,2048,896]{1,2,0:T(8,128)(2,1)S(1)}, bf16[1,2048,896]{1,2,0:T(8,128)(2,1)}, u32[]{:S(2)}) copy-start(bf16[1,2048,896]{1,2,0:T(8,128)(2,1)} %copy.43) | copy-start | bytes 11010052
Sparse Core Ops, SparseCore 0:
  176.7 76.7 all-gather.1

commit v15 on v1

--- a/solution.py
+++ b/solution.py
@@ -29,7 +29,18 @@
 def body(tokens, trainer_q, kv_pool, prompt_kv, page_table, page_count, prompt_len):
     blk_size = lax.axis_size("blk")
     mp_size = lax.axis_size("mp")
-    trainer_rows = lax.all_gather(trainer_q.astype(jnp.bfloat16), "dp", axis=1, tiled=True)
+    dp_size = lax.axis_size("dp")
+    g = lax.axis_index("dp")
+    own_piece = trainer_q.astype(jnp.bfloat16)
+    received = jnp.stack(
+        [own_piece]
+        + [
+            lax.ppermute(own_piece, "dp", [(i, (i + j) % dp_size) for i in range(dp_size)])
+            for j in range(1, dp_size)
+        ]
+    )
+    ordered = jnp.take(received, (g - jnp.arange(dp_size)) % dp_size, axis=0)
+    trainer_rows = jnp.transpose(ordered, (1, 0, 2)).reshape(own_piece.shape[0], -1)
     head_weights = lax.all_gather(trainer_rows, "blk", axis=0, tiled=True)
     head_width, model_width = head_weights.shape
     block_cols = model_width // blk_size

time: 234 us -> 231 us (0.987)
  blocking collectives: 12.5 us -> 0 us
  waiting for transfers between devices: 142 us -> 151 us
  matrix products: 16.7 us -> 14.1 us
    all_gather x1 -> x0, blocking collectives: 12.5 us -> none  [body(): lax.all_gather(trainer_q.astype(jnp.bfloat16), 'dp', axis=1, tiled=True)]
    ppermute x0 -> x3, waiting for transfers between devices: none -> 10.5 us  [body(): lax.ppermute(own_piece, 'dp', [(i, (i + j) % dp_size) for i in range(dp_s...]
    ppermute x0 -> x3, starting transfers between devices: none -> 3.68 us  [body(): lax.ppermute(own_piece, 'dp', [(i, (i + j) % dp_size) for i in range(dp_s...]
    all_gather x1, waiting for transfers between devices: 69.7 us -> 66.3 us  [body(): shard_piece = lax.all_gather(kv_pool, 'blk', axis=1, tiled=True)]
  transfers between devices with their start and end apart: 3 -> 6, of which waited for: 2 -> 5; matrix products, arithmetic and copies ran while one was open for 12% -> 13% of each run, Pallas kernels for 0% -> 0%
where the time goes in v15:
time: 231 us; the launch traced here: 229 us
  waiting for transfers between devices  151 us (65%)
  local copies, waits for them, and re-layouts  27.2 us (12%)
  starting transfers between devices  16 us (7%)
  between operations  15.6 us (7%)
  matrix products  14.1 us (6%)
  other arithmetic  5.04 us (2%)
    all_gather x1, waiting for transfers between devices, body(): head_weights = lax.all_gather(trainer_rows, 'blk', axis=0, tiled=True)  73.5 us
    all_gather x1, waiting for transfers between devices, body(): shard_piece = lax.all_gather(kv_pool, 'blk', axis=1, tiled=True)  66.3 us
    slice x2, local copies, waits for them, and re-layouts, body(): shard_piece[0].reshape(key_count, head_count, HD)  12.9 us
    all_to_all x1, starting transfers between devices, body(): pieces = lax.all_to_all(pieces, ('blk', 'mp'), 0, 0, tiled=True)  12.2 us
    ppermute x3, waiting for transfers between devices, body(): lax.ppermute(own_piece, 'dp', [(i, (i + j) % dp_size) for i in range(dp_s...  10.5 us
    dot_general x1, matrix products, body(): jnp.einsum('td,hd->th', token_local, head_weights, preferred_element_type...  9.31 us
    slice x1, local copies, waits for them, and re-layouts, body(): shard_piece[1].reshape(key_count, head_count, HD)  6.17 us
  transfers between devices with their start and end apart: 6, of which 5 were waited for; matrix products, arithmetic and copies ran while one was open for 13% of the time, Pallas kernels for 0%

profile of v15, /device:TPU:25, one launch (start us, length us, event | category | flops | bytes accessed | tf_op | source)
XLA Modules:
  0.0 228.9 jit_solution(18045067984531203395)
XLA Ops:
  7.2 0.0 copy-start.2
  7.2 0.0 all-gather.5.cloned.1.call-start
  7.2 0.7 all-gather.5.cloned.1.call-update
  7.9 0.0 all-gather.3.cloned.1.call-start
  8.0 1.0 convert_element_type.21
  9.0 2.6 %collective-permute-start.2 = (bf16[56,1792]{1,0:T(8,128)(2,1)S(1)}, bf16[56,1792]{1,0:T(8,128)(2,1)S(1)}, u32[]{:S(2)}, u32[]{:S(2)}) collective-permute-start(bf16[56,1792]{1,0:T(8,128)(2,1)S(1)} %convert_element_type.21), channel_id=1, source_target_pairs={{0,192},{64,0},{128,64},{192,128},{1,193},{65,1},{129,65},{193,129... | collective-permute-start | bytes 602120 | tf_op jit(solution)/shard_map/ppermute | solution.py:38
  11.5 0.5 collective-permute-start.1
  12.1 0.6 collective-permute-start
  12.7 1.0 convert_bitcast_fusion
  13.7 2.3 collective-permute-done.2
  16.0 2.6 %collective-permute-done.1 = bf16[56,1792]{1,0:T(8,128)(2,1)S(1)} collective-permute-done((bf16[56,1792]{1,0:T(8,128)(2,1)S(1)}, bf16[56,1792]{1,0:T(8,128)(2,1)S(1)}, u32[]{:S(2)}, u32[]{:S(2)}) %collective-permute-start.1) | collective-permute-done | bytes 200736 | tf_op jit(solution)/shard_map/ppermute | solution.py:38
  18.6 5.6 %collective-permute-done = bf16[56,1792]{1,0:T(8,128)(2,1)S(1)} collective-permute-done((bf16[56,1792]{1,0:T(8,128)(2,1)S(1)}, bf16[56,1792]{1,0:T(8,128)(2,1)S(1)}, u32[]{:S(2)}, u32[]{:S(2)}) %collective-permute-start) | collective-permute-done | bytes 200736 | tf_op jit(solution)/shard_map/ppermute | solution.py:38
  24.3 0.1 pad_maximum_fusion
  24.4 0.6 gather_fusion
  25.0 0.1 select_bitcast_fusion
  25.1 0.0 copy-start.3
  25.1 0.9 copy.45
  26.1 0.0 all-gather.3.cloned.1.call-update
  26.1 0.0 copy-done.2
  26.1 0.0 copy-start.4
  26.1 0.1 copy.47
  26.2 2.2 broadcast_in_dim.94
  28.4 12.2 %all-to-all-start = ((bf16[64,256,112]{1,2,0:T(8,128)(2,1)}), bf16[64,256,112]{1,2,0:T(8,128)(2,1)}, u32[]{:S(2)}, u32[]{:S(2)}) async-start(bf16[64,256,112]{1,2,0:T(8,128)(2,1)} %bitcast.77), calls=%async_computation | async-start | bytes 7340032 | tf_op jit(solution)/shard_map/all_to_all | solution.py:55
  41.3 0.0 copy-done.3
  41.3 0.1 fusion.40
  41.4 0.2 copy.36
  42.2 0.2 copy.37
  42.5 0.0 copy-done.4
  42.5 0.2 and_reduce_fusion
  42.6 0.1 fusion.22
  42.8 66.3 %all-gather.5.cloned.1.call-done = bf16[2,2048,896]{2,1,0:T(8,128)(2,1)} async-done(((bf16[2,128,896]{2,1,0:T(8,128)(2,1)}), bf16[2,2048,896]{2,1,0:T(8,128)(2,1)}) %all-gather.5.cloned.1.call-update) | async-done | bytes 7340048 | tf_op jit(solution)/shard_map/all_gather | solution.py:80
  109.0 6.7 %fusion.39 = (bf16[1,2048,896]{2,1,0:T(8,128)(2,1)}, bf16[1,2048,896]{2,1,0:T(8,128)(2,1)}) fusion(bf16[2,2048,896]{2,1,0:T(8,128)(2,1)} %all-gather.5.cloned.1.call-done), kind=kLoop, calls=%fused_computation.68 | loop fusion | bytes 14680064 | tf_op jit(solution)/shard_map/slice | solution.py:88
  115.7 6.2 %copy.40 = bf16[1,2048,896]{1,2,0:T(8,128)(2,1)} copy(bf16[1,2048,896]{2,1,0:T(8,128)(2,1)} %get-tuple-element.13) | data formatting | bytes 7340032 | tf_op jit(solution)/shard_map/slice | solution.py:89
  121.9 6.2 %copy.39 = bf16[1,2048,896]{1,2,0:T(8,128)(2,1)} copy(bf16[1,2048,896]{2,1,0:T(8,128)(2,1)} %get-tuple-element.12) | data formatting | bytes 7340032 | tf_op jit(solution)/shard_map/slice | solution.py:88
  128.1 73.5 %all-gather.3.cloned.1.call-done = bf16[896,7168]{1,0:T(8,128)(2,1)} async-done(((bf16[56,7168]{1,0:T(8,128)(2,1)}), bf16[896,7168]{1,0:T(8,128)(2,1)}) %all-gather.3.cloned.1.call-update) | async-done | bytes 12845072 | tf_op jit(solution)/shard_map/all_gather | solution.py:44
  201.6 1.6 constant_dynamic-slice_fusion
  203.2 1.2 copy.41
  204.5 0.0 all-to-all-done
  204.5 0.0 copy-start
  204.5 9.3 %convolution_convert_fusion = bf16[896,256]{1,0:T(8,128)(2,1)S(1)} fusion(bf16[896,7168]{1,0:T(8,128)(2,1)} %all-gather.3.cloned.1.call-done, bf16[256,7168]{0,1:T(8,128)(2,1)} %bitcast.9), kind=kOutput, calls=%fused_computation.17 | convolution fusion | flops 3288563712 | bytes 16973824 | tf_op jit(solution)/shard_map/td,hd->th/dot_general | solution.py:57
  213.8 0.0 copy-done
  213.8 0.0 copy-start.1
  213.8 1.9 fusion
  215.7 0.4 fusion.41
  216.1 2.2 fusion.1
  218.3 0.0 copy-done.1
  218.3 2.1 fusion.7
  220.4 0.2 fusion.16
  220.7 0.4 fusion.15
  221.1 1.0 copy.42
  (8 shorter events, 0.1 us)
Async XLA Ops:
  7.2 18.9 %copy-start.2 = (bf16[4096,112]{0,1:T(8,128)(2,1)S(1)}, bf16[4096,112]{0,1:T(8,128)(2,1)}, u32[]{:S(2)}) copy-start(bf16[4096,112]{0,1:T(8,128)(2,1)} %param.7) | copy-start | bytes 2752516
  7.2 101.8 %all-gather.5.cloned.1.call-start = ((), (), s32[]{:S(2)}) async-start(), calls=%async_computation.2 | async-start | bytes 7798784 | tf_op jit(solution)/shard_map/all_gather | solution.py:80
  7.9 193.7 %all-gather.3.cloned.1.call-start = ((), (), s32[]{:S(2)}) async-start(), calls=%async_computation.1 | async-start | bytes 13647872 | tf_op jit(solution)/shard_map/all_gather | solution.py:44
  9.0 7.0 %collective-permute-start.2 = (bf16[56,1792]{1,0:T(8,128)(2,1)S(1)}, bf16[56,1792]{1,0:T(8,128)(2,1)S(1)}, u32[]{:S(2)}, u32[]{:S(2)}) collective-permute-start(bf16[56,1792]{1,0:T(8,128)(2,1)S(1)} %convert_element_type.21), channel_id=1, source_target_pairs={{0,192},{64,0},{128,64},{192,128},{1,193},{65,1},{129,65},{193,129... | collective-permute-start | bytes 602120 | tf_op jit(solution)/shard_map/ppermute | solution.py:38
  11.5 7.1 %collective-permute-start.1 = (bf16[56,1792]{1,0:T(8,128)(2,1)S(1)}, bf16[56,1792]{1,0:T(8,128)(2,1)S(1)}, u32[]{:S(2)}, u32[]{:S(2)}) collective-permute-start(bf16[56,1792]{1,0:T(8,128)(2,1)S(1)} %convert_element_type.21), channel_id=1, source_target_pairs={{0,128},{64,192},{128,0},{192,64},{1,129},{65,193},{129,1},{193,65... | collective-permute-start | bytes 602120 | tf_op jit(solution)/shard_map/ppermute | solution.py:38
  12.1 12.2 %collective-permute-start = (bf16[56,1792]{1,0:T(8,128)(2,1)S(1)}, bf16[56,1792]{1,0:T(8,128)(2,1)S(1)}, u32[]{:S(2)}, u32[]{:S(2)}) collective-permute-start(bf16[56,1792]{1,0:T(8,128)(2,1)S(1)} %convert_element_type.21), channel_id=1, source_target_pairs={{0,64},{64,128},{128,192},{192,0},{1,65},{65,129},{129,193},{193,1... | collective-permute-start | bytes 602120 | tf_op jit(solution)/shard_map/ppermute | solution.py:38
  25.1 16.2 %copy-start.3 = (bf16[2,256,896]{2,1,0:T(8,128)(2,1)S(1)}, bf16[2,256,896]{2,1,0:T(8,128)(2,1)}, u32[]{:S(2)}) copy-start(bf16[2,256,896]{2,1,0:T(8,128)(2,1)} %param.10) | copy-start | bytes 2752516
  26.1 16.4 %copy-start.4 = (s32[1,64]{1,0:T(1,128)S(1)}, s32[1,64]{1,0:T(1,128)}, u32[]{:S(2)}) copy-start(s32[1,64]{1,0:T(1,128)} %param.11) | copy-start | bytes 772
  28.4 176.1 %all-to-all-start = ((bf16[64,256,112]{1,2,0:T(8,128)(2,1)}), bf16[64,256,112]{1,2,0:T(8,128)(2,1)}, u32[]{:S(2)}, u32[]{:S(2)}) async-start(bf16[64,256,112]{1,2,0:T(8,128)(2,1)} %bitcast.77), calls=%async_computation | async-start | bytes 7340032 | tf_op jit(solution)/shard_map/all_to_all | solution.py:55
  204.5 9.3 %copy-start = (bf16[1,2048,896]{1,2,0:T(8,128)(2,1)S(1)}, bf16[1,2048,896]{1,2,0:T(8,128)(2,1)}, u32[]{:S(2)}) copy-start(bf16[1,2048,896]{1,2,0:T(8,128)(2,1)} %copy.39) | copy-start | bytes 11010052
  213.8 4.5 %copy-start.1 = (bf16[1,2048,896]{1,2,0:T(8,128)(2,1)S(1)}, bf16[1,2048,896]{1,2,0:T(8,128)(2,1)}, u32[]{:S(2)}) copy-start(bf16[1,2048,896]{1,2,0:T(8,128)(2,1)} %copy.40) | copy-start | bytes 11010052
Sparse Core Ops, SparseCore 0:
  9.8 99.1 all-gather.4
  111.4 90.1 all-gather.2

commit v16 on v15

--- a/solution.py
+++ b/solution.py
@@ -31,7 +31,12 @@
     mp_size = lax.axis_size("mp")
     dp_size = lax.axis_size("dp")
     g = lax.axis_index("dp")
-    own_piece = trainer_q.astype(jnp.bfloat16)
+    group_rows, piece_cols = tokens.shape
+    own_rows = group_rows // blk_size
+    pieces = tokens.reshape(blk_size, 1, own_rows, piece_cols)
+    pieces = jnp.broadcast_to(pieces, (blk_size, mp_size, own_rows, piece_cols))
+    pieces = pieces.reshape(blk_size * mp_size, own_rows, piece_cols)
+    own_piece, pieces = lax.optimization_barrier((trainer_q.astype(jnp.bfloat16), pieces))
     received = jnp.stack(
         [own_piece]
         + [
@@ -47,11 +52,6 @@
     server_q = lax.dynamic_slice_in_dim(
         head_weights, lax.axis_index("blk") * block_cols, block_cols, axis=1
     )
-    group_rows, piece_cols = tokens.shape
-    own_rows = group_rows // blk_size
-    pieces = tokens.reshape(blk_size, 1, own_rows, piece_cols)
-    pieces = jnp.broadcast_to(pieces, (blk_size, mp_size, own_rows, piece_cols))
-    pieces = pieces.reshape(blk_size * mp_size, own_rows, piece_cols)
     pieces = lax.all_to_all(pieces, ("blk", "mp"), 0, 0, tiled=True)
     token_local = jnp.transpose(pieces, (1, 0, 2)).reshape(own_rows, -1)
     queries = jnp.einsum(

time: 231 us -> 234 us (1.013)
  matrix products: 14.1 us -> 16.7 us
    all_gather x1, waiting for transfers between devices: 66.3 us -> 63.7 us  [body(): shard_piece = lax.all_gather(kv_pool, 'blk', axis=1, tiled=True)]
where the time goes in v16:
time: 234 us; the launch traced here: 232 us
  waiting for transfers between devices  151 us (65%)
  local copies, waits for them, and re-layouts  28.7 us (12%)
  matrix products  16.7 us (7%)
  starting transfers between devices  15.9 us (7%)
  between operations  15.5 us (7%)
  other arithmetic  4.23 us (2%)
    all_gather x1, waiting for transfers between devices, body(): head_weights = lax.all_gather(trainer_rows, 'blk', axis=0, tiled=True)  74.9 us
    all_gather x1, waiting for transfers between devices, body(): shard_piece = lax.all_gather(kv_pool, 'blk', axis=1, tiled=True)  63.7 us
    slice x2, local copies, waits for them, and re-layouts, body(): shard_piece[0].reshape(key_count, head_count, HD)  12.9 us
    all_to_all x1, starting transfers between devices, body(): pieces = lax.all_to_all(pieces, ('blk', 'mp'), 0, 0, tiled=True)  12.2 us
    ppermute x3, waiting for transfers between devices, body(): lax.ppermute(own_piece, 'dp', [(i, (i + j) % dp_size) for i in range(dp_s...  11.5 us
    dot_general x1, matrix products, body(): jnp.einsum('td,hd->th', token_local, head_weights, preferred_element_type...  9.78 us
    slice x1, local copies, waits for them, and re-layouts, body(): shard_piece[1].reshape(key_count, head_count, HD)  6.19 us
  transfers between devices with their start and end apart: 6, of which 5 were waited for; matrix products, arithmetic and copies ran while one was open for 13% of the time, Pallas kernels for 0%

profile of v16, /device:TPU:25, one launch (start us, length us, event | category | flops | bytes accessed | tf_op | source)
XLA Modules:
  0.0 231.9 jit_solution(15453057047708661717)
XLA Ops:
  7.2 0.0 all-gather.5.cloned.1.call-start
  7.2 0.7 all-gather.5.cloned.1.call-update
  7.9 0.0 all-gather.3.cloned.1.call-start
  7.9 1.0 convert_element_type.18
  9.0 1.2 copy.52
  10.2 2.2 broadcast_in_dim.90
  12.4 0.0 copy-start.1
  12.4 2.5 %collective-permute-start.2 = (bf16[56,1792]{1,0:T(8,128)(2,1)S(1)}, bf16[56,1792]{1,0:T(8,128)(2,1)S(1)}, u32[]{:S(2)}, u32[]{:S(2)}) collective-permute-start(bf16[56,1792]{1,0:T(8,128)(2,1)S(1)} %convert_element_type.18), channel_id=1, source_target_pairs={{0,192},{64,0},{128,64},{192,128},{1,193},{65,1},{129,65},{193,129... | collective-permute-start | bytes 602120 | tf_op jit(solution)/shard_map/ppermute | solution.py:43
  14.9 0.5 collective-permute-start.1
  15.4 0.6 collective-permute-start
  16.0 3.3 %collective-permute-done.2 = bf16[56,1792]{1,0:T(8,128)(2,1)S(1)} collective-permute-done((bf16[56,1792]{1,0:T(8,128)(2,1)S(1)}, bf16[56,1792]{1,0:T(8,128)(2,1)S(1)}, u32[]{:S(2)}, u32[]{:S(2)}) %collective-permute-start.2) | collective-permute-done | bytes 200736 | tf_op jit(solution)/shard_map/ppermute | solution.py:43
  19.3 2.6 %collective-permute-done.1 = bf16[56,1792]{1,0:T(8,128)(2,1)S(1)} collective-permute-done((bf16[56,1792]{1,0:T(8,128)(2,1)S(1)}, bf16[56,1792]{1,0:T(8,128)(2,1)S(1)}, u32[]{:S(2)}, u32[]{:S(2)}) %collective-permute-start.1) | collective-permute-done | bytes 200736 | tf_op jit(solution)/shard_map/ppermute | solution.py:43
  22.0 5.6 %collective-permute-done = bf16[56,1792]{1,0:T(8,128)(2,1)S(1)} collective-permute-done((bf16[56,1792]{1,0:T(8,128)(2,1)S(1)}, bf16[56,1792]{1,0:T(8,128)(2,1)S(1)}, u32[]{:S(2)}, u32[]{:S(2)}) %collective-permute-start) | collective-permute-done | bytes 200736 | tf_op jit(solution)/shard_map/ppermute | solution.py:43
  27.6 0.1 pad_maximum_fusion
  27.7 0.0 copy-start.2
  27.7 0.6 gather_fusion
  28.3 0.1 select_bitcast_fusion
  28.5 0.9 copy.50
  29.4 0.0 all-gather.3.cloned.1.call-update
  29.4 12.2 %all-to-all-start = ((bf16[64,256,112]{1,2,0:T(8,128)(2,1)}), bf16[64,256,112]{1,2,0:T(8,128)(2,1)}, u32[]{:S(2)}, u32[]{:S(2)}) async-start(bf16[64,256,112]{1,2,0:T(8,128)(2,1)} %bitcast.74), calls=%async_computation | async-start | bytes 7340032 | tf_op jit(solution)/shard_map/all_to_all | solution.py:55
  43.0 0.0 copy-done.1
  43.0 0.1 fusion.40
  43.1 0.2 copy.42
  43.3 0.2 copy.41
  43.5 0.0 copy-done.2
  43.6 0.2 and_reduce_fusion
  43.7 0.1 fusion.22
  43.8 63.7 %all-gather.5.cloned.1.call-done = bf16[2,2048,896]{2,1,0:T(8,128)(2,1)} async-done(((bf16[2,128,896]{2,1,0:T(8,128)(2,1)}), bf16[2,2048,896]{2,1,0:T(8,128)(2,1)}) %all-gather.5.cloned.1.call-update) | async-done | bytes 7340048 | tf_op jit(solution)/shard_map/all_gather | solution.py:80
  107.5 6.8 %fusion.39 = (bf16[1,2048,896]{2,1,0:T(8,128)(2,1)}, bf16[1,2048,896]{2,1,0:T(8,128)(2,1)}) fusion(bf16[2,2048,896]{2,1,0:T(8,128)(2,1)} %all-gather.5.cloned.1.call-done), kind=kLoop, calls=%fused_computation.68 | loop fusion | bytes 14680064 | tf_op jit(solution)/shard_map/slice | solution.py:88
  114.3 6.2 %copy.44 = bf16[1,2048,896]{1,2,0:T(8,128)(2,1)} copy(bf16[1,2048,896]{2,1,0:T(8,128)(2,1)} %get-tuple-element.16) | data formatting | bytes 7340032 | tf_op jit(solution)/shard_map/slice | solution.py:88
  120.5 6.2 %copy.45 = bf16[1,2048,896]{1,2,0:T(8,128)(2,1)} copy(bf16[1,2048,896]{2,1,0:T(8,128)(2,1)} %get-tuple-element.17) | data formatting | bytes 7340032 | tf_op jit(solution)/shard_map/slice | solution.py:89
  126.7 74.9 %all-gather.3.cloned.1.call-done = bf16[896,7168]{1,0:T(8,128)(2,1)} async-done(((bf16[56,7168]{1,0:T(8,128)(2,1)}), bf16[896,7168]{1,0:T(8,128)(2,1)}) %all-gather.3.cloned.1.call-update) | async-done | bytes 12845072 | tf_op jit(solution)/shard_map/all_gather | solution.py:49
  201.6 1.6 constant_dynamic-slice_fusion
  203.2 1.2 copy.46
  204.5 0.0 all-to-all-done
  204.5 9.8 %convolution_convert_fusion = bf16[256,896]{1,0:T(8,128)(2,1)S(1)} fusion(bf16[256,7168]{0,1:T(8,128)(2,1)} %bitcast.9, bf16[896,7168]{1,0:T(8,128)(2,1)} %all-gather.3.cloned.1.call-done), kind=kOutput, calls=%fused_computation.17 | convolution fusion | flops 3288563712 | bytes 16973824 | tf_op jit(solution)/shard_map/td,hd->th/dot_general | solution.py:57
  214.3 0.2 copy.40
  214.5 0.4 fusion.41
  214.9 0.0 copy-start
  214.9 4.0 %fusion = (f32[4,256]{1,0:T(4,128)S(1)}, f32[4,256,2048]{2,1,0:T(8,128)S(1)}) fusion(pred[2048]{0:T(1024)(128)(4,1)S(1)} %and_reduce_fusion, bf16[256,4,224]{0,2,1:T(8,128)(2,1)S(1)} %bitcast.77, bf16[2048,4,224]{0,2,1:T(8,128)(2,1)} %bitcast.75), kind=kOutput, calls=%fused_computation.3 | convolution fusion | flops 945814528 | bytes 12523520 | tf_op jit(solution)/shard_map/thd,khd->htk/dot_general | solution.py:12
  218.8 2.4 %fusion.1 = f32[4,256]{1,0:T(4,128)S(1)} fusion(f32[4,256,2048]{2,1,0:T(8,128)S(1)} %get-tuple-element.26, f32[4,256]{1,0:T(4,128)S(1)} %get-tuple-element.22, pred[2048]{0:T(1024)(128)(4,1)S(1)} %and_reduce_fusion), kind=kLoop, calls=%fused_computation.4 | loop fusion | flops 10484736 | bytes 8398848 | tf_op jit(solution)/shard_map/reduce_sum | solution.py:19
  221.3 0.0 copy-done
  221.3 2.1 fusion.7
  223.4 0.2 fusion.16
  223.6 0.4 fusion.15
  224.1 1.0 copy.47
  (8 shorter events, 0.1 us)
Async XLA Ops:
  7.2 100.4 %all-gather.5.cloned.1.call-start = ((), (), s32[]{:S(2)}) async-start(), calls=%async_computation.2 | async-start | bytes 7798784 | tf_op jit(solution)/shard_map/all_gather | solution.py:80
  7.9 193.7 %all-gather.3.cloned.1.call-start = ((), (), s32[]{:S(2)}) async-start(), calls=%async_computation.1 | async-start | bytes 13647872 | tf_op jit(solution)/shard_map/all_gather | solution.py:49
  12.4 30.6 %copy-start.1 = (bf16[2,256,896]{2,1,0:T(8,128)(2,1)S(1)}, bf16[2,256,896]{2,1,0:T(8,128)(2,1)}, u32[]{:S(2)}) copy-start(bf16[2,256,896]{2,1,0:T(8,128)(2,1)} %param.10) | copy-start | bytes 2752516
  12.4 6.9 %collective-permute-start.2 = (bf16[56,1792]{1,0:T(8,128)(2,1)S(1)}, bf16[56,1792]{1,0:T(8,128)(2,1)S(1)}, u32[]{:S(2)}, u32[]{:S(2)}) collective-permute-start(bf16[56,1792]{1,0:T(8,128)(2,1)S(1)} %convert_element_type.18), channel_id=1, source_target_pairs={{0,192},{64,0},{128,64},{192,128},{1,193},{65,1},{129,65},{193,129... | collective-permute-start | bytes 602120 | tf_op jit(solution)/shard_map/ppermute | solution.py:43
  14.9 7.1 %collective-permute-start.1 = (bf16[56,1792]{1,0:T(8,128)(2,1)S(1)}, bf16[56,1792]{1,0:T(8,128)(2,1)S(1)}, u32[]{:S(2)}, u32[]{:S(2)}) collective-permute-start(bf16[56,1792]{1,0:T(8,128)(2,1)S(1)} %convert_element_type.18), channel_id=1, source_target_pairs={{0,128},{64,192},{128,0},{192,64},{1,129},{65,193},{129,1},{193,65... | collective-permute-start | bytes 602120 | tf_op jit(solution)/shard_map/ppermute | solution.py:43
  15.4 12.2 %collective-permute-start = (bf16[56,1792]{1,0:T(8,128)(2,1)S(1)}, bf16[56,1792]{1,0:T(8,128)(2,1)S(1)}, u32[]{:S(2)}, u32[]{:S(2)}) collective-permute-start(bf16[56,1792]{1,0:T(8,128)(2,1)S(1)} %convert_element_type.18), channel_id=1, source_target_pairs={{0,64},{64,128},{128,192},{192,0},{1,65},{65,129},{129,193},{193,1... | collective-permute-start | bytes 602120 | tf_op jit(solution)/shard_map/ppermute | solution.py:43
  27.7 15.9 %copy-start.2 = (s32[1,64]{1,0:T(1,128)S(1)}, s32[1,64]{1,0:T(1,128)}, u32[]{:S(2)}) copy-start(s32[1,64]{1,0:T(1,128)} %param.11) | copy-start | bytes 772
  29.4 175.0 %all-to-all-start = ((bf16[64,256,112]{1,2,0:T(8,128)(2,1)}), bf16[64,256,112]{1,2,0:T(8,128)(2,1)}, u32[]{:S(2)}, u32[]{:S(2)}) async-start(bf16[64,256,112]{1,2,0:T(8,128)(2,1)} %bitcast.74), calls=%async_computation | async-start | bytes 7340032 | tf_op jit(solution)/shard_map/all_to_all | solution.py:55
  214.9 6.4 %copy-start = (bf16[1,2048,896]{1,2,0:T(8,128)(2,1)S(1)}, bf16[1,2048,896]{1,2,0:T(8,128)(2,1)}, u32[]{:S(2)}) copy-start(bf16[1,2048,896]{1,2,0:T(8,128)(2,1)} %copy.45) | copy-start | bytes 11010052
Sparse Core Ops, SparseCore 0:
  9.8 97.6 all-gather.4
  109.9 91.5 all-gather.2

commit v17 on v15

--- a/solution.py
+++ b/solution.py
@@ -59,39 +59,36 @@
     )
     queries = queries.astype(jnp.bfloat16)
     head_count = head_width // HD
-    query_heads = queries.reshape(own_rows, head_count, HD)
     length = prompt_len[0]
     row_pages = page_table[0]
     live_slots = jnp.arange(row_pages.shape[0], dtype=jnp.int32) < page_count[0]
     row_index = jnp.arange(own_rows, dtype=jnp.int32)
     own_mask = (row_index[None, :] <= row_index[:, None]) & (row_index[None, :] < length)
-    softmax_state = (
-        jnp.full((head_count, own_rows), -1e30, jnp.float32),
-        jnp.zeros((head_count, own_rows), jnp.float32),
-        jnp.zeros((head_count, own_rows, HD), jnp.float32),
-    )
-    softmax_state = attend_block(
-        softmax_state,
-        query_heads,
-        prompt_kv[0].reshape(own_rows, head_count, HD),
-        prompt_kv[1].reshape(own_rows, head_count, HD),
-        own_mask,
-    )
     shard_piece = lax.all_gather(kv_pool, "blk", axis=1, tiled=True)
     key_count = shard_piece.shape[1]
     page_ids = jnp.arange(key_count, dtype=jnp.int32) // PAGE
     page_used = jnp.any((row_pages[None, :] == page_ids[:, None]) & live_slots[None, :], axis=1)
-    key_mask = jnp.broadcast_to(page_used[None, :], (own_rows, key_count))
-    running_max, row_total, weighted = attend_block(
-        softmax_state,
-        query_heads,
-        shard_piece[0].reshape(key_count, head_count, HD),
-        shard_piece[1].reshape(key_count, head_count, HD),
-        key_mask,
+    key_mask = jnp.concatenate(
+        [own_mask, jnp.broadcast_to(page_used[None, :], (own_rows, key_count))], axis=1
     )
-    mixed = weighted / row_total[:, :, None]
-    mixed = jnp.where((row_index < length)[None, :, None], mixed, 0.0)
-    mixed = jnp.transpose(mixed, (1, 0, 2)).reshape(own_rows, head_width).astype(jnp.bfloat16)
+    outputs = []
+    for h in range(head_count):
+        cols = slice(h * HD, (h + 1) * HD)
+        query_h = queries[:, cols]
+        keys_h = jnp.concatenate([prompt_kv[0][:, cols], shard_piece[0][:, cols]], axis=0)
+        values_h = jnp.concatenate([prompt_kv[1][:, cols], shard_piece[1][:, cols]], axis=0)
+        scores = lax.dot_general(
+            query_h, keys_h, (((1,), (1,)), ((), ())), preferred_element_type=jnp.float32
+        ) * HD ** (-0.5)
+        scores = jnp.where(key_mask, scores, -1e30)
+        largest = jnp.max(scores, axis=1, keepdims=True)
+        weights = jnp.where(key_mask, jnp.exp(scores - largest), 0.0)
+        row_total = jnp.sum(weights, axis=1, keepdims=True)
+        mixed = jnp.dot(
+            weights.astype(jnp.bfloat16), values_h, preferred_element_type=jnp.float32
+        ) / row_total
+        outputs.append(jnp.where((row_index < length)[:, None], mixed, 0.0))
+    mixed = jnp.concatenate(outputs, axis=1).astype(jnp.bfloat16)
     return (server_q, mixed)
 
 

time: 231 us -> 234 us (1.013)
  local copies, waits for them, and re-layouts: 27.2 us -> 22 us
  waiting for transfers between devices: 151 us -> 156 us
  starting transfers between devices: 16 us -> 18.7 us
    slice x6 -> x4, local copies, waits for them, and re-layouts: 19.6 us -> 8.41 us  [the longest x1 3.59 us: body(): shard_piece[0][:, cols]]
    all_gather x1, waiting for transfers between devices: 73.5 us -> 79.4 us  [body(): head_weights = lax.all_gather(trainer_rows, 'blk', axis=0, tiled=True)]
    ppermute x3, waiting for transfers between devices: 10.5 us -> 5.91 us  [body(): lax.ppermute(own_piece, 'dp', [(i, (i + j) % dp_size) for i in range(dp_s...]
    squeeze x0 -> x2, local copies, waits for them, and re-layouts: none -> 3.82 us  [the longest x1 3.74 us: body(): shard_piece[0][:, cols]]
    all_gather x1, waiting for transfers between devices: 66.3 us -> 69.5 us  [body(): shard_piece = lax.all_gather(kv_pool, 'blk', axis=1, tiled=True)]
    dot_general x4 -> x8, matrix products: 4.79 us -> 6.24 us  [the longest x4 3.41 us: body(): jnp.dot(weights.astype(jnp.bfloat16), values_h, preferred_element_type=jn...]
  transfers between devices with their start and end apart: 6 -> 6, of which waited for: 5 -> 4; matrix products, arithmetic and copies ran while one was open for 13% -> 9% of each run, Pallas kernels for 0% -> 0%
where the time goes in v17:
time: 234 us; the launch traced here: 232 us
  waiting for transfers between devices  156 us (67%)
  local copies, waits for them, and re-layouts  22 us (9%)
  starting transfers between devices  18.7 us (8%)
  between operations  15.6 us (7%)
  matrix products  15.5 us (7%)
  other arithmetic  4.73 us (2%)
    all_gather x1, waiting for transfers between devices, body(): head_weights = lax.all_gather(trainer_rows, 'blk', axis=0, tiled=True)  79.4 us
    all_gather x1, waiting for transfers between devices, body(): shard_piece = lax.all_gather(kv_pool, 'blk', axis=1, tiled=True)  69.5 us
    all_to_all x1, starting transfers between devices, body(): pieces = lax.all_to_all(pieces, ('blk', 'mp'), 0, 0, tiled=True)  13.1 us
    dot_general x1, matrix products, body(): jnp.einsum('td,hd->th', token_local, head_weights, preferred_element_type...  9.25 us
    ppermute x3, waiting for transfers between devices, body(): lax.ppermute(own_piece, 'dp', [(i, (i + j) % dp_size) for i in range(dp_s...  5.91 us
    ppermute x3, starting transfers between devices, body(): lax.ppermute(own_piece, 'dp', [(i, (i + j) % dp_size) for i in range(dp_s...  5.51 us
  transfers between devices with their start and end apart: 6, of which 4 were waited for; matrix products, arithmetic and copies ran while one was open for 9% of the time, Pallas kernels for 0%

profile of v17, /device:TPU:25, one launch (start us, length us, event | category | flops | bytes accessed | tf_op | source)
XLA Modules:
  0.0 232.0 jit_solution(11136181188499823580)
XLA Ops:
  7.2 0.0 all-gather.5.cloned.1.call-start
  7.2 0.7 all-gather.5.cloned.1.call-update
  7.9 0.0 all-gather.3.cloned.1.call-start
  7.9 1.0 convert_element_type.22
  9.0 2.8 %collective-permute-start.1 = (bf16[56,1792]{1,0:T(8,128)(2,1)S(1)}, bf16[56,1792]{1,0:T(8,128)(2,1)S(1)}, u32[]{:S(2)}, u32[]{:S(2)}) collective-permute-start(bf16[56,1792]{1,0:T(8,128)(2,1)S(1)} %convert_element_type.22), channel_id=1, source_target_pairs={{0,128},{64,192},{128,0},{192,64},{1,129},{65,193},{129,1},{193,65... | collective-permute-start | bytes 602120 | tf_op jit(solution)/shard_map/ppermute | solution.py:38
  11.8 0.3 collective-permute-start
  12.1 2.4 %collective-permute-start.2 = (bf16[56,1792]{1,0:T(8,128)(2,1)S(1)}, bf16[56,1792]{1,0:T(8,128)(2,1)S(1)}, u32[]{:S(2)}, u32[]{:S(2)}) collective-permute-start(bf16[56,1792]{1,0:T(8,128)(2,1)S(1)} %convert_element_type.22), channel_id=1, source_target_pairs={{0,192},{64,0},{128,64},{192,128},{1,193},{65,1},{129,65},{193,129... | collective-permute-start | bytes 602120 | tf_op jit(solution)/shard_map/ppermute | solution.py:38
  14.5 1.0 convert_bitcast_fusion
  15.5 0.9 collective-permute-done.1
  16.4 5.0 %collective-permute-done = bf16[56,1792]{1,0:T(8,128)(2,1)S(1)} collective-permute-done((bf16[56,1792]{1,0:T(8,128)(2,1)S(1)}, bf16[56,1792]{1,0:T(8,128)(2,1)S(1)}, u32[]{:S(2)}, u32[]{:S(2)}) %collective-permute-start) | collective-permute-done | bytes 200736 | tf_op jit(solution)/shard_map/ppermute | solution.py:38
  21.5 0.0 collective-permute-done.2
  21.5 0.1 pad_maximum_fusion
  21.6 0.6 gather_fusion
  22.2 0.0 copy-start.6
  22.2 0.1 select_bitcast_fusion
  22.3 0.9 copy.24
  23.3 0.0 all-gather.3.cloned.1.call-update
  23.3 0.1 copy-done.6
  23.5 0.1 copy.26
  23.5 2.2 broadcast_in_dim.82
  25.7 0.0 copy-start.13
  25.7 0.0 copy-start.7
  25.7 13.1 %all-to-all-start = ((bf16[64,256,112]{1,2,0:T(8,128)(2,1)}), bf16[64,256,112]{1,2,0:T(8,128)(2,1)}, u32[]{:S(2)}, u32[]{:S(2)}) async-start(bf16[64,256,112]{1,2,0:T(8,128)(2,1)} %bitcast.36), calls=%async_computation | async-start | bytes 7340032 | tf_op jit(solution)/shard_map/all_to_all | solution.py:55
  40.1 0.0 copy-done.13
  40.1 0.2 and_reduce_fusion
  40.4 0.0 copy-done.7
  40.4 0.1 slice_bitcast_fusion.3
  40.5 1.0 fusion.147
  41.4 0.8 fusion.146
  42.3 69.5 %all-gather.5.cloned.1.call-done = bf16[2,2048,896]{2,1,0:T(8,128)(2,1)} async-done(((bf16[2,128,896]{2,1,0:T(8,128)(2,1)}), bf16[2,2048,896]{2,1,0:T(8,128)(2,1)}) %all-gather.5.cloned.1.call-update) | async-done | bytes 7340048 | tf_op jit(solution)/shard_map/all_gather | solution.py:67
  111.8 3.7 %slice_bitcast_fusion.1 = (bf16[2048,896]{1,0:T(8,128)(2,1)S(1)}, bf16[2048,896]{1,0:T(8,128)(2,1)S(1)}) fusion(bf16[2,2048,896]{2,1,0:T(8,128)(2,1)} %all-gather.5.cloned.1.call-done), kind=kLoop, calls=%fused_computation.10 | loop fusion | bytes 14680064 | tf_op jit(solution)/shard_map/squeeze | solution.py:78
  115.5 3.6 %fusion.145 = (bf16[2048,224]{1,0:T(8,128)(2,1)}, bf16[2048,224]{1,0:T(8,128)(2,1)}, bf16[2048,224]{1,0:T(8,128)(2,1)}, bf16[2048,224]{1,0:T(8,128)(2,1)}) fusion(bf16[2048,896]{1,0:T(8,128)(2,1)S(1)} %get-tuple-element.14), kind=kLoop, calls=%fused_computation.131 | loop fusion | bytes 7340032 | tf_op jit(solution)/shard_map/slice | solution.py:78
  119.1 3.0 %fusion.144 = (bf16[2048,224]{1,0:T(8,128)(2,1)S(1)}, bf16[2048,224]{1,0:T(8,128)(2,1)S(1)}, bf16[2048,224]{1,0:T(8,128)(2,1)}, bf16[2048,224]{1,0:T(8,128)(2,1)}) fusion(bf16[2048,896]{1,0:T(8,128)(2,1)S(1)} %get-tuple-element.15), kind=kLoop, calls=%fused_computation.130 | loop fusion | bytes 7340032 | tf_op jit(solution)/shard_map/slice | solution.py:79
  122.2 79.4 %all-gather.3.cloned.1.call-done = bf16[896,7168]{1,0:T(8,128)(2,1)} async-done(((bf16[56,7168]{1,0:T(8,128)(2,1)}), bf16[896,7168]{1,0:T(8,128)(2,1)}) %all-gather.3.cloned.1.call-update) | async-done | bytes 12845072 | tf_op jit(solution)/shard_map/all_gather | solution.py:44
  201.6 1.6 constant_dynamic-slice_fusion
  203.2 1.2 copy.21
  204.5 0.0 all-to-all-done
  204.5 0.0 copy-start.5
  204.5 9.3 %fusion.12 = bf16[256,896]{0,1:T(8,128)(2,1)S(1)} fusion(bf16[896,7168]{1,0:T(8,128)(2,1)} %all-gather.3.cloned.1.call-done, bf16[256,7168]{0,1:T(8,128)(2,1)} %bitcast.11), kind=kOutput, calls=%fused_computation.25 | convolution fusion | flops 3288563712 | bytes 16973824 | tf_op jit(solution)/shard_map/td,hd->th/dot_general | solution.py:57
  213.7 0.0 copy-done.5
  213.7 0.0 copy-done.12
  213.8 0.0 copy-start.4
  213.8 0.0 copy-start.11
  213.8 0.7 fusion.148
  214.5 0.5 copy-done.4
  215.0 0.0 copy-done.11
  215.0 0.7 fusion.150
  215.7 0.5 copy-done.3
  216.2 0.0 copy-done.10
  216.2 0.7 fusion.151
  216.9 0.5 copy-done.2
  217.4 0.0 copy-done.9
  217.4 0.7 fusion.149
  218.2 0.0 copy-start.8
  218.2 2.2 fusion.4
  220.3 0.0 copy-done.1
  220.4 0.0 copy-done.8
  220.4 0.0 copy-start
  220.4 0.8 fusion.82
  221.2 0.4 copy-done
  221.6 0.9 fusion.97
  222.4 0.9 fusion.112
  223.3 0.9 fusion.67
  224.2 1.0 copy.22
  (15 shorter events, 0.1 us)
Async XLA Ops:
  7.2 104.6 %all-gather.5.cloned.1.call-start = ((), (), s32[]{:S(2)}) async-start(), calls=%async_computation.2 | async-start | bytes 7798784 | tf_op jit(solution)/shard_map/all_gather | solution.py:67
  7.9 193.7 %all-gather.3.cloned.1.call-start = ((), (), s32[]{:S(2)}) async-start(), calls=%async_computation.1 | async-start | bytes 13647872 | tf_op jit(solution)/shard_map/all_gather | solution.py:44
  9.0 7.4 %collective-permute-start.1 = (bf16[56,1792]{1,0:T(8,128)(2,1)S(1)}, bf16[56,1792]{1,0:T(8,128)(2,1)S(1)}, u32[]{:S(2)}, u32[]{:S(2)}) collective-permute-start(bf16[56,1792]{1,0:T(8,128)(2,1)S(1)} %convert_element_type.22), channel_id=1, source_target_pairs={{0,128},{64,192},{128,0},{192,64},{1,129},{65,193},{129,1},{193,65... | collective-permute-start | bytes 602120 | tf_op jit(solution)/shard_map/ppermute | solution.py:38
  11.8 9.7 %collective-permute-start = (bf16[56,1792]{1,0:T(8,128)(2,1)S(1)}, bf16[56,1792]{1,0:T(8,128)(2,1)S(1)}, u32[]{:S(2)}, u32[]{:S(2)}) collective-permute-start(bf16[56,1792]{1,0:T(8,128)(2,1)S(1)} %convert_element_type.22), channel_id=1, source_target_pairs={{0,64},{64,128},{128,192},{192,0},{1,65},{65,129},{129,193},{193,1... | collective-permute-start | bytes 602120 | tf_op jit(solution)/shard_map/ppermute | solution.py:38
  12.1 9.3 %collective-permute-start.2 = (bf16[56,1792]{1,0:T(8,128)(2,1)S(1)}, bf16[56,1792]{1,0:T(8,128)(2,1)S(1)}, u32[]{:S(2)}, u32[]{:S(2)}) collective-permute-start(bf16[56,1792]{1,0:T(8,128)(2,1)S(1)} %convert_element_type.22), channel_id=1, source_target_pairs={{0,192},{64,0},{128,64},{192,128},{1,193},{65,1},{129,65},{193,129... | collective-permute-start | bytes 602120 | tf_op jit(solution)/shard_map/ppermute | solution.py:38
  22.2 1.3 copy-start.6
  25.7 14.4 %copy-start.13 = (s32[1,64]{1,0:T(1,128)S(1)}, s32[1,64]{1,0:T(1,128)}, u32[]{:S(2)}) copy-start(s32[1,64]{1,0:T(1,128)} %param.11) | copy-start | bytes 772
  25.7 14.7 %copy-start.7 = (bf16[2,256,896]{2,1,0:T(8,128)(2,1)S(1)}, bf16[2,256,896]{2,1,0:T(8,128)(2,1)}, u32[]{:S(2)}) copy-start(bf16[2,256,896]{2,1,0:T(8,128)(2,1)} %param.10) | copy-start | bytes 2752516
  25.7 178.8 %all-to-all-start = ((bf16[64,256,112]{1,2,0:T(8,128)(2,1)}), bf16[64,256,112]{1,2,0:T(8,128)(2,1)}, u32[]{:S(2)}, u32[]{:S(2)}) async-start(bf16[64,256,112]{1,2,0:T(8,128)(2,1)} %bitcast.36), calls=%async_computation | async-start | bytes 7340032 | tf_op jit(solution)/shard_map/all_to_all | solution.py:55
  204.5 9.3 %copy-start.5 = (bf16[2048,224]{1,0:T(8,128)(2,1)S(1)}, bf16[2048,224]{1,0:T(8,128)(2,1)}, u32[]{:S(2)}) copy-start(bf16[2048,224]{1,0:T(8,128)(2,1)} %get-tuple-element.21) | copy-start | bytes 2752516
  204.5 9.3 %copy-start.12 = (bf16[256,224]{1,0:T(8,128)(2,1)S(1)}, bf16[256,224]{1,0:T(8,128)(2,1)}, u32[]{:S(2)}) copy-start(bf16[256,224]{1,0:T(8,128)(2,1)} %get-tuple-element.31) | copy-start | bytes 344068
  213.8 1.2 copy-start.4
  213.8 1.2 copy-start.11
  215.0 1.2 copy-start.3
  215.0 1.2 copy-start.10
  216.2 1.2 copy-start.2
  216.2 1.2 copy-start.9
  218.2 2.2 copy-start.1
  218.2 2.2 copy-start.8
  220.4 1.2 copy-start
Sparse Core Ops, SparseCore 0:
  9.8 101.9 all-gather.4
  114.2 87.3 all-gather.2

commit v18 on v15

--- a/solution.py
+++ b/solution.py
@@ -44,9 +44,9 @@
     head_weights = lax.all_gather(trainer_rows, "blk", axis=0, tiled=True)
     head_width, model_width = head_weights.shape
     block_cols = model_width // blk_size
-    server_q = lax.dynamic_slice_in_dim(
-        head_weights, lax.axis_index("blk") * block_cols, block_cols, axis=1
-    )
+    piece_rows = trainer_rows.shape[0]
+    outgoing = jnp.transpose(trainer_rows.reshape(piece_rows, blk_size, block_cols), (1, 0, 2))
+    server_q = lax.all_to_all(outgoing, "blk", 0, 0, tiled=True).reshape(head_width, block_cols)
     group_rows, piece_cols = tokens.shape
     own_rows = group_rows // blk_size
     pieces = tokens.reshape(blk_size, 1, own_rows, piece_cols)

time: 231 us -> 238 us (1.030)
  starting transfers between devices: 16 us -> 24 us
  waiting for transfers between devices: 151 us -> 148 us
  local copies, waits for them, and re-layouts: 27.2 us -> 29.6 us
    all_to_all x1, waiting for transfers between devices: 0.01 us -> 85.7 us  [body(): pieces = lax.all_to_all(pieces, ('blk', 'mp'), 0, 0, tiled=True)]
    all_gather x1, waiting for transfers between devices: 66.3 us -> 0.01 us  [body(): shard_piece = lax.all_gather(kv_pool, 'blk', axis=1, tiled=True)]
    all_gather x1, waiting for transfers between devices: 73.5 us -> 33.6 us  [body(): head_weights = lax.all_gather(trainer_rows, 'blk', axis=0, tiled=True)]
    all_to_all x0 -> x1, waiting for transfers between devices: none -> 21.7 us  [body(): lax.all_to_all(outgoing, 'blk', 0, 0, tiled=True)]
    all_to_all x0 -> x1, starting transfers between devices: none -> 7.25 us  [body(): lax.all_to_all(outgoing, 'blk', 0, 0, tiled=True)]
    ppermute x3, waiting for transfers between devices: 10.5 us -> 6.47 us  [body(): lax.ppermute(own_piece, 'dp', [(i, (i + j) % dp_size) for i in range(dp_s...]
  transfers between devices with their start and end apart: 6 -> 7, of which waited for: 5 -> 5; matrix products, arithmetic and copies ran while one was open for 13% -> 13% of each run, Pallas kernels for 0% -> 0%
where the time goes in v18:
time: 238 us; the launch traced here: 236 us
  waiting for transfers between devices  148 us (62%)
  local copies, waits for them, and re-layouts  29.6 us (12%)
  starting transfers between devices  24 us (10%)
  between operations  15.5 us (7%)
  matrix products  14.1 us (6%)
  other arithmetic  5.09 us (2%)
    all_to_all x1, waiting for transfers between devices, body(): pieces = lax.all_to_all(pieces, ('blk', 'mp'), 0, 0, tiled=True)  85.7 us
    all_gather x1, waiting for transfers between devices, body(): head_weights = lax.all_gather(trainer_rows, 'blk', axis=0, tiled=True)  33.6 us
    all_to_all x1, waiting for transfers between devices, body(): lax.all_to_all(outgoing, 'blk', 0, 0, tiled=True)  21.7 us
    slice x2, local copies, waits for them, and re-layouts, body(): shard_piece[0].reshape(key_count, head_count, HD)  12.9 us
    all_to_all x1, starting transfers between devices, body(): pieces = lax.all_to_all(pieces, ('blk', 'mp'), 0, 0, tiled=True)  11.8 us
    dot_general x1, matrix products, body(): jnp.einsum('td,hd->th', token_local, head_weights, preferred_element_type...  9.31 us
    all_to_all x1, starting transfers between devices, body(): lax.all_to_all(outgoing, 'blk', 0, 0, tiled=True)  7.25 us
    ppermute x3, waiting for transfers between devices, body(): lax.ppermute(own_piece, 'dp', [(i, (i + j) % dp_size) for i in range(dp_s...  6.47 us
  transfers between devices with their start and end apart: 7, of which 5 were waited for; matrix products, arithmetic and copies ran while one was open for 13% of the time, Pallas kernels for 0%

profile of v18, /device:TPU:25, one launch (start us, length us, event | category | flops | bytes accessed | tf_op | source)
XLA Modules:
  0.0 236.4 jit_solution(16123475763697248446)
XLA Ops:
  7.2 0.0 copy-start.2
  7.2 0.0 all-gather.5.cloned.1.call-start
  7.2 0.7 all-gather.5.cloned.1.call-update
  7.9 0.0 all-gather.3.cloned.1.call-start
  8.0 1.0 convert_element_type.21
  9.0 1.3 collective-permute-start
  10.3 2.5 %collective-permute-start.1 = (bf16[56,1792]{1,0:T(8,128)(2,1)S(1)}, bf16[56,1792]{1,0:T(8,128)(2,1)S(1)}, u32[]{:S(2)}, u32[]{:S(2)}) collective-permute-start(bf16[56,1792]{1,0:T(8,128)(2,1)S(1)} %convert_element_type.21), channel_id=1, source_target_pairs={{0,128},{64,192},{128,0},{192,64},{1,129},{65,193},{129,1},{193,65... | collective-permute-start | bytes 602120 | tf_op jit(solution)/shard_map/ppermute | solution.py:38
  12.7 1.2 collective-permute-start.2
  13.9 1.0 convert_bitcast_fusion
  14.9 1.2 collective-permute-done
  16.1 5.3 %collective-permute-done.1 = bf16[56,1792]{1,0:T(8,128)(2,1)S(1)} collective-permute-done((bf16[56,1792]{1,0:T(8,128)(2,1)S(1)}, bf16[56,1792]{1,0:T(8,128)(2,1)S(1)}, u32[]{:S(2)}, u32[]{:S(2)}) %collective-permute-start.1) | collective-permute-done | bytes 200736 | tf_op jit(solution)/shard_map/ppermute | solution.py:38
  21.4 0.0 collective-permute-done.2
  21.4 0.1 pad_maximum_fusion
  21.5 0.6 gather_fusion
  22.1 0.2 fusion.22
  22.3 1.0 copy.51
  23.3 0.0 all-gather.3.cloned.1.call-update
  23.3 0.3 copy.38
  23.7 0.9 reshape_reshape.3
  24.6 1.5 copy.39
  26.1 7.2 %all-to-all-start = ((bf16[16,56,448]{2,1,0:T(8,128)(2,1)}), bf16[16,56,448]{2,1,0:T(8,128)(2,1)S(1)}, u32[]{:S(2)}, u32[]{:S(2)}) async-start(bf16[16,56,448]{2,1,0:T(8,128)(2,1)} %copy.39), calls=%async_computation | async-start | bytes 1835008 | tf_op jit(solution)/shard_map/all_to_all | solution.py:49
  33.3 0.0 copy-done.2
  33.3 0.0 copy-start.3
  33.3 0.1 copy.53
  33.4 21.7 %all-to-all-done = bf16[16,56,448]{2,1,0:T(8,128)(2,1)S(1)} async-done(((bf16[16,56,448]{2,1,0:T(8,128)(2,1)}), bf16[16,56,448]{2,1,0:T(8,128)(2,1)S(1)}, u32[]{:S(2)}, u32[]{:S(2)}) %all-to-all-start) | async-done | bytes 802848 | tf_op jit(solution)/shard_map/all_to_all | solution.py:49
  55.1 2.2 broadcast_in_dim.94
  57.3 11.8 %all-to-all-start.1 = ((bf16[64,256,112]{1,2,0:T(8,128)(2,1)}), bf16[64,256,112]{1,2,0:T(8,128)(2,1)}, u32[]{:S(2)}, u32[]{:S(2)}) async-start(bf16[64,256,112]{1,2,0:T(8,128)(2,1)} %bitcast.80), calls=%async_computation.1 | async-start | bytes 7340032 | tf_op jit(solution)/shard_map/all_to_all | solution.py:55
  69.7 1.2 fusion.42
  70.9 0.2 copy.42
  71.8 0.2 copy.43
  72.1 0.0 copy-done.3
  72.1 0.2 and_reduce_fusion
  72.2 0.1 fusion.24
  72.3 1.2 copy.47
  73.6 0.0 all-gather.5.cloned.1.call-done
  73.6 6.7 %fusion.41 = (bf16[1,2048,896]{2,1,0:T(8,128)(2,1)}, bf16[1,2048,896]{2,1,0:T(8,128)(2,1)}) fusion(bf16[2,2048,896]{2,1,0:T(8,128)(2,1)} %all-gather.5.cloned.1.call-done), kind=kLoop, calls=%fused_computation.69 | loop fusion | bytes 14680064 | tf_op jit(solution)/shard_map/slice | solution.py:88
  80.3 6.2 %copy.45 = bf16[1,2048,896]{1,2,0:T(8,128)(2,1)} copy(bf16[1,2048,896]{2,1,0:T(8,128)(2,1)} %get-tuple-element.12) | data formatting | bytes 7340032 | tf_op jit(solution)/shard_map/slice | solution.py:88
  86.5 6.2 %copy.46 = bf16[1,2048,896]{1,2,0:T(8,128)(2,1)} copy(bf16[1,2048,896]{2,1,0:T(8,128)(2,1)} %get-tuple-element.13) | data formatting | bytes 7340032 | tf_op jit(solution)/shard_map/slice | solution.py:89
  92.7 85.7 %all-to-all-done.1 = bf16[64,256,112]{1,2,0:T(8,128)(2,1)} async-done(((bf16[64,256,112]{1,2,0:T(8,128)(2,1)}), bf16[64,256,112]{1,2,0:T(8,128)(2,1)}, u32[]{:S(2)}, u32[]{:S(2)}) %all-to-all-start.1) | async-done | bytes 3670048 | tf_op jit(solution)/shard_map/all_to_all | solution.py:55
  178.4 33.6 %all-gather.3.cloned.1.call-done = bf16[896,7168]{1,0:T(8,128)(2,1)} async-done(((bf16[56,7168]{1,0:T(8,128)(2,1)}), bf16[896,7168]{1,0:T(8,128)(2,1)}) %all-gather.3.cloned.1.call-update) | async-done | bytes 12845072 | tf_op jit(solution)/shard_map/all_gather | solution.py:44
  212.0 0.0 copy-start
  212.0 9.3 %convolution_convert_fusion = bf16[896,256]{1,0:T(8,128)(2,1)S(1)} fusion(bf16[896,7168]{1,0:T(8,128)(2,1)} %all-gather.3.cloned.1.call-done, bf16[256,7168]{0,1:T(8,128)(2,1)} %bitcast.11), kind=kOutput, calls=%fused_computation.17 | convolution fusion | flops 3288563712 | bytes 16973824 | tf_op jit(solution)/shard_map/td,hd->th/dot_general | solution.py:57
  221.4 0.4 fusion.43
  221.7 0.0 copy-done
  221.8 0.0 copy-start.1
  221.8 1.9 fusion
  223.6 2.2 fusion.1
  225.8 0.0 copy-done.1
  225.8 2.1 fusion.7
  228.0 0.2 fusion.16
  228.2 0.4 fusion.15
  228.6 1.0 copy.48
  (8 shorter events, 0.1 us)
Async XLA Ops:
  7.2 26.1 %copy-start.2 = (bf16[4096,112]{0,1:T(8,128)(2,1)S(1)}, bf16[4096,112]{0,1:T(8,128)(2,1)}, u32[]{:S(2)}) copy-start(bf16[4096,112]{0,1:T(8,128)(2,1)} %param.7) | copy-start | bytes 2752516
  7.2 66.4 %all-gather.5.cloned.1.call-start = ((), (), s32[]{:S(2)}) async-start(), calls=%async_computation.3 | async-start | bytes 7798784 | tf_op jit(solution)/shard_map/all_gather | solution.py:80
  7.9 204.1 %all-gather.3.cloned.1.call-start = ((), (), s32[]{:S(2)}) async-start(), calls=%async_computation.2 | async-start | bytes 13647872 | tf_op jit(solution)/shard_map/all_gather | solution.py:44
  9.0 7.1 %collective-permute-start = (bf16[56,1792]{1,0:T(8,128)(2,1)S(1)}, bf16[56,1792]{1,0:T(8,128)(2,1)S(1)}, u32[]{:S(2)}, u32[]{:S(2)}) collective-permute-start(bf16[56,1792]{1,0:T(8,128)(2,1)S(1)} %convert_element_type.21), channel_id=1, source_target_pairs={{0,64},{64,128},{128,192},{192,0},{1,65},{65,129},{129,193},{193,1... | collective-permute-start | bytes 602120 | tf_op jit(solution)/shard_map/ppermute | solution.py:38
  10.3 11.1 %collective-permute-start.1 = (bf16[56,1792]{1,0:T(8,128)(2,1)S(1)}, bf16[56,1792]{1,0:T(8,128)(2,1)S(1)}, u32[]{:S(2)}, u32[]{:S(2)}) collective-permute-start(bf16[56,1792]{1,0:T(8,128)(2,1)S(1)} %convert_element_type.21), channel_id=1, source_target_pairs={{0,128},{64,192},{128,0},{192,64},{1,129},{65,193},{129,1},{193,65... | collective-permute-start | bytes 602120 | tf_op jit(solution)/shard_map/ppermute | solution.py:38
  12.7 8.7 %collective-permute-start.2 = (bf16[56,1792]{1,0:T(8,128)(2,1)S(1)}, bf16[56,1792]{1,0:T(8,128)(2,1)S(1)}, u32[]{:S(2)}, u32[]{:S(2)}) collective-permute-start(bf16[56,1792]{1,0:T(8,128)(2,1)S(1)} %convert_element_type.21), channel_id=1, source_target_pairs={{0,192},{64,0},{128,64},{192,128},{1,193},{65,1},{129,65},{193,129... | collective-permute-start | bytes 602120 | tf_op jit(solution)/shard_map/ppermute | solution.py:38
  26.1 29.0 %all-to-all-start = ((bf16[16,56,448]{2,1,0:T(8,128)(2,1)}), bf16[16,56,448]{2,1,0:T(8,128)(2,1)S(1)}, u32[]{:S(2)}, u32[]{:S(2)}) async-start(bf16[16,56,448]{2,1,0:T(8,128)(2,1)} %copy.39), calls=%async_computation | async-start | bytes 1835008 | tf_op jit(solution)/shard_map/all_to_all | solution.py:49
  33.3 38.8 %copy-start.3 = (s32[1,64]{1,0:T(1,128)S(1)}, s32[1,64]{1,0:T(1,128)}, u32[]{:S(2)}) copy-start(s32[1,64]{1,0:T(1,128)} %param.11) | copy-start | bytes 772
  57.3 121.1 %all-to-all-start.1 = ((bf16[64,256,112]{1,2,0:T(8,128)(2,1)}), bf16[64,256,112]{1,2,0:T(8,128)(2,1)}, u32[]{:S(2)}, u32[]{:S(2)}) async-start(bf16[64,256,112]{1,2,0:T(8,128)(2,1)} %bitcast.80), calls=%async_computation.1 | async-start | bytes 7340032 | tf_op jit(solution)/shard_map/all_to_all | solution.py:55
  212.0 9.7 %copy-start = (bf16[1,2048,896]{1,2,0:T(8,128)(2,1)S(1)}, bf16[1,2048,896]{1,2,0:T(8,128)(2,1)}, u32[]{:S(2)}) copy-start(bf16[1,2048,896]{1,2,0:T(8,128)(2,1)} %copy.45) | copy-start | bytes 11010052
  221.8 4.1 %copy-start.1 = (bf16[1,2048,896]{1,2,0:T(8,128)(2,1)S(1)}, bf16[1,2048,896]{1,2,0:T(8,128)(2,1)}, u32[]{:S(2)}) copy-start(bf16[1,2048,896]{1,2,0:T(8,128)(2,1)} %copy.46) | copy-start | bytes 11010052
Sparse Core Ops, SparseCore 0:
  9.8 62.6 all-gather.4
  74.4 137.6 all-gather.2
